TPU v7x, 512 devices: a whole 4x8x8 slice. The times are simulated.
512 devices in a mesh: gy: 16 (over x_lo, z), gx: 32 (over x_hi, y, core).
Axes of the slice: x: 4 (x_hi: 2, x_lo: 2; x = x_hi * 2 + x_lo), y: 8, z: 8, core: 2. Of those that a mesh axis runs over, the one named last changes fastest.
Arguments:
- field: bfloat16 [1024, 512, 128], P('gy', 'gx'), may hold values from -8 to 8
- cotangent: bfloat16 [512, 256, 256], P('gy', 'gx'), may hold values from -6 to 6
- gain_fine: float32 [128], replicated, may hold values from 0.1 to 1.9
- weight_fine: bfloat16 [3, 3, 128, 128], replicated, may hold values from -0.1875 to 0.1875
- projection: bfloat16 [128, 256], replicated, may hold values from -0.5 to 0.5
- gain_coarse: float32 [256], replicated, may hold values from 0.1 to 1.9
- weight_coarse: bfloat16 [3, 3, 256, 256], replicated, may hold values from -0.125 to 0.125
Outputs:
- coarse_output: bfloat16 [512, 256, 256], P('gy', 'gx')
- field_grad: bfloat16 [1024, 512, 128], P('gy', 'gx')
- fine_weight_grad: float32 [3, 3, 128, 128], replicated
- fine_gain_grad: float32 [128], replicated
- projection_grad: float32 [128, 256], replicated
- coarse_weight_grad: float32 [3, 3, 256, 256], replicated
- coarse_gain_grad: float32 [256], replicated
All inputs are finite; a program needn't handle non-finite values.
Results may differ from a plain program's by a relative error of at most 0.014.
Values may be sent and summed in bfloat16 or wider, within the bound.
No kernel may reach another device: no remote copies, remote signals or barrier semaphores. Data moves between devices by JAX's collectives and lax.ppermute only.
A program may use at most 64 MiB of HBM per device.

v0:
```python
import functools

import jax
import jax.numpy as jnp
from jax import lax
from jax.sharding import Mesh
from jax.sharding import PartitionSpec as P

GROUPS = 32
GY = ("gy_0", "gy_1")
GX = ("gx_0", "gx_1", "gx_2")
GY_GX = ("gy_0", "gy_1", "gx_0", "gx_1", "gx_2")


EPSILON = 1e-05


def extended(cells, sides, width):
    for axis, dim in sides:
        count = lax.axis_size(axis)
        ends = count - 1
        head = lax.slice_in_dim(cells, 0, width, axis=dim)
        tail = lax.slice_in_dim(cells, cells.shape[dim] - width, cells.shape[dim], axis=dim)
        cells = jnp.concatenate(
            [
                lax.ppermute(tail, axis, [(i, (i + 1) % count) for i in range(ends)]),
                cells,
                lax.ppermute(head, axis, [((i + 1) % count, i) for i in range(ends)]),
            ],
            axis=dim,
        )
    return cells


def one_axis_at_a_time(x, axes):
    return functools.reduce(lax.psum, axes, x)


def in_one(arrays, axis):
    ends = [0]
    for a in arrays:
        ends.append(ends[-1] + a.size)
    so_far = lax.psum(jnp.concatenate([a.ravel() for a in arrays]), axis)
    return tuple((so_far[b:e].reshape(a.shape) for a, b, e in zip(arrays, ends, ends[1:])))


def conv_forward(padded, weight, height, width):
    channels = padded.shape[2]
    total = jnp.zeros((height * width, weight.shape[3]), jnp.float32)
    for row_tap in range(3):
        for col_tap in range(3):
            window = padded[row_tap : row_tap + height, col_tap : col_tap + width].reshape(
                height * width, channels
            )
            total = total + jnp.dot(
                window, weight[row_tap, col_tap], preferred_element_type=jnp.float32
            )
    return total.reshape(height, width, weight.shape[3])


def conv_transpose(padded, weight, height, width):
    channels = padded.shape[2]
    total = jnp.zeros((height * width, weight.shape[2]), jnp.float32)
    for row_tap in range(3):
        for col_tap in range(3):
            window = padded[
                2 - row_tap : 2 - row_tap + height, 2 - col_tap : 2 - col_tap + width
            ].reshape(height * width, channels)
            total = total + jnp.dot(
                window, weight[row_tap, col_tap].T, preferred_element_type=jnp.float32
            )
    return total.reshape(height, width, weight.shape[2])


def conv_weight(padded, grads, height, width):
    channels = padded.shape[2]
    flat_grads = grads.reshape(height * width, grads.shape[2])
    taps = []
    for row_tap in range(3):
        for col_tap in range(3):
            window = padded[row_tap : row_tap + height, col_tap : col_tap + width].reshape(
                height * width, channels
            )
            taps.append(
                lax.dot_general(
                    window, flat_grads, (((0,), (0,)), ((), ())), preferred_element_type=jnp.float32
                )
            )
    return jnp.stack(taps).reshape(3, 3, channels, grads.shape[2])


def tile_rims(values):
    rowed = extended(values, ((GY, 0),), 1)
    return extended(rowed, ((GX, 1),), 1)


def upsample(values):
    rows, cols, channels = values.shape
    return jnp.broadcast_to(values[:, None, :, None, :], (rows, 2, cols, 2, channels)).reshape(
        2 * rows, 2 * cols, channels
    )


def global_sums(pair):
    return (one_axis_at_a_time(pair[0], GY_GX), one_axis_at_a_time(pair[1], GY_GX))


def normalize(values, count):
    channels = values.shape[2]
    grouped = values.reshape(-1, GROUPS, channels // GROUPS)
    first, second = global_sums(
        (jnp.sum(grouped, axis=(0, 2)), jnp.sum(grouped * grouped, axis=(0, 2)))
    )
    average = first / count
    variance = second / count - average * average
    inverse = lax.rsqrt(variance + EPSILON)
    normed = (grouped - average[None, :, None]) * inverse[None, :, None]
    return (normed.reshape(values.shape), inverse)


def norm_backward(dnorm, normed, inverse, count):
    channels = normed.shape[2]
    dgroup = dnorm.reshape(-1, GROUPS, channels // GROUPS)
    ngroup = normed.reshape(-1, GROUPS, channels // GROUPS)
    first, second = global_sums(
        (jnp.sum(dgroup, axis=(0, 2)), jnp.sum(dgroup * ngroup, axis=(0, 2)))
    )
    result = inverse[None, :, None] * (
        dgroup - (first / count)[None, :, None] - ngroup * (second / count)[None, :, None]
    )
    return result.reshape(normed.shape)


def silu_slope(act):
    sigma = jax.nn.sigmoid(act)
    return sigma * (1.0 + act * (1.0 - sigma))


def on_device(field, cotangent, gain_fine, weight_fine, projection, gain_coarse, weight_coarse):
    height, width, chan_fine = field.shape
    chan_coarse = projection.shape[1]
    half_h, half_w = (height // 2, width // 2)
    cells_all = height * width * lax.axis_size(GY) * lax.axis_size(GX)
    fine_count = cells_all * (chan_fine // GROUPS)
    coarse_count = cells_all // 4 * (chan_coarse // GROUPS)
    values = field.astype(jnp.float32)
    normed_fine, inverse_fine = normalize(values, fine_count)
    act_fine = normed_fine * gain_fine
    hidden_fine = jax.nn.silu(act_fine).astype(jnp.bfloat16)
    padded_fine = tile_rims(hidden_fine)
    block_fine = (values + conv_forward(padded_fine, weight_fine, height, width)).astype(
        jnp.bfloat16
    )
    pooled = jnp.mean(
        block_fine.astype(jnp.float32).reshape(half_h, 2, half_w, 2, chan_fine), axis=(1, 3)
    ).astype(jnp.bfloat16)
    coarse_in = (
        jnp.dot(pooled.reshape(-1, chan_fine), projection, preferred_element_type=jnp.float32)
        .reshape(half_h, half_w, chan_coarse)
        .astype(jnp.bfloat16)
    )
    coarse_vals = coarse_in.astype(jnp.float32)
    normed_coarse, inverse_coarse = normalize(coarse_vals, coarse_count)
    act_coarse = normed_coarse * gain_coarse
    hidden_coarse = jax.nn.silu(act_coarse).astype(jnp.bfloat16)
    padded_coarse = tile_rims(hidden_coarse)
    coarse_output = (
        coarse_vals + conv_forward(padded_coarse, weight_coarse, half_h, half_w)
    ).astype(jnp.bfloat16)
    padded_grad = tile_rims(cotangent)
    coarse_weight_grad = conv_weight(padded_coarse, cotangent, half_h, half_w)
    dact_coarse = conv_transpose(padded_grad, weight_coarse, half_h, half_w) * silu_slope(
        act_coarse
    )
    coarse_gain_grad = jnp.sum((dact_coarse * normed_coarse).reshape(-1, chan_coarse), axis=0)
    dcoarse = (
        cotangent.astype(jnp.float32)
        + norm_backward(dact_coarse * gain_coarse, normed_coarse, inverse_coarse, coarse_count)
    ).astype(jnp.bfloat16)
    projection_grad = lax.dot_general(
        pooled.reshape(-1, chan_fine),
        dcoarse.reshape(-1, chan_coarse),
        (((0,), (0,)), ((), ())),
        preferred_element_type=jnp.float32,
    )
    dpool = jnp.dot(
        dcoarse.reshape(-1, chan_coarse), projection.T, preferred_element_type=jnp.float32
    ).reshape(half_h, half_w, chan_fine)
    small_dblock = (dpool * 0.25).astype(jnp.bfloat16)
    dblock = upsample(small_dblock)
    padded_dblock = upsample(tile_rims(small_dblock))[1:-1, 1:-1]
    fine_weight_grad = conv_weight(padded_fine, dblock, height, width)
    dact_fine = conv_transpose(padded_dblock, weight_fine, height, width) * silu_slope(act_fine)
    fine_gain_grad = jnp.sum((dact_fine * normed_fine).reshape(-1, chan_fine), axis=0)
    field_grad = (
        dblock.astype(jnp.float32)
        + norm_backward(dact_fine * gain_fine, normed_fine, inverse_fine, fine_count)
    ).astype(jnp.bfloat16)
    fine_weight_grad, fine_gain_grad, projection_grad, coarse_weight_grad, coarse_gain_grad = (
        in_one(
            (
                fine_weight_grad,
                fine_gain_grad,
                projection_grad,
                coarse_weight_grad,
                coarse_gain_grad,
            ),
            GY_GX,
        )
    )
    return (
        coarse_output,
        field_grad,
        fine_weight_grad,
        fine_gain_grad,
        projection_grad,
        coarse_weight_grad,
        coarse_gain_grad,
    )


def solution(mesh):
    finer = Mesh(mesh.devices.reshape(2, 8, 2, 8, 2), ("gy_0", "gy_1", "gx_0", "gx_1", "gx_2"))
    in_specs = (P(GY, GX, None), P(GY, GX, None), P(), P(), P(), P(), P())
    out_specs = (P(GY, GX, None), P(GY, GX, None), P(), P(), P(), P(), P())
    return jax.shard_map(
        on_device, mesh=finer, in_specs=in_specs, out_specs=out_specs, check_vma=False
    )
```

profile of v0, /device:TPU:1, one launch (start us, length us, event | category | flops | bytes accessed | tf_op | source)
XLA Modules:
  0.0 611.8 jit_solution(15122413380415157542)
XLA Ops:
  8.9 4.3 all-reduce.19
  13.2 19.7 %all-reduce.7 = (f32[32]{0:T(128)S(1)}, f32[32]{0:T(128)S(1)}) all-reduce(f32[32]{0:T(128)S(1)} %get-tuple-element.55, f32[32]{0:T(128)S(1)} %get-tuple-element.56), channel_id=1, replica_groups=mesh['gy_0'=2,'gy_1'=8,'gx_0'=2,'gx_1'=8,'gx_2'=2] {'gy_1'}, use_global_device_ids=true, to_apply=%region_10.0 | all-reduce | flops 64 | bytes 512 | tf_op jit(solution)/shard_map/psum | solution.py:36
  33.0 5.3 all-reduce.15
  38.2 14.0 %all-reduce.3 = (f32[32]{0:T(128)S(1)}, f32[32]{0:T(128)S(1)}) all-reduce(f32[32]{0:T(128)S(1)} %get-tuple-element.47, f32[32]{0:T(128)S(1)} %get-tuple-element.48), channel_id=1, replica_groups=mesh['gy_0'=2,'gy_1'=8,'gx_0'=2,'gx_1'=8,'gx_2'=2] {'gx_1'}, use_global_device_ids=true, to_apply=%region_12.13 | all-reduce | flops 64 | bytes 512 | tf_op jit(solution)/shard_map/psum | solution.py:36
  52.2 12.4 %all-reduce.11 = (f32[32]{0:T(128)S(1)}, f32[32]{0:T(128)S(1)}) all-reduce(f32[32]{0:T(128)S(1)} %get-tuple-element.23, f32[32]{0:T(128)S(1)} %get-tuple-element.24), channel_id=1, replica_groups=mesh['gy_0'=2,'gy_1'=8,'gx_0'=2,'gx_1'=8,'gx_2'=2] {'gx_2'}, use_global_device_ids=true, to_apply=%region_13.14 | all-reduce | flops 64 | bytes 512 | tf_op jit(solution)/shard_map/psum | solution.py:36
  67.5 4.0 collective-permute-start
  75.5 2.6 collective-permute-start.2
  78.0 1.9 collective-permute-start.3
  81.0 3.6 collective-permute-start.11
  84.6 1.9 collective-permute-start.10
  94.5 8.3 %all-reduce.18 = (f32[32]{0:T(128)S(1)}, f32[32]{0:T(128)S(1)}) all-reduce(f32[32]{0:T(128)S(1)} %reduce_sum.140, f32[32]{0:T(128)S(1)} %reduce_sum.134), channel_id=1, replica_groups=mesh['gy_0'=2,'gy_1'=8,'gx_0'=2,'gx_1'=8,'gx_2'=2] {'gy_0'}, use_global_device_ids=true, to_apply=%region_24.25 | all-reduce | flops 64 | bytes 512 | tf_op jit(solution)/shard_map/psum | solution.py:36
  102.8 10.7 %all-reduce.6 = (f32[32]{0:T(128)S(1)}, f32[32]{0:T(128)S(1)}) all-reduce(f32[32]{0:T(128)S(1)} %get-tuple-element.53, f32[32]{0:T(128)S(1)} %get-tuple-element.54), channel_id=1, replica_groups=mesh['gy_0'=2,'gy_1'=8,'gx_0'=2,'gx_1'=8,'gx_2'=2] {'gy_1'}, use_global_device_ids=true, to_apply=%region_25.26 | all-reduce | flops 64 | bytes 512 | tf_op jit(solution)/shard_map/psum | solution.py:36
  113.5 8.6 %all-reduce.14 = (f32[32]{0:T(128)S(1)}, f32[32]{0:T(128)S(1)}) all-reduce(f32[32]{0:T(128)S(1)} %get-tuple-element.29, f32[32]{0:T(128)S(1)} %get-tuple-element.30), channel_id=1, replica_groups=mesh['gy_0'=2,'gy_1'=8,'gx_0'=2,'gx_1'=8,'gx_2'=2] {'gx_0'}, use_global_device_ids=true, to_apply=%region_26.27 | all-reduce | flops 64 | bytes 512 | tf_op jit(solution)/shard_map/psum | solution.py:36
  122.1 15.9 %all-reduce.2 = (f32[32]{0:T(128)S(1)}, f32[32]{0:T(128)S(1)}) all-reduce(f32[32]{0:T(128)S(1)} %get-tuple-element.45, f32[32]{0:T(128)S(1)} %get-tuple-element.46), channel_id=1, replica_groups=mesh['gy_0'=2,'gy_1'=8,'gx_0'=2,'gx_1'=8,'gx_2'=2] {'gx_1'}, use_global_device_ids=true, to_apply=%region_27.28 | all-reduce | flops 64 | bytes 512 | tf_op jit(solution)/shard_map/psum | solution.py:36
  138.0 11.5 %all-reduce.10 = (f32[32]{0:T(128)S(1)}, f32[32]{0:T(128)S(1)}) all-reduce(f32[32]{0:T(128)S(1)} %get-tuple-element.21, f32[32]{0:T(128)S(1)} %get-tuple-element.22), channel_id=1, replica_groups=mesh['gy_0'=2,'gy_1'=8,'gx_0'=2,'gx_1'=8,'gx_2'=2] {'gx_2'}, use_global_device_ids=true, to_apply=%region_28.29 | all-reduce | flops 64 | bytes 512 | tf_op jit(solution)/shard_map/psum | solution.py:36
  154.3 3.8 all-reduce.17
  158.1 11.9 %all-reduce.5 = (f32[32]{0:T(128)S(1)}, f32[32]{0:T(128)S(1)}) all-reduce(f32[32]{0:T(128)S(1)} %get-tuple-element.51, f32[32]{0:T(128)S(1)} %get-tuple-element.52), channel_id=1, replica_groups=mesh['gy_0'=2,'gy_1'=8,'gx_0'=2,'gx_1'=8,'gx_2'=2] {'gy_1'}, use_global_device_ids=true, to_apply=%region_39.40 | all-reduce | flops 64 | bytes 512 | tf_op jit(solution)/shard_map/psum | solution.py:36
  170.0 5.7 all-reduce.13
  175.7 12.7 %all-reduce.1 = (f32[32]{0:T(128)S(1)}, f32[32]{0:T(128)S(1)}) all-reduce(f32[32]{0:T(128)S(1)} %get-tuple-element.43, f32[32]{0:T(128)S(1)} %get-tuple-element.44), channel_id=1, replica_groups=mesh['gy_0'=2,'gy_1'=8,'gx_0'=2,'gx_1'=8,'gx_2'=2] {'gx_1'}, use_global_device_ids=true, to_apply=%region_41.42 | all-reduce | flops 64 | bytes 512 | tf_op jit(solution)/shard_map/psum | solution.py:36
  188.4 11.4 %all-reduce.9 = (f32[32]{0:T(128)S(1)}, f32[32]{0:T(128)S(1)}) all-reduce(f32[32]{0:T(128)S(1)} %get-tuple-element.19, f32[32]{0:T(128)S(1)} %get-tuple-element.20), channel_id=1, replica_groups=mesh['gy_0'=2,'gy_1'=8,'gx_0'=2,'gx_1'=8,'gx_2'=2] {'gx_2'}, use_global_device_ids=true, to_apply=%region_42.43 | all-reduce | flops 64 | bytes 512 | tf_op jit(solution)/shard_map/psum | solution.py:36
  202.6 4.0 collective-permute-start.4
  208.1 4.0 collective-permute-start.12
  218.9 3.4 collective-permute-start.15
  222.3 2.2 collective-permute-start.14
  227.1 2.6 collective-permute-start.7
  236.3 4.5 all-reduce.16
  240.8 14.6 %all-reduce.4 = (f32[32]{0:T(128)S(1)}, f32[32]{0:T(128)S(1)}) all-reduce(f32[32]{0:T(128)S(1)} %get-tuple-element.49, f32[32]{0:T(128)S(1)} %get-tuple-element.50), channel_id=1, replica_groups=mesh['gy_0'=2,'gy_1'=8,'gx_0'=2,'gx_1'=8,'gx_2'=2] {'gy_1'}, use_global_device_ids=true, to_apply=%region_53.54 | all-reduce | flops 64 | bytes 512 | tf_op jit(solution)/shard_map/psum | solution.py:36
  255.4 5.7 all-reduce.12
  261.1 15.7 %all-reduce = (f32[32]{0:T(128)S(1)}, f32[32]{0:T(128)S(1)}) all-reduce(f32[32]{0:T(128)S(1)} %get-tuple-element.41, f32[32]{0:T(128)S(1)} %get-tuple-element.42), channel_id=1, replica_groups=mesh['gy_0'=2,'gy_1'=8,'gx_0'=2,'gx_1'=8,'gx_2'=2] {'gx_1'}, use_global_device_ids=true, to_apply=%region_55.56 | all-reduce | flops 64 | bytes 512 | tf_op jit(solution)/shard_map/psum | solution.py:36
  276.8 11.6 %all-reduce.8 = (f32[32]{0:T(128)S(1)}, f32[32]{0:T(128)S(1)}) all-reduce(f32[32]{0:T(128)S(1)} %get-tuple-element.17, f32[32]{0:T(128)S(1)} %get-tuple-element.18), channel_id=1, replica_groups=mesh['gy_0'=2,'gy_1'=8,'gx_0'=2,'gx_1'=8,'gx_2'=2] {'gx_2'}, use_global_device_ids=true, to_apply=%region_56.57 | all-reduce | flops 64 | bytes 512 | tf_op jit(solution)/shard_map/psum | solution.py:36
  298.0 20.0 %dynamic-update-slice.3 = f32[770432]{0:T(1024)} dynamic-update-slice(f32[770432]{0:T(1024)} %constant_dynamic-update-slice_fusion.5, f32[589824]{0:T(1024)S(1)} %bitcast.340, s32[]{} %constant.32) | dynamic-update-slice | bytes 4718596
  321.4 274.0 %all-reduce.22.cloned.1.call-done = f32[770432]{0:T(1024)} async-done(((f32[770432]{0:T(1024)}), f32[770432]{0:T(1024)}) %all-reduce.22.cloned.1.call-update) | async-done | bytes 3081744 | tf_op jit(solution)/shard_map/psum | solution.py:43
  (214 shorter events, 64.2 us)
Async XLA Ops:
  7.2 86.0 %copy-start = (bf16[128,256]{1,0:T(8,128)(2,1)S(1)}, bf16[128,256]{1,0:T(8,128)(2,1)}, u32[]{:S(2)}) copy-start(bf16[128,256]{1,0:T(8,128)(2,1)} %param.11) | copy-start | bytes 196612
  7.2 80.4 %copy-start.4 = (bf16[32,8,256]{2,1,0:T(8,128)(2,1)S(1)}, bf16[32,8,256]{2,1,0:T(8,128)(2,1)}, u32[]{:S(2)}) copy-start(bf16[32,8,256]{2,1,0:T(8,128)(2,1)} %param.8) | copy-start | bytes 393220
  7.2 80.4 %copy-start.2 = (bf16[3,3,256,256]{3,2,1,0:T(8,128)(2,1)S(1)}, bf16[3,3,256,256]{3,2,1,0:T(8,128)(2,1)}, u32[]{:S(2)}) copy-start(bf16[3,3,256,256]{3,2,1,0:T(8,128)(2,1)} %param.13) | copy-start | bytes 3538948
  7.2 588.2 %all-reduce.22.cloned.1.call-start = ((), (), s32[]{:S(2)}) async-start(), calls=%async_computation | async-start | bytes 6168576 | tf_op jit(solution)/shard_map/psum | solution.py:43
  65.0 16.0 %copy-start.17 = (f32[128]{0:T(128)}, f32[128]{0:T(128)S(1)}, u32[]{:S(2)}) copy-start(f32[128]{0:T(128)S(1)} %sub.77) | copy-start | bytes 1540
  66.2 9.2 %collective-permute-start.1 = (bf16[1,16,128]{2,1,0:T(8,128)(2,1)S(1)}, bf16[1,16,128]{2,1,0:T(8,128)(2,1)S(1)}, u32[]{:S(2)}, u32[]{:S(2)}) collective-permute-start(bf16[1,16,128]{2,1,0:T(8,128)(2,1)S(1)} %get-tuple-element.82), channel_id=1, source_target_pairs={{32,0},{64,32},{96,64},{128,96},{160,128},{192,160},{224,192},{256... | collective-permute-start | bytes 12296 | tf_op jit(solution)/shard_map/ppermute | solution.py:28
  67.5 7.9 %collective-permute-start = (bf16[1,16,128]{2,1,0:T(8,128)(2,1)S(1)}, bf16[1,16,128]{2,1,0:T(8,128)(2,1)S(1)}, u32[]{:S(2)}, u32[]{:S(2)}) collective-permute-start(bf16[1,16,128]{2,1,0:T(8,128)(2,1)S(1)} %get-tuple-element.81), channel_id=1, source_target_pairs={{0,32},{32,64},{64,96},{96,128},{128,160},{160,192},{192,224},{224... | collective-permute-start | bytes 12296 | tf_op jit(solution)/shard_map/ppermute | solution.py:26
  72.2 7.8 %collective-permute-start.8 = (bf16[1,8,256]{2,1,0:T(8,128)(2,1)S(1)}, bf16[1,8,256]{2,1,0:T(8,128)(2,1)S(1)}, u32[]{:S(2)}, u32[]{:S(2)}) collective-permute-start(bf16[1,8,256]{2,1,0:T(8,128)(2,1)S(1)} %get-tuple-element.90), channel_id=1, source_target_pairs={{0,32},{32,64},{64,96},{96,128},{128,160},{160,192},{192,224},{224... | collective-permute-start | bytes 12296 | tf_op jit(solution)/shard_map/ppermute | solution.py:26
  74.1 6.8 %collective-permute-start.9 = (bf16[1,8,256]{2,1,0:T(8,128)(2,1)S(1)}, bf16[1,8,256]{2,1,0:T(8,128)(2,1)S(1)}, u32[]{:S(2)}, u32[]{:S(2)}) collective-permute-start(bf16[1,8,256]{2,1,0:T(8,128)(2,1)S(1)} %get-tuple-element.89), channel_id=1, source_target_pairs={{32,0},{64,32},{96,64},{128,96},{160,128},{192,160},{224,192},{256... | collective-permute-start | bytes 12296 | tf_op jit(solution)/shard_map/ppermute | solution.py:28
  75.5 14.0 %collective-permute-start.2 = (bf16[66,1,128]{2,1,0:T(2,128)(2,1)S(1)}, bf16[66,1,128]{2,1,0:T(2,128)(2,1)S(1)}, u32[]{:S(2)}, u32[]{:S(2)}) collective-permute-start(bf16[66,1,128]{2,1,0:T(2,128)(2,1)S(1)} %get-tuple-element.75), channel_id=1, source_target_pairs={{0,1},{1,2},{2,3},{3,4},{4,5},{5,6},{6,7},{7,8},{8,9},{9,10},{10,1... | collective-permute-start | bytes 50696 | tf_op jit(solution)/shard_map/ppermute | solution.py:26
  78.0 11.4 %collective-permute-start.3 = (bf16[66,1,128]{2,1,0:T(2,128)(2,1)S(1)}, bf16[66,1,128]{2,1,0:T(2,128)(2,1)S(1)}, u32[]{:S(2)}, u32[]{:S(2)}) collective-permute-start(bf16[66,1,128]{2,1,0:T(2,128)(2,1)S(1)} %get-tuple-element.76), channel_id=1, source_target_pairs={{1,0},{2,1},{3,2},{4,3},{5,4},{6,5},{7,6},{8,7},{9,8},{10,9},{11,1... | collective-permute-start | bytes 50696 | tf_op jit(solution)/shard_map/ppermute | solution.py:28
  81.0 70.1 %collective-permute-start.11 = (bf16[34,1,256]{2,1,0:T(2,128)(2,1)S(1)}, bf16[34,1,256]{2,1,0:T(2,128)(2,1)S(1)}, u32[]{:S(2)}, u32[]{:S(2)}) collective-permute-start(bf16[34,1,256]{2,1,0:T(2,128)(2,1)S(1)} %get-tuple-element.84), channel_id=1, source_target_pairs={{0,1},{1,2},{2,3},{3,4},{4,5},{5,6},{6,7},{7,8},{8,9},{9,10},{10,1... | collective-permute-start | bytes 52232 | tf_op jit(solution)/shard_map/ppermute | solution.py:26
  84.6 65.2 %collective-permute-start.10 = (bf16[34,1,256]{2,1,0:T(2,128)(2,1)S(1)}, bf16[34,1,256]{2,1,0:T(2,128)(2,1)S(1)}, u32[]{:S(2)}, u32[]{:S(2)}) collective-permute-start(bf16[34,1,256]{2,1,0:T(2,128)(2,1)S(1)} %get-tuple-element.83), channel_id=1, source_target_pairs={{1,0},{2,1},{3,2},{4,3},{5,4},{6,5},{7,6},{8,7},{9,8},{10,9},{11,1... | collective-permute-start | bytes 52232 | tf_op jit(solution)/shard_map/ppermute | solution.py:28
  88.5 1.5 copy-start.12
  90.0 1.1 copy-start.6
  149.5 2.7 copy-start.21
  149.8 2.5 copy-start.8
  149.8 2.5 copy-start.16
  201.3 23.1 %collective-permute-start.5 = (bf16[1,8,256]{2,1,0:T(8,128)(2,1)S(1)}, bf16[1,8,256]{2,1,0:T(8,128)(2,1)S(1)}, u32[]{:S(2)}, u32[]{:S(2)}) collective-permute-start(bf16[1,8,256]{2,1,0:T(8,128)(2,1)S(1)} %get-tuple-element.92), channel_id=1, source_target_pairs={{32,0},{64,32},{96,64},{128,96},{160,128},{192,160},{224,192},{256... | collective-permute-start | bytes 12296 | tf_op jit(solution)/shard_map/ppermute | solution.py:28
  202.6 21.8 %collective-permute-start.4 = (bf16[1,8,256]{2,1,0:T(8,128)(2,1)S(1)}, bf16[1,8,256]{2,1,0:T(8,128)(2,1)S(1)}, u32[]{:S(2)}, u32[]{:S(2)}) collective-permute-start(bf16[1,8,256]{2,1,0:T(8,128)(2,1)S(1)} %get-tuple-element.91), channel_id=1, source_target_pairs={{0,32},{32,64},{64,96},{96,128},{128,160},{160,192},{192,224},{224... | collective-permute-start | bytes 12296 | tf_op jit(solution)/shard_map/ppermute | solution.py:26
  206.8 12.0 %collective-permute-start.13 = (bf16[1,8,128]{2,1,0:T(8,128)(2,1)S(1)}, bf16[1,8,128]{2,1,0:T(8,128)(2,1)S(1)}, u32[]{:S(2)}, u32[]{:S(2)}) collective-permute-start(bf16[1,8,128]{2,1,0:T(8,128)(2,1)S(1)} %get-tuple-element.96), channel_id=1, source_target_pairs={{32,0},{64,32},{96,64},{128,96},{160,128},{192,160},{224,192},{256... | collective-permute-start | bytes 6152 | tf_op jit(solution)/shard_map/ppermute | solution.py:28
  208.1 10.7 %collective-permute-start.12 = (bf16[1,8,128]{2,1,0:T(8,128)(2,1)S(1)}, bf16[1,8,128]{2,1,0:T(8,128)(2,1)S(1)}, u32[]{:S(2)}, u32[]{:S(2)}) collective-permute-start(bf16[1,8,128]{2,1,0:T(8,128)(2,1)S(1)} %get-tuple-element.95), channel_id=1, source_target_pairs={{0,32},{32,64},{64,96},{96,128},{128,160},{160,192},{192,224},{224... | collective-permute-start | bytes 6152 | tf_op jit(solution)/shard_map/ppermute | solution.py:26
  215.0 3.5 copy-start.11
  218.9 11.7 %collective-permute-start.15 = (bf16[34,1,128]{2,1,0:T(2,128)(2,1)S(1)}, bf16[34,1,128]{2,1,0:T(2,128)(2,1)S(1)}, u32[]{:S(2)}, u32[]{:S(2)}) collective-permute-start(bf16[34,1,128]{2,1,0:T(2,128)(2,1)S(1)} %get-tuple-element.94), channel_id=1, source_target_pairs={{1,0},{2,1},{3,2},{4,3},{5,4},{6,5},{7,6},{8,7},{9,8},{10,9},{11,1... | collective-permute-start | bytes 26120 | tf_op jit(solution)/shard_map/ppermute | solution.py:28
  222.3 8.3 %collective-permute-start.14 = (bf16[34,1,128]{2,1,0:T(2,128)(2,1)S(1)}, bf16[34,1,128]{2,1,0:T(2,128)(2,1)S(1)}, u32[]{:S(2)}, u32[]{:S(2)}) collective-permute-start(bf16[34,1,128]{2,1,0:T(2,128)(2,1)S(1)} %get-tuple-element.93), channel_id=1, source_target_pairs={{0,1},{1,2},{2,3},{3,4},{4,5},{5,6},{6,7},{7,8},{8,9},{9,10},{10,1... | collective-permute-start | bytes 26120 | tf_op jit(solution)/shard_map/ppermute | solution.py:26
  225.2 67.6 %collective-permute-start.6 = (bf16[34,1,256]{2,1,0:T(2,128)(2,1)}, bf16[34,1,256]{2,1,0:T(2,128)(2,1)S(1)}, u32[]{:S(2)}, u32[]{:S(2)}) collective-permute-start(bf16[34,1,256]{2,1,0:T(2,128)(2,1)} %get-tuple-element.87), channel_id=1, source_target_pairs={{0,1},{1,2},{2,3},{3,4},{4,5},{5,6},{6,7},{7,8},{8,9},{9,10},{10,1... | collective-permute-start | bytes 52232 | tf_op jit(solution)/shard_map/ppermute | solution.py:26
  227.1 65.7 %collective-permute-start.7 = (bf16[34,1,256]{2,1,0:T(2,128)(2,1)S(1)}, bf16[34,1,256]{2,1,0:T(2,128)(2,1)}, u32[]{:S(2)}, u32[]{:S(2)}) collective-permute-start(bf16[34,1,256]{2,1,0:T(2,128)(2,1)S(1)} %get-tuple-element.88), channel_id=1, source_target_pairs={{1,0},{2,1},{3,2},{4,3},{5,4},{6,5},{7,6},{8,7},{9,8},{10,9},{11,1... | collective-permute-start | bytes 52232 | tf_op jit(solution)/shard_map/ppermute | solution.py:28
  292.7 1.2 copy-start.15
  298.0 20.0 %copy-start.20 = (f32[256]{0:T(256)S(1)}, f32[256]{0:T(256)}, u32[]{:S(2)}) copy-start(f32[256]{0:T(256)} %get-tuple-element.9) | copy-start | bytes 3076
  317.9 1.4 copy-start.3
  317.9 1.6 copy-start.14
  319.4 1.2 copy-start.9
  (7 other events, 6.3 us)
Sparse Core Ops, SparseCore 0:
  319.5 275.9 all-reduce.21
where the time goes:
time: 615 us; the launch traced here: 612 us
  waiting for transfers between devices  274 us (45%)
  blocking collectives  208 us (34%)
  local copies, waits for them, and re-layouts  43.8 us (7%)
  starting transfers between devices  39.2 us (6%)
  matrix products  22.9 us (4%)
  between operations  15.2 us (2%)
  other arithmetic  8.34 us (1%)
    psum x1, waiting for transfers between devices, in_one(): so_far = lax.psum(jnp.concatenate([a.ravel() for a in arrays]), axis)  274 us
    psum x20, blocking collectives, one_axis_at_a_time(): return functools.reduce(lax.psum, axes, x)  208 us
    unnamed x52, local copies, waits for them, and re-layouts  27.1 us
    ppermute x8, starting transfers between devices, extended(): lax.ppermute(tail, axis, [(i, (i + 1) % count) for i in range(ends)])  24.2 us
    ppermute x8, starting transfers between devices, extended(): lax.ppermute(head, axis, [((i + 1) % count, i) for i in range(ends)])  15 us
  transfers between devices with their start and end apart: 17, of which 1 were waited for; matrix products, arithmetic and copies ran while one was open for 5% of the time, Pallas kernels for 0%

commit v1 on v0

v1 whole, which is shorter than its diff:
```python
import jax
import jax.numpy as jnp
from jax import lax
from jax.sharding import Mesh
from jax.sharding import PartitionSpec as P

GROUPS = 32
GY = ("gy_0", "gy_1")
GX = ("gx_0", "gx_1", "gx_2")
GY_GX = GY + GX
NEAR = ("gx_1", "gx_2")
FAR = ("gx_0", "gy_0", "gy_1")
STAGES = (("gx_2",), ("gx_0", "gy_0"), ("gx_1", "gy_1"))
LANES = 128
EPSILON = 1e-05


def exchanged(parts, axis):
    count = lax.axis_size(axis)
    up = [(i, i + 1) for i in range(count - 1)]
    down = [(i + 1, i) for i in range(count - 1)]
    heads = jnp.concatenate([head.reshape(-1, LANES) for head, _ in parts])
    tails = jnp.concatenate([tail.reshape(-1, LANES) for _, tail in parts])
    before = lax.ppermute(tails, axis, up)
    after = lax.ppermute(heads, axis, down)
    result, at = [], 0
    for head, _ in parts:
        rows = head.size // LANES
        result.append(
            (before[at : at + rows].reshape(head.shape), after[at : at + rows].reshape(head.shape))
        )
        at += rows
    return result


def with_rims(fine, coarse, wide, narrow):
    (f0, f1), (c0, c1) = exchanged(
        ((fine[:wide], fine[-wide:]), (coarse[:narrow], coarse[-narrow:])), GY
    )
    fine = jnp.concatenate([f0, fine, f1])
    coarse = jnp.concatenate([c0, coarse, c1])
    (f0, f1), (c0, c1) = exchanged(
        ((fine[:, :wide], fine[:, -wide:]), (coarse[:, :narrow], coarse[:, -narrow:])), GX
    )
    return jnp.concatenate([f0, fine, f1], axis=1), jnp.concatenate([c0, coarse, c1], axis=1)


def total(values):
    for axes in (NEAR, FAR):
        count = lax.axis_size(axes)
        copies = jnp.broadcast_to(values[None], (count,) + values.shape)
        values = jnp.sum(lax.all_to_all(copies, axes, 0, 0, tiled=True), axis=0)
    return values


def group_totals(first, second):
    pair = jnp.concatenate(
        [
            jnp.sum(first.reshape(GROUPS, -1), axis=1),
            jnp.sum(second.reshape(GROUPS, -1), axis=1),
            jnp.zeros((LANES - 2 * GROUPS,), jnp.float32),
        ]
    )
    sums = total(pair[None])[0]
    return sums[:GROUPS], sums[GROUPS : 2 * GROUPS]


def gradient_totals(rows):
    part = rows.astype(jnp.bfloat16)
    for axes in STAGES:
        count = lax.axis_size(axes)
        pieces = lax.all_to_all(
            part.reshape(count, -1, LANES), axes, 0, 0, tiled=True
        )
        part = jnp.sum(pieces.astype(jnp.float32), axis=0).astype(jnp.bfloat16)
    for axes in STAGES[::-1]:
        count = lax.axis_size(axes)
        copies = jnp.broadcast_to(part[None], (count,) + part.shape)
        part = lax.all_to_all(copies, axes, 0, 0, tiled=True).reshape(-1, LANES)
    return part


def conv_forward(padded, weight, height, width):
    channels = padded.shape[2]
    total = jnp.zeros((height * width, weight.shape[3]), jnp.float32)
    for row_tap in range(3):
        for col_tap in range(3):
            window = padded[row_tap : row_tap + height, col_tap : col_tap + width].reshape(
                height * width, channels
            )
            total = total + jnp.dot(
                window, weight[row_tap, col_tap], preferred_element_type=jnp.float32
            )
    return total.reshape(height, width, weight.shape[3])


def conv_transpose(padded, weight, height, width):
    channels = padded.shape[2]
    total = jnp.zeros((height * width, weight.shape[2]), jnp.float32)
    for row_tap in range(3):
        for col_tap in range(3):
            window = padded[
                2 - row_tap : 2 - row_tap + height, 2 - col_tap : 2 - col_tap + width
            ].reshape(height * width, channels)
            total = total + jnp.dot(
                window, weight[row_tap, col_tap].T, preferred_element_type=jnp.float32
            )
    return total.reshape(height, width, weight.shape[2])


def conv_weight(padded, grads, height, width):
    channels = padded.shape[2]
    flat_grads = grads.reshape(height * width, grads.shape[2])
    taps = []
    for row_tap in range(3):
        for col_tap in range(3):
            window = padded[row_tap : row_tap + height, col_tap : col_tap + width].reshape(
                height * width, channels
            )
            taps.append(
                lax.dot_general(
                    window, flat_grads, (((0,), (0,)), ((), ())), preferred_element_type=jnp.float32
                )
            )
    return jnp.stack(taps).reshape(9 * channels, grads.shape[2])


def inside(height, width, rim):
    row = lax.broadcasted_iota(jnp.int32, (height + 2 * rim, width + 2 * rim, 1), 0)
    col = lax.broadcasted_iota(jnp.int32, (height + 2 * rim, width + 2 * rim, 1), 1)
    row = row - rim + lax.axis_index(GY) * height
    col = col - rim + lax.axis_index(GX) * width
    rows, cols = height * lax.axis_size(GY), width * lax.axis_size(GX)
    return (row >= 0) & (row < rows) & (col >= 0) & (col < cols)


def upsample(values):
    rows, cols, channels = values.shape
    return jnp.broadcast_to(values[:, None, :, None, :], (rows, 2, cols, 2, channels)).reshape(
        2 * rows, 2 * cols, channels
    )


def per_channel(values, channels):
    return jnp.repeat(values, channels // GROUPS)


def silu_slope(act):
    sigma = jax.nn.sigmoid(act)
    return sigma * (1.0 + act * (1.0 - sigma))


def moments(first, second, count, channels):
    average = first / count
    inverse = lax.rsqrt(second / count - average * average + EPSILON)
    return per_channel(average, channels), per_channel(inverse, channels)


def on_device(field, cotangent, gain_fine, weight_fine, projection, gain_coarse, weight_coarse):
    height, width, chan_fine = field.shape
    chan_coarse = projection.shape[1]
    half_h, half_w = (height // 2, width // 2)
    cells_all = height * width * lax.axis_size(GY_GX)
    fine_count = cells_all * (chan_fine // GROUPS)
    coarse_count = cells_all // 4 * (chan_coarse // GROUPS)

    values = field.astype(jnp.float32)
    first, second = group_totals(
        jnp.sum(values, axis=(0, 1)), jnp.sum(values * values, axis=(0, 1))
    )
    wide_field, wide_grad = with_rims(field, cotangent, 3, 2)

    mean_fine, inverse_fine = moments(first, second, fine_count, chan_fine)
    wide_values = wide_field.astype(jnp.float32)
    wide_act = (wide_values - mean_fine) * inverse_fine * gain_fine
    hidden_fine = jnp.where(inside(height, width, 3), jax.nn.silu(wide_act), 0.0).astype(
        jnp.bfloat16
    )
    block_fine = (
        wide_values[1:-1, 1:-1] + conv_forward(hidden_fine, weight_fine, height + 4, width + 4)
    ).astype(jnp.bfloat16)
    pooled = jnp.mean(
        block_fine.astype(jnp.float32).reshape(half_h + 2, 2, half_w + 2, 2, chan_fine),
        axis=(1, 3),
    ).astype(jnp.bfloat16)
    coarse_in = (
        jnp.dot(pooled.reshape(-1, chan_fine), projection, preferred_element_type=jnp.float32)
        .reshape(half_h + 2, half_w + 2, chan_coarse)
        .astype(jnp.bfloat16)
    )
    wide_coarse = coarse_in.astype(jnp.float32)
    coarse_vals = wide_coarse[1:-1, 1:-1]
    first, second = group_totals(
        jnp.sum(coarse_vals, axis=(0, 1)), jnp.sum(coarse_vals * coarse_vals, axis=(0, 1))
    )

    mean_coarse, inverse_coarse = moments(first, second, coarse_count, chan_coarse)
    in_coarse = inside(half_h, half_w, 1)
    normed_coarse = (wide_coarse - mean_coarse) * inverse_coarse
    act_coarse = normed_coarse * gain_coarse
    hidden_coarse = jnp.where(in_coarse, jax.nn.silu(act_coarse), 0.0).astype(jnp.bfloat16)
    coarse_output = (
        coarse_vals + conv_forward(hidden_coarse, weight_coarse, half_h, half_w)
    ).astype(jnp.bfloat16)
    dact_coarse = conv_transpose(
        wide_grad, weight_coarse, half_h + 2, half_w + 2
    ) * silu_slope(act_coarse)
    dnorm = dact_coarse * gain_coarse
    own = (slice(1, -1), slice(1, -1))
    coarse_gain_grad = jnp.sum(dact_coarse[own] * normed_coarse[own], axis=(0, 1))
    first, second = group_totals(
        jnp.sum(dnorm[own], axis=(0, 1)), coarse_gain_grad * gain_coarse
    )
    coarse_weight_grad = conv_weight(hidden_coarse, cotangent, half_h, half_w)
    dcoarse = wide_grad[1:-1, 1:-1].astype(jnp.float32) + inverse_coarse * (
        dnorm
        - per_channel(first / coarse_count, chan_coarse)
        - normed_coarse * per_channel(second / coarse_count, chan_coarse)
    )
    dcoarse = jnp.where(in_coarse, dcoarse, 0.0).astype(jnp.bfloat16)
    projection_grad = lax.dot_general(
        pooled[own].reshape(-1, chan_fine),
        dcoarse[own].reshape(-1, chan_coarse),
        (((0,), (0,)), ((), ())),
        preferred_element_type=jnp.float32,
    )
    small_dblock = (
        jnp.dot(
            dcoarse.reshape(-1, chan_coarse), projection.T, preferred_element_type=jnp.float32
        ).reshape(half_h + 2, half_w + 2, chan_fine)
        * 0.25
    ).astype(jnp.bfloat16)
    wide_dblock = upsample(small_dblock)[1:-1, 1:-1]
    dblock = wide_dblock[1:-1, 1:-1]

    hidden_own = hidden_fine[2:-2, 2:-2]
    fine_weight_grad = conv_weight(hidden_own, dblock, height, width)
    normed_fine = (values - mean_fine) * inverse_fine
    act_fine = normed_fine * gain_fine
    dact_fine = conv_transpose(wide_dblock, weight_fine, height, width) * silu_slope(act_fine)
    dnorm = dact_fine * gain_fine
    fine_gain_grad = jnp.sum(dact_fine * normed_fine, axis=(0, 1))
    first = jnp.sum(jnp.sum(dnorm, axis=(0, 1)).reshape(GROUPS, -1), axis=1)
    second = jnp.sum((fine_gain_grad * gain_fine).reshape(GROUPS, -1), axis=1)
    small = jnp.concatenate(
        [
            fine_gain_grad,
            coarse_gain_grad,
            first,
            second,
            jnp.zeros((LANES - 2 * GROUPS,), jnp.float32),
        ]
    )
    sums = total(small.reshape(-1, LANES)).reshape(-1)
    fine_gain_grad, coarse_gain_grad, first, second = jnp.split(
        sums[: chan_fine + chan_coarse + 2 * GROUPS],
        [chan_fine, chan_fine + chan_coarse, chan_fine + chan_coarse + GROUPS],
    )
    field_grad = (
        dblock.astype(jnp.float32)
        + inverse_fine
        * (
            dnorm
            - per_channel(first / fine_count, chan_fine)
            - normed_fine * per_channel(second / fine_count, chan_fine)
        )
    ).astype(jnp.bfloat16)

    tall = 9 * chan_coarse
    rows = [
        coarse_weight_grad[:, :LANES],
        coarse_weight_grad[:, LANES:],
        fine_weight_grad,
        projection_grad[:, :LANES],
        projection_grad[:, LANES:],
    ]
    used = sum(r.shape[0] for r in rows)
    devices = lax.axis_size(GY_GX)
    spare = -used % (4 * devices)
    grads = gradient_totals(
        jnp.concatenate(
            [r.astype(jnp.bfloat16) for r in rows] + [jnp.zeros((spare, LANES), jnp.bfloat16)]
        )
    ).astype(jnp.float32)
    at, pieces = 0, []
    for r in rows:
        pieces.append(grads[at : at + r.shape[0]])
        at += r.shape[0]
    return (
        coarse_output,
        field_grad,
        pieces[2].reshape(weight_fine.shape),
        fine_gain_grad,
        jnp.concatenate(pieces[3:], axis=1),
        jnp.concatenate(pieces[:2], axis=1).reshape(weight_coarse.shape),
        coarse_gain_grad,
    )


def solution(mesh):
    finer = Mesh(mesh.devices.reshape(2, 8, 2, 8, 2), GY_GX)
    in_specs = (P(GY, GX, None), P(GY, GX, None), P(), P(), P(), P(), P())
    out_specs = (P(GY, GX, None), P(GY, GX, None), P(), P(), P(), P(), P())
    return jax.shard_map(
        on_device, mesh=finer, in_specs=in_specs, out_specs=out_specs, check_vma=False
    )
```

time: 615 us -> 274 us (0.45)
  blocking collectives: 208 us -> 15.9 us
  waiting for transfers between devices: 274 us -> 83.2 us
  starting transfers between devices: 39.2 us -> 86.6 us
  between operations: 15.2 us -> 2.19 us
    psum x1 -> x0, waiting for transfers between devices: 274 us -> none  [in_one(): so_far = lax.psum(jnp.concatenate([a.ravel() for a in arrays]), axis)]
    psum x20 -> x0, blocking collectives: 208 us -> none  [one_axis_at_a_time(): return functools.reduce(lax.psum, axes, x)]
    all_to_all x0 -> x12, waiting for transfers between devices: none -> 82.5 us  [the longest x8 46.1 us: total(): values = jnp.sum(lax.all_to_all(copies, axes, 0, 0, tiled=True), axis=0)]
    all_to_all x0 -> x12, starting transfers between devices: none -> 75 us  [the longest x8 58.3 us: total(): values = jnp.sum(lax.all_to_all(copies, axes, 0, 0, tiled=True), axis=0)]
    ppermute x16 -> x4, starting transfers between devices: 39.1 us -> 11.6 us  [the longest x2 8.44 us: exchanged(): before = lax.ppermute(tails, axis, up)]
    unnamed x52 -> x101, local copies, waits for them, and re-layouts: 27.1 us -> 8.81 us
    all_to_all x0 -> x2, blocking collectives: none -> 15.9 us  [the longest x1 9.5 us: gradient_totals(): part = lax.all_to_all(copies, axes, 0, 0, tiled=True).reshape(-1, LANES)]
    reshape x2 -> x50, local copies, waits for them, and re-layouts: 2.44 us -> 16 us  [the longest x9 5.92 us: conv_transpose(): window = padded[2 - row_tap:2 - row_tap + height, 2 - col_tap:2 - col_tap...]
  transfers between devices with their start and end apart: 17 -> 16, of which waited for: 1 -> 13; matrix products, arithmetic and copies ran while one was open for 5% -> 9% of each run, Pallas kernels for 0% -> 0%
where the time goes in v1:
time: 274 us; the launch traced here: 273 us
  starting transfers between devices  86.6 us (32%)
  waiting for transfers between devices  83.2 us (30%)
  local copies, waits for them, and re-layouts  47.6 us (17%)
  matrix products  22.8 us (8%)
  blocking collectives  15.9 us (6%)
  other arithmetic  14.3 us (5%)
    all_to_all x8, starting transfers between devices, total(): values = jnp.sum(lax.all_to_all(copies, axes, 0, 0, tiled=True), axis=0)  58.3 us
    all_to_all x8, waiting for transfers between devices, total(): values = jnp.sum(lax.all_to_all(copies, axes, 0, 0, tiled=True), axis=0)  46.1 us
    all_to_all x2, waiting for transfers between devices, gradient_totals(): lax.all_to_all(part.reshape(count, -1, LANES), axes, 0, 0, tiled=True)  19.1 us
    all_to_all x2, waiting for transfers between devices, gradient_totals(): part = lax.all_to_all(copies, axes, 0, 0, tiled=True).reshape(-1, LANES)  17.3 us
    dot_general x18, matrix products, conv_forward(): jnp.dot(window, weight[row_tap, col_tap], preferred_element_type=jnp.floa...  12.6 us
    all_to_all x1, blocking collectives, gradient_totals(): part = lax.all_to_all(copies, axes, 0, 0, tiled=True).reshape(-1, LANES)  9.5 us
    unnamed x101, local copies, waits for them, and re-layouts  8.81 us
    all_to_all x2, starting transfers between devices, gradient_totals(): lax.all_to_all(part.reshape(count, -1, LANES), axes, 0, 0, tiled=True)  8.47 us
  transfers between devices with their start and end apart: 16, of which 13 were waited for; matrix products, arithmetic and copies ran while one was open for 9% of the time, Pallas kernels for 0%

profile of v1, /device:TPU:1, one launch (start us, length us, event | category | flops | bytes accessed | tf_op | source)
XLA Modules:
  0.0 272.6 jit_solution(5080567660604994240)
XLA Ops:
  3.5 5.4 %collective-permute-start = (bf16[80,128]{1,0:T(8,128)(2,1)S(1)}, bf16[80,128]{1,0:T(8,128)(2,1)S(1)}, u32[]{:S(2)}, u32[]{:S(2)}) collective-permute-start(bf16[80,128]{1,0:T(8,128)(2,1)S(1)} %pad_maximum_fusion.12), channel_id=1, source_target_pairs={{0,32},{32,64},{64,96},{96,128},{128,160},{160,192},{192,224},{224... | collective-permute-start | bytes 61448 | tf_op jit(solution)/shard_map/ppermute | solution.py:24
  11.2 9.2 %all-to-all-start = ((f32[16,1,128]{2,1,0:T(1,128)}), f32[16,1,128]{2,1,0:T(1,128)S(1)}, u32[]{:S(2)}, u32[]{:S(2)}) async-start(f32[16,1,128]{2,1,0:T(1,128)} %broadcast_in_dim.133), calls=%async_computation | async-start | bytes 16384 | tf_op jit(solution)/shard_map/all_to_all | solution.py:52
  23.0 4.4 %all-to-all-done = f32[16,1,128]{2,1,0:T(1,128)S(1)} async-done(((f32[16,1,128]{2,1,0:T(1,128)}), f32[16,1,128]{2,1,0:T(1,128)S(1)}, u32[]{:S(2)}, u32[]{:S(2)}) %all-to-all-start) | async-done | bytes 8224 | tf_op jit(solution)/shard_map/all_to_all | solution.py:52
  28.0 13.5 %all-to-all-start.1 = ((f32[32,1,128]{2,1,0:T(1,128)}), f32[32,1,128]{2,1,0:T(1,128)S(1)}, u32[]{:S(2)}, u32[]{:S(2)}) async-start(f32[32,1,128]{2,1,0:T(1,128)} %broadcast_in_dim.134), calls=%async_computation.1 | async-start | bytes 32768 | tf_op jit(solution)/shard_map/all_to_all | solution.py:52
  41.9 3.0 %collective-permute-start.2 = (bf16[354,128]{1,0:T(8,128)(2,1)S(1)}, bf16[354,128]{1,0:T(8,128)(2,1)S(1)}, u32[]{:S(2)}, u32[]{:S(2)}) collective-permute-start(bf16[354,128]{1,0:T(8,128)(2,1)S(1)} %pad_maximum_fusion.4), channel_id=1, source_target_pairs={{0,1},{1,2},{2,3},{3,4},{4,5},{5,6},{6,7},{7,8},{8,9},{9,10},{10,1... | collective-permute-start | bytes 271880 | tf_op jit(solution)/shard_map/ppermute | solution.py:24
  45.1 1.9 collective-permute-start.3
  47.1 3.0 %all-to-all-done.1 = f32[32,1,128]{2,1,0:T(1,128)S(1)} async-done(((f32[32,1,128]{2,1,0:T(1,128)}), f32[32,1,128]{2,1,0:T(1,128)S(1)}, u32[]{:S(2)}, u32[]{:S(2)}) %all-to-all-start.1) | async-done | bytes 16416 | tf_op jit(solution)/shard_map/all_to_all | solution.py:52
  78.8 1.7 reduce_sum.274
  81.9 10.1 %all-to-all-start.2 = ((f32[16,1,128]{2,1,0:T(1,128)}), f32[16,1,128]{2,1,0:T(1,128)S(1)}, u32[]{:S(2)}, u32[]{:S(2)}) async-start(f32[16,1,128]{2,1,0:T(1,128)} %broadcast_in_dim.139), calls=%async_computation.2 | async-start | bytes 16384 | tf_op jit(solution)/shard_map/all_to_all | solution.py:52
  95.6 3.5 %all-to-all-done.2 = f32[16,1,128]{2,1,0:T(1,128)S(1)} async-done(((f32[16,1,128]{2,1,0:T(1,128)}), f32[16,1,128]{2,1,0:T(1,128)S(1)}, u32[]{:S(2)}, u32[]{:S(2)}) %all-to-all-start.2) | async-done | bytes 8224 | tf_op jit(solution)/shard_map/all_to_all | solution.py:52
  99.7 7.0 %all-to-all-start.3 = ((f32[32,1,128]{2,1,0:T(1,128)}), f32[32,1,128]{2,1,0:T(1,128)S(1)}, u32[]{:S(2)}, u32[]{:S(2)}) async-start(f32[32,1,128]{2,1,0:T(1,128)} %broadcast_in_dim.140), calls=%async_computation.3 | async-start | bytes 32768 | tf_op jit(solution)/shard_map/all_to_all | solution.py:52
  107.8 7.3 %all-to-all-done.3 = f32[32,1,128]{2,1,0:T(1,128)S(1)} async-done(((f32[32,1,128]{2,1,0:T(1,128)}), f32[32,1,128]{2,1,0:T(1,128)S(1)}, u32[]{:S(2)}, u32[]{:S(2)}) %all-to-all-start.3) | async-done | bytes 16416 | tf_op jit(solution)/shard_map/all_to_all | solution.py:52
  118.7 5.3 %all-to-all-start.4 = ((f32[16,1,128]{2,1,0:T(1,128)}), f32[16,1,128]{2,1,0:T(1,128)S(1)}, u32[]{:S(2)}, u32[]{:S(2)}) async-start(f32[16,1,128]{2,1,0:T(1,128)} %broadcast_in_dim.144), calls=%async_computation.4 | async-start | bytes 16384 | tf_op jit(solution)/shard_map/all_to_all | solution.py:52
  124.1 7.0 %all-to-all-done.4 = f32[16,1,128]{2,1,0:T(1,128)S(1)} async-done(((f32[16,1,128]{2,1,0:T(1,128)}), f32[16,1,128]{2,1,0:T(1,128)S(1)}, u32[]{:S(2)}, u32[]{:S(2)}) %all-to-all-start.4) | async-done | bytes 8224 | tf_op jit(solution)/shard_map/all_to_all | solution.py:52
  131.7 3.8 %all-to-all-start.5 = ((f32[32,1,128]{2,1,0:T(1,128)}), f32[32,1,128]{2,1,0:T(1,128)S(1)}, u32[]{:S(2)}, u32[]{:S(2)}) async-start(f32[32,1,128]{2,1,0:T(1,128)} %broadcast_in_dim.145), calls=%async_computation.5 | async-start | bytes 32768 | tf_op jit(solution)/shard_map/all_to_all | solution.py:52
  135.7 8.5 %all-to-all-done.5 = f32[32,1,128]{2,1,0:T(1,128)S(1)} async-done(((f32[32,1,128]{2,1,0:T(1,128)}), f32[32,1,128]{2,1,0:T(1,128)S(1)}, u32[]{:S(2)}, u32[]{:S(2)}) %all-to-all-start.5) | async-done | bytes 16416 | tf_op jit(solution)/shard_map/all_to_all | solution.py:52
  159.9 6.4 %all_to_all.70 = bf16[2,3072,128]{2,1,0:T(8,128)(2,1)S(1)} all-to-all(bf16[2,3072,128]{2,1,0:T(8,128)(2,1)S(1)} %bitcast.379), channel_id=1, replica_groups=mesh['gy_0'=2,'gy_1'=8,'gx_0'=2,'gx_1'=8,'gx_2'=2] {'gx_2'}, dimensions={0} | all-to-all | bytes 3145728 | tf_op jit(solution)/shard_map/all_to_all | solution.py:72
  167.7 3.6 %all-to-all-start.9 = ((bf16[4,768,128]{2,1,0:T(8,128)(2,1)}), bf16[4,768,128]{2,1,0:T(8,128)(2,1)S(1)}, u32[]{:S(2)}, u32[]{:S(2)}) async-start(bf16[4,768,128]{2,1,0:T(8,128)(2,1)} %bitcast.377), calls=%async_computation.9 | async-start | bytes 1572864 | tf_op jit(solution)/shard_map/all_to_all | solution.py:72
  174.4 1.8 convolution_add_fusion.28
  176.2 7.1 %all-to-all-done.9 = bf16[4,768,128]{2,1,0:T(8,128)(2,1)S(1)} async-done(((bf16[4,768,128]{2,1,0:T(8,128)(2,1)}), bf16[4,768,128]{2,1,0:T(8,128)(2,1)S(1)}, u32[]{:S(2)}, u32[]{:S(2)}) %all-to-all-start.9) | async-done | bytes 786464 | tf_op jit(solution)/shard_map/all_to_all | solution.py:72
  183.9 4.5 %all-to-all-start.6 = ((f32[16,4,128]{2,1,0:T(4,128)}), f32[16,4,128]{2,1,0:T(4,128)S(1)}, u32[]{:S(2)}, u32[]{:S(2)}) async-start(f32[16,4,128]{2,1,0:T(4,128)} %broadcast_in_dim.150), calls=%async_computation.6 | async-start | bytes 65536 | tf_op jit(solution)/shard_map/all_to_all | solution.py:52
  190.4 1.7 reshape.481
  192.1 3.8 %all-to-all-done.6 = f32[16,4,128]{2,1,0:T(4,128)S(1)} async-done(((f32[16,4,128]{2,1,0:T(4,128)}), f32[16,4,128]{2,1,0:T(4,128)S(1)}, u32[]{:S(2)}, u32[]{:S(2)}) %all-to-all-start.6) | async-done | bytes 32800 | tf_op jit(solution)/shard_map/all_to_all | solution.py:52
  195.9 4.8 %all-to-all-start.10 = ((bf16[64,12,128]{2,1,0:T(8,128)(2,1)}), bf16[64,12,128]{2,1,0:T(8,128)(2,1)S(1)}, u32[]{:S(2)}, u32[]{:S(2)}) async-start(bf16[64,12,128]{2,1,0:T(8,128)(2,1)} %reshape.481), calls=%async_computation.10 | async-start | bytes 524288 | tf_op jit(solution)/shard_map/all_to_all | solution.py:72
  202.1 12.0 %all-to-all-done.10 = bf16[64,12,128]{2,1,0:T(8,128)(2,1)S(1)} async-done(((bf16[64,12,128]{2,1,0:T(8,128)(2,1)}), bf16[64,12,128]{2,1,0:T(8,128)(2,1)S(1)}, u32[]{:S(2)}, u32[]{:S(2)}) %all-to-all-start.10) | async-done | bytes 196640 | tf_op jit(solution)/shard_map/all_to_all | solution.py:72
  214.8 4.8 %all-to-all-start.7 = ((f32[32,4,128]{2,1,0:T(4,128)}), f32[32,4,128]{2,1,0:T(4,128)S(1)}, u32[]{:S(2)}, u32[]{:S(2)}) async-start(f32[32,4,128]{2,1,0:T(4,128)} %broadcast_in_dim.151), calls=%async_computation.7 | async-start | bytes 131072 | tf_op jit(solution)/shard_map/all_to_all | solution.py:52
  219.9 8.7 %all-to-all-done.7 = f32[32,4,128]{2,1,0:T(4,128)S(1)} async-done(((f32[32,4,128]{2,1,0:T(4,128)}), f32[32,4,128]{2,1,0:T(4,128)S(1)}, u32[]{:S(2)}, u32[]{:S(2)}) %all-to-all-start.7) | async-done | bytes 65568 | tf_op jit(solution)/shard_map/all_to_all | solution.py:52
  229.3 4.7 %all-to-all-start.11 = ((bf16[64,12,128]{2,1,0:T(8,128)(2,1)}), bf16[64,12,128]{2,1,0:T(8,128)(2,1)S(1)}, u32[]{:S(2)}, u32[]{:S(2)}) async-start(bf16[64,12,128]{2,1,0:T(8,128)(2,1)} %broadcast_in_dim.155), calls=%async_computation.11 | async-start | bytes 524288 | tf_op jit(solution)/shard_map/all_to_all | solution.py:79
  235.4 11.1 %all-to-all-done.11 = bf16[64,12,128]{2,1,0:T(8,128)(2,1)S(1)} async-done(((bf16[64,12,128]{2,1,0:T(8,128)(2,1)}), bf16[64,12,128]{2,1,0:T(8,128)(2,1)S(1)}, u32[]{:S(2)}, u32[]{:S(2)}) %all-to-all-start.11) | async-done | bytes 196640 | tf_op jit(solution)/shard_map/all_to_all | solution.py:79
  247.5 3.5 %all-to-all-start.12 = ((bf16[4,768,128]{2,1,0:T(8,128)(2,1)}), bf16[4,768,128]{2,1,0:T(8,128)(2,1)S(1)}, u32[]{:S(2)}, u32[]{:S(2)}) async-start(bf16[4,768,128]{2,1,0:T(8,128)(2,1)} %broadcast_in_dim.157), calls=%async_computation.12 | async-start | bytes 1572864 | tf_op jit(solution)/shard_map/all_to_all | solution.py:79
  253.3 6.1 %all-to-all-done.12 = bf16[4,768,128]{2,1,0:T(8,128)(2,1)S(1)} async-done(((bf16[4,768,128]{2,1,0:T(8,128)(2,1)}), bf16[4,768,128]{2,1,0:T(8,128)(2,1)S(1)}, u32[]{:S(2)}, u32[]{:S(2)}) %all-to-all-start.12) | async-done | bytes 786464 | tf_op jit(solution)/shard_map/all_to_all | solution.py:79
  259.5 9.5 %all_to_all.71 = bf16[2,3072,128]{2,1,0:T(8,128)(2,1)S(1)} all-to-all(bf16[2,3072,128]{2,1,0:T(8,128)(2,1)S(1)} %broadcast_in_dim.159), channel_id=1, replica_groups=mesh['gy_0'=2,'gy_1'=8,'gx_0'=2,'gx_1'=8,'gx_2'=2] {'gx_2'}, dimensions={0} | all-to-all | bytes 3145728 | tf_op jit(solution)/shard_map/all_to_all | solution.py:79
  (355 shorter events, 81.4 us)
Async XLA Ops:
  0.6 79.9 %copy-start = (bf16[128,256]{1,0:T(8,128)(2,1)S(1)}, bf16[128,256]{1,0:T(8,128)(2,1)}, u32[]{:S(2)}) copy-start(bf16[128,256]{1,0:T(8,128)(2,1)} %param.11) | copy-start | bytes 196612
  2.1 39.4 %collective-permute-start.1 = (bf16[80,128]{1,0:T(8,128)(2,1)S(1)}, bf16[80,128]{1,0:T(8,128)(2,1)S(1)}, u32[]{:S(2)}, u32[]{:S(2)}) collective-permute-start(bf16[80,128]{1,0:T(8,128)(2,1)S(1)} %pad_maximum_fusion.13), channel_id=1, source_target_pairs={{32,0},{64,32},{96,64},{128,96},{160,128},{192,160},{224,192},{256... | collective-permute-start | bytes 61448 | tf_op jit(solution)/shard_map/ppermute | solution.py:25
  3.5 38.1 %collective-permute-start = (bf16[80,128]{1,0:T(8,128)(2,1)S(1)}, bf16[80,128]{1,0:T(8,128)(2,1)S(1)}, u32[]{:S(2)}, u32[]{:S(2)}) collective-permute-start(bf16[80,128]{1,0:T(8,128)(2,1)S(1)} %pad_maximum_fusion.12), channel_id=1, source_target_pairs={{0,32},{32,64},{64,96},{96,128},{128,160},{160,192},{192,224},{224... | collective-permute-start | bytes 61448 | tf_op jit(solution)/shard_map/ppermute | solution.py:24
  10.5 31.4 %copy-start.35 = (f32[64]{0:T(128)}, f32[64]{0:T(128)S(1)}, u32[]{:S(2)}) copy-start(f32[64]{0:T(128)S(1)} %broadcast.198) | copy-start | bytes 772
  11.2 16.2 %all-to-all-start = ((f32[16,1,128]{2,1,0:T(1,128)}), f32[16,1,128]{2,1,0:T(1,128)S(1)}, u32[]{:S(2)}, u32[]{:S(2)}) async-start(f32[16,1,128]{2,1,0:T(1,128)} %broadcast_in_dim.133), calls=%async_computation | async-start | bytes 16384 | tf_op jit(solution)/shard_map/all_to_all | solution.py:52
  28.0 22.1 %all-to-all-start.1 = ((f32[32,1,128]{2,1,0:T(1,128)}), f32[32,1,128]{2,1,0:T(1,128)S(1)}, u32[]{:S(2)}, u32[]{:S(2)}) async-start(f32[32,1,128]{2,1,0:T(1,128)} %broadcast_in_dim.134), calls=%async_computation.1 | async-start | bytes 32768 | tf_op jit(solution)/shard_map/all_to_all | solution.py:52
  41.9 8.6 %collective-permute-start.2 = (bf16[354,128]{1,0:T(8,128)(2,1)S(1)}, bf16[354,128]{1,0:T(8,128)(2,1)S(1)}, u32[]{:S(2)}, u32[]{:S(2)}) collective-permute-start(bf16[354,128]{1,0:T(8,128)(2,1)S(1)} %pad_maximum_fusion.4), channel_id=1, source_target_pairs={{0,1},{1,2},{2,3},{3,4},{4,5},{5,6},{6,7},{7,8},{8,9},{9,10},{10,1... | collective-permute-start | bytes 271880 | tf_op jit(solution)/shard_map/ppermute | solution.py:24
  45.1 6.2 %collective-permute-start.3 = (bf16[354,128]{1,0:T(8,128)(2,1)S(1)}, bf16[354,128]{1,0:T(8,128)(2,1)S(1)}, u32[]{:S(2)}, u32[]{:S(2)}) collective-permute-start(bf16[354,128]{1,0:T(8,128)(2,1)S(1)} %pad_maximum_fusion.5), channel_id=1, source_target_pairs={{1,0},{2,1},{3,2},{4,3},{5,4},{6,5},{7,6},{8,7},{9,8},{10,9},{11,1... | collective-permute-start | bytes 271880 | tf_op jit(solution)/shard_map/ppermute | solution.py:25
  50.4 8.6 %copy-start.38 = (f32[128]{0:T(128)}, f32[128]{0:T(128)S(1)}, u32[]{:S(2)}) copy-start(f32[128]{0:T(128)S(1)} %mul.181) | copy-start | bytes 1540
  50.6 8.4 %copy-start.40 = (f32[128]{0:T(128)}, f32[128]{0:T(128)S(1)}, u32[]{:S(2)}) copy-start(f32[128]{0:T(128)S(1)} %sub.84) | copy-start | bytes 1540
  78.8 13.3 %copy-start.2 = (bf16[3,3,256,256]{3,2,1,0:T(8,128)(2,1)S(1)}, bf16[3,3,256,256]{3,2,1,0:T(8,128)(2,1)}, u32[]{:S(2)}) copy-start(bf16[3,3,256,256]{3,2,1,0:T(8,128)(2,1)} %param.13) | copy-start | bytes 3538948
  78.8 13.3 %copy-start.18 = (bf16[340,256]{1,0:T(8,128)(2,1)S(1)}, bf16[340,256]{1,0:T(8,128)(2,1)}, u32[]{:S(2)}) copy-start(bf16[340,256]{1,0:T(8,128)(2,1)} %reshape.452) | copy-start | bytes 522244
  80.5 11.9 %copy-start.19 = (bf16[340,256]{1,0:T(8,128)(2,1)S(1)}, bf16[340,256]{1,0:T(8,128)(2,1)}, u32[]{:S(2)}) copy-start(bf16[340,256]{1,0:T(8,128)(2,1)} %reshape.453) | copy-start | bytes 522244
  80.5 12.1 %copy-start.20 = (bf16[340,256]{1,0:T(8,128)(2,1)S(1)}, bf16[340,256]{1,0:T(8,128)(2,1)}, u32[]{:S(2)}) copy-start(bf16[340,256]{1,0:T(8,128)(2,1)} %reshape.454) | copy-start | bytes 522244
  81.9 17.1 %all-to-all-start.2 = ((f32[16,1,128]{2,1,0:T(1,128)}), f32[16,1,128]{2,1,0:T(1,128)S(1)}, u32[]{:S(2)}, u32[]{:S(2)}) async-start(f32[16,1,128]{2,1,0:T(1,128)} %broadcast_in_dim.139), calls=%async_computation.2 | async-start | bytes 16384 | tf_op jit(solution)/shard_map/all_to_all | solution.py:52
  95.5 20.0 %copy-start.34 = (f32[256]{0:T(256)S(1)}, f32[256]{0:T(256)}, u32[]{:S(2)}) copy-start(f32[256]{0:T(256)} %param.12) | copy-start | bytes 3076
  99.7 15.4 %all-to-all-start.3 = ((f32[32,1,128]{2,1,0:T(1,128)}), f32[32,1,128]{2,1,0:T(1,128)S(1)}, u32[]{:S(2)}, u32[]{:S(2)}) async-start(f32[32,1,128]{2,1,0:T(1,128)} %broadcast_in_dim.140), calls=%async_computation.3 | async-start | bytes 32768 | tf_op jit(solution)/shard_map/all_to_all | solution.py:52
  115.5 20.0 %copy-start.44 = (pred[10]{0:T(512)(128)(4,1)S(1)}, pred[10]{0:T(512)(128)(4,1)}, u32[]{:S(2)}) copy-start(pred[10]{0:T(512)(128)(4,1)} %get-tuple-element.106) | copy-start | bytes 34
  115.6 20.0 %copy-start.45 = (pred[10]{0:T(512)(128)(4,1)S(1)}, pred[10]{0:T(512)(128)(4,1)}, u32[]{:S(2)}) copy-start(pred[10]{0:T(512)(128)(4,1)} %get-tuple-element.107) | copy-start | bytes 34
  118.7 12.4 %all-to-all-start.4 = ((f32[16,1,128]{2,1,0:T(1,128)}), f32[16,1,128]{2,1,0:T(1,128)S(1)}, u32[]{:S(2)}, u32[]{:S(2)}) async-start(f32[16,1,128]{2,1,0:T(1,128)} %broadcast_in_dim.144), calls=%async_computation.4 | async-start | bytes 16384 | tf_op jit(solution)/shard_map/all_to_all | solution.py:52
  131.7 12.4 %all-to-all-start.5 = ((f32[32,1,128]{2,1,0:T(1,128)}), f32[32,1,128]{2,1,0:T(1,128)S(1)}, u32[]{:S(2)}, u32[]{:S(2)}) async-start(f32[32,1,128]{2,1,0:T(1,128)} %broadcast_in_dim.145), calls=%async_computation.5 | async-start | bytes 32768 | tf_op jit(solution)/shard_map/all_to_all | solution.py:52
  167.7 3.7 %copy-start.29 = (bf16[32,8,256]{2,0,1:T(8,128)(2,1)S(1)}, bf16[32,8,256]{2,0,1:T(8,128)(2,1)}, u32[]{:S(2)}) copy-start(bf16[32,8,256]{2,0,1:T(8,128)(2,1)} %get-tuple-element.83) | copy-start | bytes 393220
  167.7 15.6 %all-to-all-start.9 = ((bf16[4,768,128]{2,1,0:T(8,128)(2,1)}), bf16[4,768,128]{2,1,0:T(8,128)(2,1)S(1)}, u32[]{:S(2)}, u32[]{:S(2)}) async-start(bf16[4,768,128]{2,1,0:T(8,128)(2,1)} %bitcast.377), calls=%async_computation.9 | async-start | bytes 1572864 | tf_op jit(solution)/shard_map/all_to_all | solution.py:72
  171.6 16.8 %copy-start.28 = (bf16[32,8,256]{2,0,1:T(8,128)(2,1)S(1)}, bf16[32,8,256]{2,0,1:T(8,128)(2,1)}, u32[]{:S(2)}) copy-start(bf16[32,8,256]{2,0,1:T(8,128)(2,1)} %get-tuple-element.79) | copy-start | bytes 393220
  183.9 12.0 %all-to-all-start.6 = ((f32[16,4,128]{2,1,0:T(4,128)}), f32[16,4,128]{2,1,0:T(4,128)S(1)}, u32[]{:S(2)}, u32[]{:S(2)}) async-start(f32[16,4,128]{2,1,0:T(4,128)} %broadcast_in_dim.150), calls=%async_computation.6 | async-start | bytes 65536 | tf_op jit(solution)/shard_map/all_to_all | solution.py:52
  190.4 11.5 %copy-start.27 = (bf16[32,8,256]{2,0,1:T(8,128)(2,1)S(1)}, bf16[32,8,256]{2,0,1:T(8,128)(2,1)}, u32[]{:S(2)}) copy-start(bf16[32,8,256]{2,0,1:T(8,128)(2,1)} %get-tuple-element.77) | copy-start | bytes 393220
  192.1 27.5 %copy-start.26 = (bf16[32,8,256]{2,0,1:T(8,128)(2,1)S(1)}, bf16[32,8,256]{2,0,1:T(8,128)(2,1)}, u32[]{:S(2)}) copy-start(bf16[32,8,256]{2,0,1:T(8,128)(2,1)} %get-tuple-element.76) | copy-start | bytes 393220
  195.9 18.3 %all-to-all-start.10 = ((bf16[64,12,128]{2,1,0:T(8,128)(2,1)}), bf16[64,12,128]{2,1,0:T(8,128)(2,1)S(1)}, u32[]{:S(2)}, u32[]{:S(2)}) async-start(bf16[64,12,128]{2,1,0:T(8,128)(2,1)} %reshape.481), calls=%async_computation.10 | async-start | bytes 524288 | tf_op jit(solution)/shard_map/all_to_all | solution.py:72
  214.8 13.8 %all-to-all-start.7 = ((f32[32,4,128]{2,1,0:T(4,128)}), f32[32,4,128]{2,1,0:T(4,128)S(1)}, u32[]{:S(2)}, u32[]{:S(2)}) async-start(f32[32,4,128]{2,1,0:T(4,128)} %broadcast_in_dim.151), calls=%async_computation.7 | async-start | bytes 131072 | tf_op jit(solution)/shard_map/all_to_all | solution.py:52
  229.3 17.2 %all-to-all-start.11 = ((bf16[64,12,128]{2,1,0:T(8,128)(2,1)}), bf16[64,12,128]{2,1,0:T(8,128)(2,1)S(1)}, u32[]{:S(2)}, u32[]{:S(2)}) async-start(bf16[64,12,128]{2,1,0:T(8,128)(2,1)} %broadcast_in_dim.155), calls=%async_computation.11 | async-start | bytes 524288 | tf_op jit(solution)/shard_map/all_to_all | solution.py:79
  246.6 4.5 %copy-start.5 = (f32[64,16,128]{2,0,1:T(8,128)S(1)}, f32[64,16,128]{2,0,1:T(8,128)}, u32[]{:S(2)}) copy-start(f32[64,16,128]{2,0,1:T(8,128)} %get-tuple-element.41) | copy-start | bytes 1572868
  247.5 11.8 %all-to-all-start.12 = ((bf16[4,768,128]{2,1,0:T(8,128)(2,1)}), bf16[4,768,128]{2,1,0:T(8,128)(2,1)S(1)}, u32[]{:S(2)}, u32[]{:S(2)}) async-start(bf16[4,768,128]{2,1,0:T(8,128)(2,1)} %broadcast_in_dim.157), calls=%async_computation.12 | async-start | bytes 1572864 | tf_op jit(solution)/shard_map/all_to_all | solution.py:79
  (30 other events, 45.4 us)

commit v2 on v1

v2 whole, which is shorter than its diff:
```python
import functools

import jax
import jax.numpy as jnp
from jax import lax
from jax.experimental import pallas as pl
from jax.experimental.pallas import tpu as pltpu
from jax.sharding import Mesh
from jax.sharding import PartitionSpec as P

GROUPS = 32
GY = ("gy_0", "gy_1")
GX = ("gx_0", "gx_1", "gx_2")
GY_GX = GY + GX
NEAR = ("gx_1", "gx_2")
FAR = ("gx_0", "gy_0", "gy_1")
STAGES = (("gx_2",), ("gx_0", "gy_0"), ("gx_1", "gy_1"))
LANES = 128
EPSILON = 1e-05

PITCH = 32
FINE_RIM = 3
COARSE_RIM = 2


def exchanged(parts, axis):
    count = lax.axis_size(axis)
    up = [(i, i + 1) for i in range(count - 1)]
    down = [(i + 1, i) for i in range(count - 1)]
    heads = jnp.concatenate([head.reshape(-1, LANES) for head, _ in parts])
    tails = jnp.concatenate([tail.reshape(-1, LANES) for _, tail in parts])
    before = lax.ppermute(tails, axis, up)
    after = lax.ppermute(heads, axis, down)
    result, at = [], 0
    for head, _ in parts:
        rows = head.size // LANES
        result.append(
            (before[at : at + rows].reshape(head.shape), after[at : at + rows].reshape(head.shape))
        )
        at += rows
    return result


def ring(own, left, right, pitch):
    rows, cols, channels = own.shape
    gap = pitch - cols - left.shape[1] - right.shape[1]
    return jnp.concatenate([own, right, jnp.zeros((rows, gap, channels), own.dtype), left], axis=1)


def with_rims(fine, coarse, wide, narrow):
    (f0, f1), (c0, c1) = exchanged(
        ((fine[:wide], fine[-wide:]), (coarse[:narrow], coarse[-narrow:])), GY
    )
    fine = jnp.concatenate([f0, fine, f1])
    coarse = jnp.concatenate([c0, coarse, c1])
    (f0, f1), (c0, c1) = exchanged(
        ((fine[:, :wide], fine[:, -wide:]), (coarse[:, :narrow], coarse[:, -narrow:])), GX
    )
    return ring(fine, f0, f1, PITCH), ring(coarse, c0, c1, PITCH // 2)


def call(body, outs, *args, scratch=()):
    spaces = [
        pl.BlockSpec(memory_space=pltpu.SMEM if a.dtype == jnp.int32 else pltpu.VMEM) for a in args
    ]
    return pl.pallas_call(
        body,
        out_shape=[jax.ShapeDtypeStruct(shape, dtype) for shape, dtype in outs],
        in_specs=spaces,
        out_specs=[pl.BlockSpec(memory_space=pltpu.VMEM) for _ in outs],
        scratch_shapes=[pltpu.VMEM(shape, dtype) for shape, dtype in scratch],
    )(*args)


def group_sum(values, size):
    lanes = values.shape[1]
    lane = lax.broadcasted_iota(jnp.int32, values.shape, 1)
    step = 1
    while step < size:
        after = pltpu.roll(values, lanes - step, 1)
        before = pltpu.roll(values, step, 1)
        values = values + jnp.where((lane & step) == 0, after, before)
        step *= 2
    return values


def wide(row):
    return jnp.broadcast_to(row, (8, row.shape[1]))


def moments(first, second, count, size):
    average = group_sum(wide(first), size) / count
    square = group_sum(wide(second), size) / count
    return average, lax.rsqrt(square - average * average + EPSILON)


def sigmoid(act):
    return 1.0 / (1.0 + jnp.exp(-act))


def in_grid(shape, first_row, first_col, rim, rows, cols):
    row = lax.broadcasted_iota(jnp.int32, shape, 0) + first_row
    place = lax.broadcasted_iota(jnp.int32, shape, 1)
    col = jnp.where(place < shape[1] - rim, place, place - shape[1]) + first_col
    return (row >= 0) & (row < rows) & (col >= 0) & (col < cols)


def over_cells(values):
    lanes = values.shape[-1]
    return jnp.sum(jnp.sum(values.reshape(-1, 8, lanes), axis=0), axis=0, keepdims=True)


def spread(copies, rows):
    for k, row in enumerate(rows):
        copies[:, k, :] = jnp.broadcast_to(row, (copies.shape[0], LANES))


def field_sums(field, copies):
    first = jnp.zeros((8, LANES), jnp.float32)
    second = jnp.zeros((8, LANES), jnp.float32)
    for at in range(0, field.shape[0], 8):
        v = field[at : at + 8].astype(jnp.float32).reshape(-1, 8, LANES)
        first = first + jnp.sum(v, axis=0)
        second = second + jnp.sum(v * v, axis=0)
    spread(
        copies, [jnp.sum(first, axis=0, keepdims=True), jnp.sum(second, axis=0, keepdims=True)]
    )


def relay(received, copies):
    sums = jnp.sum(received[...], axis=0)
    for k in range(copies.shape[1]):
        copies[:, k, :] = jnp.broadcast_to(sums[k : k + 1], (copies.shape[0], LANES))


def fine_forward(count, rows, cols, place, x, sums, gain, weight, projection,
                 hidden, pooled, coarse, copies, stats, block):
    tot = jnp.sum(sums[...], axis=0)
    average, inverse = moments(tot[0:1], tot[1:2], count, LANES // GROUPS)
    stats[0] = average
    stats[1] = inverse
    average, scale = average[0:1], inverse[0:1] * gain[...]
    lines = x.shape[0]
    step = 10
    for at in range(0, lines, step):
        v = x[at : at + step].astype(jnp.float32)
        act = (v - average) * scale
        h = act * sigmoid(act)
        keep = in_grid(
            h.shape, at - FINE_RIM + place[0], place[1], FINE_RIM, rows, cols
        )
        h = jnp.where(keep, h, 0.0)
        hidden[at : at + step, :, 0:LANES] = pltpu.roll(h, 1, 1).astype(jnp.bfloat16)
        hidden[at : at + step, :, LANES : 2 * LANES] = h.astype(jnp.bfloat16)
        hidden[at : at + step, :, 2 * LANES :] = pltpu.roll(h, PITCH - 1, 1).astype(jnp.bfloat16)
    step = (lines - 2) // 4
    for at in range(0, lines - 2, step):
        acc = x[at + 1 : at + 1 + step].astype(jnp.float32).reshape(step * PITCH, LANES)
        conv = jnp.zeros_like(acc)
        for tap in range(3):
            conv = conv + jnp.dot(
                hidden[at + tap : at + tap + step].reshape(step * PITCH, 3 * LANES),
                weight[tap],
                preferred_element_type=jnp.float32,
            )
        block[at * PITCH : (at + step) * PITCH] = (
            (acc + conv).astype(jnp.bfloat16).astype(jnp.float32)
        )
    half = PITCH // 2
    step = (lines - 2) // 4
    first = jnp.zeros((1, coarse.shape[1]), jnp.float32)
    second = jnp.zeros((1, coarse.shape[1]), jnp.float32)
    for at in range(0, (lines - 2) // 2, step):
        size = 2 * step * half
        pair = block[pl.ds(2 * at * PITCH, size, stride=2), :] + block[
            pl.ds(2 * at * PITCH + 1, size, stride=2), :
        ]
        mean = 0.25 * jnp.sum(pair.reshape(step, 2, half, LANES), axis=1)
        mean = mean.reshape(step * half, LANES).astype(jnp.bfloat16)
        pooled[at * half : (at + step) * half] = mean
        cells = jnp.dot(mean, projection[...], preferred_element_type=jnp.float32).astype(
            jnp.bfloat16
        )
        coarse[at * half : (at + step) * half] = cells
        own = cells.astype(jnp.float32).reshape(step, half, -1)[:, : half // 2]
        low = 1 if at == 0 else 0
        high = step - 1 if at + step == (lines - 2) // 2 else step
        own = own[low:high]
        first = first + over_cells(own)
        second = second + over_cells(own * own)
    spread(copies, [first[:, :LANES], first[:, LANES:], second[:, :LANES], second[:, LANES:]])


def coarse_transpose(grad, weight, out, shifted):
    half = PITCH // 2
    lines = grad.shape[0]
    step = lines // 4
    for at in range(0, lines, step):
        g = grad[at : at + step].astype(jnp.float32)
        shifted[0, at : at + step] = pltpu.roll(g, half - 1, 1).astype(jnp.bfloat16)
        shifted[1, at : at + step] = grad[at : at + step]
        shifted[2, at : at + step] = pltpu.roll(g, 1, 1).astype(jnp.bfloat16)
    step = (lines - 2) // 2
    for at in range(0, lines - 2, step):
        acc = jnp.zeros((step * half, weight.shape[2]), jnp.float32)
        for row_tap in range(3):
            for col_tap in range(3):
                begin = at + 2 - row_tap
                acc = acc + lax.dot_general(
                    shifted[col_tap, begin : begin + step].reshape(step * half, -1),
                    weight[row_tap, col_tap],
                    (((1,), (1,)), ((), ())),
                    preferred_element_type=jnp.float32,
                )
        out[at * half : (at + step) * half] = acc


def coarse_middle(count, rows, cols, place, sums, coarse, pre, gain,
                  hidden, dnorm, copies, stats):
    tot = jnp.sum(sums[...], axis=0)
    average, inverse = moments(
        jnp.concatenate([tot[0:1], tot[1:2]], axis=1),
        jnp.concatenate([tot[2:3], tot[3:4]], axis=1),
        count,
        2 * LANES // GROUPS,
    )
    stats[0] = average
    stats[1] = inverse
    average, inverse = average[0:1], inverse[0:1]
    half = PITCH // 2
    lines = coarse.shape[0] // half
    channels = coarse.shape[1]
    step = lines // 2
    first = jnp.zeros((1, channels), jnp.float32)
    second = jnp.zeros((1, channels), jnp.float32)
    for at in range(0, lines, step):
        span = slice(at * half, (at + step) * half)
        normed = (coarse[span].astype(jnp.float32) - average) * inverse
        act = normed * gain[...]
        sigma = sigmoid(act)
        h = (act * sigma).reshape(step, half, channels)
        h = jnp.where(
            in_grid(h.shape, at - 1 + place[2], place[3], COARSE_RIM, rows, cols), h, 0.0
        )
        hidden[at : at + step, :, 0:channels] = pltpu.roll(h, 1, 1).astype(jnp.bfloat16)
        hidden[at : at + step, :, channels : 2 * channels] = h.astype(jnp.bfloat16)
        hidden[at : at + step, :, 2 * channels :] = pltpu.roll(h, half - 1, 1).astype(jnp.bfloat16)
        dact = pre[span] * (sigma * (1.0 + act * (1.0 - sigma)))
        dn = dact * gain[...]
        dnorm[span] = dn
        low = 1 if at == 0 else 0
        high = step - 1 if at + step == lines else step
        own = slice(low, high), slice(0, half // 2)
        first = first + over_cells(dn.reshape(step, half, channels)[own])
        second = second + over_cells((dact * normed).reshape(step, half, channels)[own])
    spread(copies, [first[:, :LANES], first[:, LANES:], second[:, :LANES], second[:, LANES:]])


def coarse_rest(hidden, coarse, grad, weight, out, rows_out):
    half = PITCH // 2
    height = out.shape[0]
    channels = out.shape[2]
    step = height // 2
    for at in range(0, height, step):
        acc = coarse[(at + 1) * half : (at + 1 + step) * half].astype(jnp.float32)
        conv = jnp.zeros_like(acc)
        for tap in range(3):
            conv = conv + jnp.dot(
                hidden[at + tap : at + tap + step].reshape(step * half, 3 * channels),
                weight[tap],
                preferred_element_type=jnp.float32,
            )
        out[at : at + step] = (acc + conv).reshape(step, half, channels)[:, : half // 2].astype(
            jnp.bfloat16
        )
    g = grad[2 : 2 + height].astype(jnp.float32)
    own = lax.broadcasted_iota(jnp.int32, g.shape, 1) < half // 2
    g = jnp.where(own, g, 0.0).astype(jnp.bfloat16).reshape(height * half, channels)
    tall = 9 * channels
    for tap in range(3):
        k = lax.dot_general(
            hidden[tap : tap + height].reshape(height * half, 3 * channels),
            g,
            (((0,), (0,)), ((), ())),
            preferred_element_type=jnp.float32,
        ).astype(jnp.bfloat16)
        at = tap * 3 * channels
        rows_out[at : at + 3 * channels] = k[:, :LANES]
        rows_out[tall + at : tall + at + 3 * channels] = k[:, LANES:]


def fine_backward(coarse_count, rows, cols, place, sums, coarse, pooled, grad, dnorm, stats_c,
                  gain_c, projection, weight_t, x, hidden, stats_f, gain_f, rows_in,
                  rows_out, gain_c_grad, partial, up, shifted, taps):
    rows_out[0 : rows_in.shape[0]] = rows_in[...]
    tot = jnp.sum(sums[...], axis=0)
    first = jnp.concatenate([tot[0:1], tot[1:2]], axis=1)
    second = jnp.concatenate([tot[2:3], tot[3:4]], axis=1)
    gain_c_grad[...] = second
    size = 2 * LANES // GROUPS
    a_sum = group_sum(wide(first), size)[0:1] / coarse_count
    b_sum = group_sum(wide(second * gain_c[...]), size)[0:1] / coarse_count
    average, inverse = stats_c[0, 0:1], stats_c[1, 0:1]
    half = PITCH // 2
    lines = coarse.shape[0] // half
    channels = coarse.shape[1]
    height = 2 * (lines - 2)
    step = lines // 2
    proj_grad = jnp.zeros((LANES, channels), jnp.float32)
    for at in range(0, lines, step):
        span = slice(at * half, (at + step) * half)
        normed = (coarse[span].astype(jnp.float32) - average) * inverse
        g = grad[at + 1 : at + 1 + step].astype(jnp.float32).reshape(step * half, channels)
        d = g + inverse * (dnorm[span] - a_sum - normed * b_sum)
        d = d.reshape(step, half, channels)
        d = jnp.where(
            in_grid(d.shape, at - 1 + place[2], place[3], COARSE_RIM, rows, cols), d, 0.0
        )
        line = lax.broadcasted_iota(jnp.int32, d.shape, 0) + at
        spot = lax.broadcasted_iota(jnp.int32, d.shape, 1)
        own = (line >= 1) & (line < lines - 1) & (spot < half // 2)
        own = jnp.where(own, d, 0.0).astype(jnp.bfloat16).reshape(step * half, channels)
        d = d.astype(jnp.bfloat16).reshape(step * half, channels)
        proj_grad = proj_grad + lax.dot_general(
            pooled[span], own, (((0,), (0,)), ((), ())), preferred_element_type=jnp.float32
        )
        small = lax.dot_general(
            d, projection[...], (((1,), (1,)), ((), ())), preferred_element_type=jnp.float32
        )
        small = (small * 0.25).astype(jnp.bfloat16).astype(jnp.float32)
        up[pl.ds(at * PITCH, step * half, stride=2), :] = small
        up[pl.ds(at * PITCH + 1, step * half, stride=2), :] = small
    for at in range(0, lines, step):
        u = up[at * PITCH : (at + step) * PITCH].reshape(step, PITCH, LANES)
        shifted[at : at + step, :, 0:LANES] = pltpu.roll(u, PITCH - 1, 1).astype(jnp.bfloat16)
        shifted[at : at + step, :, LANES : 2 * LANES] = u.astype(jnp.bfloat16)
        shifted[at : at + step, :, 2 * LANES :] = pltpu.roll(u, 1, 1).astype(jnp.bfloat16)
    width = PITCH // 2
    for tap in range(3):
        for at in range(0, lines, step):
            y = jnp.dot(
                shifted[at : at + step, 0:width, :].reshape(step * width, 3 * LANES),
                weight_t[tap],
                preferred_element_type=jnp.float32,
            )
            taps[tap, at : at + step] = y.reshape(step, width, LANES)
    average, inverse = stats_f[0, 0:1], stats_f[1, 0:1]
    first = jnp.zeros((1, LANES), jnp.float32)
    second = jnp.zeros((1, LANES), jnp.float32)
    step = 8
    for at in range(0, lines - 2, step):
        even = taps[0, at + 1 : at + 1 + step] + taps[1, at + 1 : at + 1 + step] + taps[
            2, at : at + step
        ]
        odd = taps[0, at + 2 : at + 2 + step] + taps[1, at + 1 : at + 1 + step] + taps[
            2, at + 1 : at + 1 + step
        ]
        both = jnp.stack([even, odd], axis=1).reshape(2 * step, width, LANES)
        begin = FINE_RIM + 2 * at
        v = x[begin : begin + 2 * step, 0:width, :].astype(jnp.float32)
        normed = (v - average) * inverse
        act = normed * gain_f[...]
        sigma = sigmoid(act)
        dact = both * (sigma * (1.0 + act * (1.0 - sigma)))
        dn = dact * gain_f[...]
        first = first + over_cells(dn)
        second = second + over_cells(dact * normed)
        u = up[(at + 1) * PITCH : (at + 1 + step) * PITCH].reshape(step, PITCH, LANES)[:, 0:width]
        u = jnp.broadcast_to(u[:, None], (step, 2, width, LANES)).reshape(2 * step, width, LANES)
        partial[2 * at : 2 * at + 2 * step] = u + inverse * dn
    d = up[PITCH : (lines - 1) * PITCH].reshape(lines - 2, PITCH, LANES)[:, 0:width]
    d = jnp.broadcast_to(
        d.astype(jnp.bfloat16)[:, None], (lines - 2, 2, width, LANES)
    ).reshape(height * width, LANES)
    at = 18 * channels
    for tap in range(3):
        begin = FINE_RIM - 1 + tap
        k = lax.dot_general(
            hidden[begin : begin + height, 0:width, :].reshape(height * width, 3 * LANES),
            d,
            (((0,), (0,)), ((), ())),
            preferred_element_type=jnp.float32,
        )
        rows_out[at : at + 3 * LANES] = k.astype(jnp.bfloat16)
        at += 3 * LANES
    proj_grad = proj_grad.astype(jnp.bfloat16)
    rows_out[at : at + LANES] = proj_grad[:, :LANES]
    rows_out[at + LANES : at + 2 * LANES] = proj_grad[:, LANES:]
    at += 2 * LANES
    spare = rows_out.shape[0] - at
    small = jnp.concatenate([first, second], axis=0)
    high = small.astype(jnp.bfloat16).astype(jnp.float32)
    middle = (small - high).astype(jnp.bfloat16).astype(jnp.float32)
    low = small - high - middle
    tail = jnp.concatenate([high, middle, low, jnp.zeros_like(low)], axis=0)
    rows_out[at:] = jnp.concatenate(
        [jnp.zeros((spare - 8, LANES), jnp.float32), tail], axis=0
    ).astype(jnp.bfloat16)


def finish(fine_count, rows, partial, x, stats, gain,
           field_grad, weight_f, gain_f, proj, weight_c):
    count = rows.shape[0]
    small = rows[count - 8 :].astype(jnp.float32)
    small = small[0:2] + small[2:4] + small[4:6]
    first, second = small[0:1], small[1:2]
    gain_f[...] = second
    size = LANES // GROUPS
    a_sum = group_sum(wide(first), size)[0:1] / fine_count
    b_sum = group_sum(wide(second * gain[...]), size)[0:1] / fine_count
    average, inverse = stats[0, 0:1], stats[1, 0:1]
    height, width, _ = partial.shape
    step = 16
    for at in range(0, height, step):
        v = x[FINE_RIM + at : FINE_RIM + at + step, 0:width, :].astype(jnp.float32)
        normed = (v - average) * inverse
        field_grad[at : at + step] = (
            partial[at : at + step] - inverse * (a_sum + normed * b_sum)
        ).astype(jnp.bfloat16)
    tall = weight_c.shape[0]
    weight_c[:, :LANES] = rows[0:tall].astype(jnp.float32)
    weight_c[:, LANES:] = rows[tall : 2 * tall].astype(jnp.float32)
    at = 2 * tall
    weight_f[...] = rows[at : at + weight_f.shape[0]].astype(jnp.float32)
    at += weight_f.shape[0]
    proj[:, :LANES] = rows[at : at + LANES].astype(jnp.float32)
    proj[:, LANES:] = rows[at + LANES : at + 2 * LANES].astype(jnp.float32)


def gathered(copies):
    far = lax.axis_size(FAR)
    received = lax.all_to_all(copies, NEAR, 0, 0, tiled=True)
    (copies,) = call(relay, [((far,) + copies.shape[1:], jnp.float32)], received)
    return lax.all_to_all(copies, FAR, 0, 0, tiled=True)


def planes(values):
    high = lax.reduce_precision(values, 8, 7)
    middle = lax.reduce_precision(values - high, 8, 7)
    low = values - high - middle
    return jnp.concatenate([high, middle, low, jnp.zeros((2, LANES), jnp.float32)]).astype(
        jnp.bfloat16
    )


def from_planes(rows):
    rows = rows.astype(jnp.float32)
    return rows[0:2] + rows[2:4] + rows[4:6]


def gradient_totals(part):
    holder = True
    for axes in STAGES:
        count = lax.axis_size(axes)
        pieces = lax.all_to_all(part.reshape(count, -1, LANES), axes, 0, 0, tiled=True)
        sums = jnp.sum(pieces.astype(jnp.float32), axis=0)
        holder = holder & (lax.axis_index(axes) == count - 1)
        tail = jnp.where(holder, planes(from_planes(sums[-8:])), sums[-8:].astype(jnp.bfloat16))
        part = lax.dynamic_update_slice(
            sums.astype(jnp.bfloat16), tail, (sums.shape[0] - 8, 0)
        )
    for axes in STAGES[::-1]:
        count = lax.axis_size(axes)
        copies = jnp.broadcast_to(part[None], (count,) + part.shape)
        part = lax.all_to_all(copies, axes, 0, 0, tiled=True).reshape(-1, LANES)
    return part


def on_device(field, cotangent, gain_fine, weight_fine, projection, gain_coarse, weight_coarse):
    height, width, chan_fine = field.shape
    chan_coarse = projection.shape[1]
    half_h, half_w = (height // 2, width // 2)
    cells_all = height * width * lax.axis_size(GY_GX)
    fine_count = cells_all * (chan_fine // GROUPS)
    coarse_count = cells_all // 4 * (chan_coarse // GROUPS)
    rows, cols = height * lax.axis_size(GY), width * lax.axis_size(GX)
    f32, bf16 = jnp.float32, jnp.bfloat16
    near = lax.axis_size(NEAR)
    row, col = lax.axis_index(GY), lax.axis_index(GX)
    place = jnp.stack([row * height, col * width, row * half_h, col * half_w]).astype(jnp.int32)
    gain_f, gain_c = gain_fine.reshape(1, -1), gain_coarse.reshape(1, -1)
    weight_t = weight_fine.transpose(0, 1, 3, 2).reshape(3, 3 * chan_fine, chan_fine)

    (copies,) = call(field_sums, [((near, 2, LANES), f32)], field)
    sums = gathered(copies)
    x, grad = with_rims(field, cotangent, FINE_RIM, COARSE_RIM)
    lines = half_h + 2
    cells = lines * PITCH // 2
    (pre,) = call(
        coarse_transpose,
        [((cells, chan_coarse), f32)],
        grad,
        weight_coarse,
        scratch=[((3,) + grad.shape, bf16)],
    )
    hidden_f, pooled, coarse, copies, stats_f = call(
        functools.partial(fine_forward, fine_count, rows, cols),
        [
            (x.shape[:2] + (3 * chan_fine,), bf16),
            ((cells, chan_fine), bf16),
            ((cells, chan_coarse), bf16),
            ((near, 4, LANES), f32),
            ((2, 8, chan_fine), f32),
        ],
        place,
        x,
        sums,
        gain_f,
        weight_fine.reshape(3, 3 * chan_fine, chan_fine),
        projection,
        scratch=[((2 * lines * PITCH + 8, chan_fine), f32)],
    )
    sums = gathered(copies)
    hidden_c, dnorm, copies, stats_c = call(
        functools.partial(coarse_middle, coarse_count, rows // 2, cols // 2),
        [
            ((lines, PITCH // 2, 3 * chan_coarse), bf16),
            ((cells, chan_coarse), f32),
            ((near, 4, LANES), f32),
            ((2, 8, chan_coarse), f32),
        ],
        place,
        sums,
        coarse,
        pre,
        gain_c,
    )
    sums = gathered(copies)
    used = 18 * chan_coarse + 9 * chan_fine + chan_coarse
    used += -(used + 8) % (4 * lax.axis_size(GY_GX)) + 8
    coarse_output, parts = call(
        coarse_rest,
        [((half_h, half_w, chan_coarse), bf16), ((18 * chan_coarse, LANES), bf16)],
        hidden_c,
        coarse,
        grad,
        weight_coarse.reshape(3, 3 * chan_coarse, chan_coarse),
    )
    parts, coarse_gain_grad, partial = call(
        functools.partial(fine_backward, coarse_count, rows // 2, cols // 2),
        [
            ((used, LANES), bf16),
            ((1, chan_coarse), f32),
            ((height, width, chan_fine), f32),
        ],
        place,
        sums,
        coarse,
        pooled,
        grad,
        dnorm,
        stats_c,
        gain_c,
        projection,
        weight_t,
        x,
        hidden_f,
        stats_f,
        gain_f,
        parts,
        scratch=[
            ((lines * PITCH + 8, chan_fine), f32),
            ((lines, PITCH, 3 * chan_fine), bf16),
            ((3, lines, PITCH // 2, chan_fine), f32),
        ],
    )
    totals = gradient_totals(parts)
    field_grad, fine_weight_grad, fine_gain_grad, projection_grad, coarse_weight_grad = call(
        functools.partial(finish, fine_count),
        [
            ((height, width, chan_fine), bf16),
            ((9 * chan_fine, chan_fine), f32),
            ((1, chan_fine), f32),
            ((chan_fine, chan_coarse), f32),
            ((9 * chan_coarse, chan_coarse), f32),
        ],
        totals,
        partial,
        x,
        stats_f,
        gain_f,
    )
    return (
        coarse_output,
        field_grad,
        fine_weight_grad.reshape(weight_fine.shape),
        fine_gain_grad.reshape(-1),
        projection_grad,
        coarse_weight_grad.reshape(weight_coarse.shape),
        coarse_gain_grad.reshape(-1),
    )


def solution(mesh):
    finer = Mesh(mesh.devices.reshape(2, 8, 2, 8, 2), GY_GX)
    in_specs = (P(GY, GX, None), P(GY, GX, None), P(), P(), P(), P(), P())
    out_specs = (P(GY, GX, None), P(GY, GX, None), P(), P(), P(), P(), P())
    return jax.shard_map(
        on_device, mesh=finer, in_specs=in_specs, out_specs=out_specs, check_vma=False
    )
```

time: 274 us -> 213 us (0.78)
  blocking collectives: 15.9 us -> 59.6 us
  local copies, waits for them, and re-layouts: 47.6 us -> 8.16 us
  waiting for transfers between devices: 83.2 us -> 47.8 us
  Pallas kernels: 0 us -> 29.2 us
  starting transfers between devices: 86.6 us -> 59.8 us
  matrix products: 22.8 us -> 0 us
  other arithmetic: 14.3 us -> 5.66 us
    all_to_all x10 -> x5, waiting for transfers between devices: 63.4 us -> 23.5 us  [the longest x3 16.3 us: gathered(): return lax.all_to_all(copies, FAR, 0, 0, tiled=True)]
    all_to_all x1 -> x3, blocking collectives: 9.5 us -> 39.3 us  [gradient_totals(): part = lax.all_to_all(copies, axes, 0, 0, tiled=True).reshape(-1, LANES)]
    pallas_call x0 -> x10, Pallas kernels: none -> 29.2 us  [call(): pl.pallas_call(body, out_shape=[jax.ShapeDtypeStruct(shape, dtype) for sh...]
    all_to_all x10 -> x5, starting transfers between devices: 66.5 us -> 40.1 us  [the longest x3 22 us: gathered(): return lax.all_to_all(copies, FAR, 0, 0, tiled=True)]
    dot_general x57 -> x0, matrix products: 22.8 us -> none  [the longest x18 12.6 us: conv_forward(): jnp.dot(window, weight[row_tap, col_tap], preferred_element_type=jnp.floa...]
    reshape x30 -> x0, local copies, waits for them, and re-layouts: 14 us -> none  [the longest x9 5.92 us: conv_transpose(): window = padded[2 - row_tap:2 - row_tap + height, 2 - col_tap:2 - col_tap...]
    all_to_all x0 -> x1, blocking collectives: none -> 13 us  [gathered(): received = lax.all_to_all(copies, NEAR, 0, 0, tiled=True)]
    slice x40 -> x2, local copies, waits for them, and re-layouts: 13.1 us -> 1.49 us  [the longest x1 0.76 us: with_rims(): coarse[:narrow]]
  transfers between devices with their start and end apart: 16 -> 11, of which waited for: 13 -> 6; matrix products, arithmetic and copies ran while one was open for 9% -> 2% of each run, Pallas kernels for 0% -> 5%
where the time goes in v2:
time: 213 us; the launch traced here: 211 us
  starting transfers between devices  59.8 us (28%)
  blocking collectives  59.6 us (28%)
  waiting for transfers between devices  47.8 us (22%)
  Pallas kernels  29.2 us (14%)
  local copies, waits for them, and re-layouts  8.16 us (4%)
  other arithmetic  5.66 us (3%)
    all_to_all x3, blocking collectives, gradient_totals(): part = lax.all_to_all(copies, axes, 0, 0, tiled=True).reshape(-1, LANES)  39.3 us
    pallas_call x10, Pallas kernels, call(): pl.pallas_call(body, out_shape=[jax.ShapeDtypeStruct(shape, dtype) for sh...  29.2 us
    all_to_all x2, waiting for transfers between devices, gradient_totals(): lax.all_to_all(part.reshape(count, -1, LANES), axes, 0, 0, tiled=True)  24.4 us
    all_to_all x3, starting transfers between devices, gathered(): return lax.all_to_all(copies, FAR, 0, 0, tiled=True)  22 us
    all_to_all x2, starting transfers between devices, gathered(): received = lax.all_to_all(copies, NEAR, 0, 0, tiled=True)  18 us
    all_to_all x3, waiting for transfers between devices, gathered(): return lax.all_to_all(copies, FAR, 0, 0, tiled=True)  16.3 us
    all_to_all x1, blocking collectives, gathered(): received = lax.all_to_all(copies, NEAR, 0, 0, tiled=True)  13 us
    ppermute x2, starting transfers between devices, exchanged(): before = lax.ppermute(tails, axis, up)  8.34 us
  transfers between devices with their start and end apart: 11, of which 6 were waited for; matrix products, arithmetic and copies ran while one was open for 2% of the time, Pallas kernels for 5%

profile of v2, /device:TPU:1, one launch (start us, length us, event | category | flops | bytes accessed | tf_op | source)
XLA Modules:
  0.0 211.3 jit_solution(17349945395745275114)
XLA Ops:
  2.2 4.8 %collective-permute-start = (bf16[80,128]{1,0:T(8,128)(2,1)S(1)}, bf16[80,128]{1,0:T(8,128)(2,1)S(1)}, u32[]{:S(2)}, u32[]{:S(2)}) collective-permute-start(bf16[80,128]{1,0:T(8,128)(2,1)S(1)} %pad_maximum_fusion.7), channel_id=1, source_target_pairs={{0,32},{32,64},{64,96},{96,128},{128,160},{160,192},{192,224},{224... | collective-permute-start | bytes 61448 | tf_op jit(solution)/shard_map/ppermute | solution.py:32
  8.3 1.6 shard_map.126
  9.9 8.1 %all-to-all-start = ((f32[16,2,128]{2,1,0:T(2,128)}), f32[16,2,128]{2,1,0:T(2,128)S(1)}, u32[]{:S(2)}, u32[]{:S(2)}) async-start(f32[16,2,128]{2,1,0:T(2,128)} %shard_map.126), calls=%async_computation | async-start | bytes 32768 | tf_op jit(solution)/shard_map/all_to_all | solution.py:432
  19.4 3.5 %collective-permute-start.3 = (bf16[354,128]{1,0:T(8,128)(2,1)S(1)}, bf16[354,128]{1,0:T(8,128)(2,1)S(1)}, u32[]{:S(2)}, u32[]{:S(2)}) collective-permute-start(bf16[354,128]{1,0:T(8,128)(2,1)S(1)} %pad_maximum_fusion.3), channel_id=1, source_target_pairs={{0,1},{1,2},{2,3},{3,4},{4,5},{5,6},{6,7},{7,8},{8,9},{9,10},{10,1... | collective-permute-start | bytes 271880 | tf_op jit(solution)/shard_map/ppermute | solution.py:32
  22.9 1.9 collective-permute-start.2
  26.2 1.4 shard_map.127
  27.5 14.3 %all-to-all-start.1 = ((f32[32,2,128]{2,1,0:T(2,128)}), f32[32,2,128]{2,1,0:T(2,128)S(1)}, u32[]{:S(2)}, u32[]{:S(2)}) async-start(f32[32,2,128]{2,1,0:T(2,128)} %shard_map.127), calls=%async_computation.1 | async-start | bytes 65536 | tf_op jit(solution)/shard_map/all_to_all | solution.py:434
  43.0 7.6 %all-to-all-done.1.sums = f32[32,2,128]{2,1,0:T(2,128)S(1)} async-done(((f32[32,2,128]{2,1,0:T(2,128)}), f32[32,2,128]{2,1,0:T(2,128)S(1)}, u32[]{:S(2)}, u32[]{:S(2)}) %all-to-all-start.1) | async-done | bytes 32800 | tf_op jit(solution)/shard_map/all_to_all | solution.py:434
  51.3 3.9 %shard_map.128 = (bf16[70,32,384]{2,1,0:T(8,128)(2,1)}, bf16[544,128]{1,0:T(8,128)(2,1)}, bf16[544,256]{1,0:T(8,128)(2,1)}, f32[16,4,128]{2,1,0:T(4,128)}, f32[2,8,128]{2,1,0:T(8,128)}) custom-call(s32[4]{0:T(128)} %pad_add_fusion.place, bf16[70,32,128]{2,1,0:T(8,128)(2,1)} %pad_maximum_fusion.x, f32[32,2,128]{2,1,0:T(2,128)} %copy-done.4, ...), custom_call_target="tpu_custom_call" | custom-call | tf_op jit(solution)/shard_map/pallas_call | solution.py:66
  55.1 10.0 %all-to-all-start.2 = ((f32[16,4,128]{2,1,0:T(4,128)}), f32[16,4,128]{2,1,0:T(4,128)S(1)}, u32[]{:S(2)}, u32[]{:S(2)}) async-start(f32[16,4,128]{2,1,0:T(4,128)} %get-tuple-element.26), calls=%async_computation.2 | async-start | bytes 65536 | tf_op jit(solution)/shard_map/all_to_all | solution.py:432
  65.3 7.2 %all-to-all-done.2.received = f32[16,4,128]{2,1,0:T(4,128)S(1)} async-done(((f32[16,4,128]{2,1,0:T(4,128)}), f32[16,4,128]{2,1,0:T(4,128)S(1)}, u32[]{:S(2)}, u32[]{:S(2)}) %all-to-all-start.2) | async-done | bytes 32800 | tf_op jit(solution)/shard_map/all_to_all | solution.py:432
  73.1 1.4 shard_map.129
  74.5 3.9 %all-to-all-start.3 = ((f32[32,4,128]{2,1,0:T(4,128)}), f32[32,4,128]{2,1,0:T(4,128)S(1)}, u32[]{:S(2)}, u32[]{:S(2)}) async-start(f32[32,4,128]{2,1,0:T(4,128)} %shard_map.129), calls=%async_computation.3 | async-start | bytes 131072 | tf_op jit(solution)/shard_map/all_to_all | solution.py:434
  79.3 3.1 %shard_map.130.pre = f32[544,256]{1,0:T(8,128)} custom-call(bf16[36,16,256]{2,1,0:T(8,128)(2,1)} %pad_maximum_fusion.1.grad, bf16[3,3,256,256]{3,2,1,0:T(8,128)(2,1)} %weight.1), custom_call_target="tpu_custom_call" | custom-call | tf_op jit(solution)/shard_map/pallas_call | solution.py:66
  82.4 4.9 %all-to-all-done.3.sums = f32[32,4,128]{2,1,0:T(4,128)S(1)} async-done(((f32[32,4,128]{2,1,0:T(4,128)}), f32[32,4,128]{2,1,0:T(4,128)S(1)}, u32[]{:S(2)}, u32[]{:S(2)}) %all-to-all-start.3) | async-done | bytes 65568 | tf_op jit(solution)/shard_map/all_to_all | solution.py:434
  87.9 3.1 %shard_map.131 = (bf16[34,16,768]{2,1,0:T(8,128)(2,1)}, f32[544,256]{1,0:T(8,128)}, f32[16,4,128]{2,1,0:T(4,128)}, f32[2,8,256]{2,1,0:T(8,128)}) custom-call(s32[4]{0:T(128)} %pad_add_fusion.place, f32[32,4,128]{2,1,0:T(4,128)} %copy-done.3, bf16[544,256]{1,0:T(8,128)(2,1)} %get-tuple-element.27.coarse, f32[544,256]{1,0:T(8,128)} %shard_map.130.pre, ...), custom_call_target="tpu_custom_call" | custom-call | tf_op jit(solution)/shard_map/pallas_call | solution.py:66
  91.0 13.0 %all_to_all.60.received = f32[16,4,128]{2,1,0:T(4,128)} all-to-all(f32[16,4,128]{2,1,0:T(4,128)} %get-tuple-element.30), channel_id=1, replica_groups=mesh['gy_0'=2,'gy_1'=8,'gx_0'=2,'gx_1'=8,'gx_2'=2] {'gx_1','gx_2'}, dimensions={0} | all-to-all | bytes 65536 | tf_op jit(solution)/shard_map/all_to_all | solution.py:432
  104.0 1.4 shard_map.133
  105.4 3.9 %all-to-all-start.5 = ((f32[32,4,128]{2,1,0:T(4,128)}), f32[32,4,128]{2,1,0:T(4,128)S(1)}, u32[]{:S(2)}, u32[]{:S(2)}) async-start(f32[32,4,128]{2,1,0:T(4,128)} %shard_map.133), calls=%async_computation.5 | async-start | bytes 131072 | tf_op jit(solution)/shard_map/all_to_all | solution.py:434
  110.2 4.1 %shard_map.132 = (bf16[32,8,256]{2,1,0:T(8,128)(2,1)}, bf16[4608,128]{1,0:T(8,128)(2,1)}) custom-call(bf16[34,16,768]{2,1,0:T(8,128)(2,1)} %get-tuple-element.28.hidden, bf16[544,256]{1,0:T(8,128)(2,1)} %get-tuple-element.27.coarse, bf16[36,16,256]{2,1,0:T(8,128)(2,1)} %pad_maximum_fusion.1.grad, bf16[3,768,256]{2,1,0:T(8,128)(2,1)} %bitcast.23), custom_call_target="tpu_custom_call" | custom-call | tf_op jit(solution)/shard_map/pallas_call | solution.py:66
  114.4 3.7 %all-to-all-done.5.sums = f32[32,4,128]{2,1,0:T(4,128)S(1)} async-done(((f32[32,4,128]{2,1,0:T(4,128)}), f32[32,4,128]{2,1,0:T(4,128)S(1)}, u32[]{:S(2)}, u32[]{:S(2)}) %all-to-all-start.5) | async-done | bytes 65568 | tf_op jit(solution)/shard_map/all_to_all | solution.py:434
  118.7 5.7 %shard_map.134 = (bf16[6144,128]{1,0:T(8,128)(2,1)}, f32[1,256]{1,0:T(1,128)}, f32[64,16,128]{2,1,0:T(8,128)}) custom-call(s32[4]{0:T(128)} %pad_add_fusion.place, f32[32,4,128]{2,1,0:T(4,128)} %copy-done.2, bf16[544,256]{1,0:T(8,128)(2,1)} %get-tuple-element.27.coarse, bf16[544,128]{1,0:T(8,128)(2,1)} %get-tuple-element.31.pooled, ...), custom_call_target="tpu_custom_call" | custom-call | tf_op jit(solution)/shard_map/pallas_call | solution.py:66
  124.4 7.3 %all_to_all.61 = bf16[2,3072,128]{2,1,0:T(8,128)(2,1)S(1)} all-to-all(bf16[2,3072,128]{2,1,0:T(8,128)(2,1)} %bitcast.25), channel_id=1, replica_groups=mesh['gy_0'=2,'gy_1'=8,'gx_0'=2,'gx_1'=8,'gx_2'=2] {'gx_2'}, dimensions={0} | all-to-all | bytes 3145728 | tf_op jit(solution)/shard_map/all_to_all | solution.py:455
  133.0 1.3 fusion.1
  134.3 3.5 %all-to-all-start.7 = ((bf16[4,768,128]{2,1,0:T(8,128)(2,1)}), bf16[4,768,128]{2,1,0:T(8,128)(2,1)S(1)}, u32[]{:S(2)}, u32[]{:S(2)}) async-start(bf16[4,768,128]{2,1,0:T(8,128)(2,1)} %bitcast.15), calls=%async_computation.7 | async-start | bytes 1572864 | tf_op jit(solution)/shard_map/all_to_all | solution.py:455
  137.9 12.0 %all-to-all-done.7 = bf16[4,768,128]{2,1,0:T(8,128)(2,1)S(1)} async-done(((bf16[4,768,128]{2,1,0:T(8,128)(2,1)}), bf16[4,768,128]{2,1,0:T(8,128)(2,1)S(1)}, u32[]{:S(2)}, u32[]{:S(2)}) %all-to-all-start.7) | async-done | bytes 786464 | tf_op jit(solution)/shard_map/all_to_all | solution.py:455
  150.8 4.6 %all-to-all-start.8 = ((bf16[64,12,128]{2,1,0:T(8,128)(2,1)}), bf16[64,12,128]{2,1,0:T(8,128)(2,1)S(1)}, u32[]{:S(2)}, u32[]{:S(2)}) async-start(bf16[64,12,128]{2,1,0:T(8,128)(2,1)} %reshape.134), calls=%async_computation.8 | async-start | bytes 524288 | tf_op jit(solution)/shard_map/all_to_all | solution.py:455
  155.5 12.4 %all-to-all-done.8 = bf16[64,12,128]{2,1,0:T(8,128)(2,1)S(1)} async-done(((bf16[64,12,128]{2,1,0:T(8,128)(2,1)}), bf16[64,12,128]{2,1,0:T(8,128)(2,1)S(1)}, u32[]{:S(2)}, u32[]{:S(2)}) %all-to-all-start.8) | async-done | bytes 196640 | tf_op jit(solution)/shard_map/all_to_all | solution.py:455
  168.2 18.2 %all_to_all.62 = bf16[64,12,128]{2,1,0:T(8,128)(2,1)S(1)} all-to-all(bf16[64,12,128]{2,1,0:T(8,128)(2,1)S(1)} %broadcast_in_dim.28), channel_id=1, replica_groups=mesh['gy_0'=2,'gy_1'=8,'gx_0'=2,'gx_1'=8,'gx_2'=2] {'gx_1','gy_1'}, dimensions={0} | all-to-all | bytes 393216 | tf_op jit(solution)/shard_map/all_to_all | solution.py:465
  186.6 11.0 %all_to_all.63 = bf16[4,768,128]{2,1,0:T(8,128)(2,1)S(1)} all-to-all(bf16[4,768,128]{2,1,0:T(8,128)(2,1)S(1)} %broadcast_in_dim.30), channel_id=1, replica_groups=mesh['gy_0'=2,'gy_1'=8,'gx_0'=2,'gx_1'=8,'gx_2'=2] {'gx_0','gy_0'}, dimensions={0} | all-to-all | bytes 1572864 | tf_op jit(solution)/shard_map/all_to_all | solution.py:465
  197.7 10.1 %all_to_all.64 = bf16[2,3072,128]{2,1,0:T(8,128)(2,1)} all-to-all(bf16[2,3072,128]{2,1,0:T(8,128)(2,1)S(1)} %broadcast_in_dim.32), channel_id=1, replica_groups=mesh['gy_0'=2,'gy_1'=8,'gx_0'=2,'gx_1'=8,'gx_2'=2] {'gx_2'}, dimensions={0} | all-to-all | bytes 3145728 | tf_op jit(solution)/shard_map/all_to_all | solution.py:465
  207.8 3.5 %shard_map.135 = (bf16[64,16,128]{2,1,0:T(8,128)(2,1)}, f32[1152,128]{1,0:T(8,128)}, f32[1,128]{1,0:T(1,128)}, f32[128,256]{1,0:T(8,128)}, f32[2304,256]{1,0:T(8,128)}) custom-call(bf16[6144,128]{1,0:T(8,128)(2,1)} %bitcast.22, f32[64,16,128]{2,1,0:T(8,128)} %get-tuple-element.38.partial, bf16[70,32,128]{2,1,0:T(8,128)(2,1)} %pad_maximum_fusion.x, ...), custom_call_target="tpu_custom_call" | custom-call | tf_op jit(solution)/shard_map/pallas_call | solution.py:66
  (81 shorter events, 13.8 us)
Async XLA Ops:
  0.6 18.5 %copy-start = (bf16[64,16,128]{2,1,0:T(8,128)(2,1)S(1)}, bf16[64,16,128]{2,1,0:T(8,128)(2,1)}, u32[]{:S(2)}) copy-start(bf16[64,16,128]{2,1,0:T(8,128)(2,1)} %field.1) | copy-start | bytes 786436
  2.2 15.9 %collective-permute-start = (bf16[80,128]{1,0:T(8,128)(2,1)S(1)}, bf16[80,128]{1,0:T(8,128)(2,1)S(1)}, u32[]{:S(2)}, u32[]{:S(2)}) collective-permute-start(bf16[80,128]{1,0:T(8,128)(2,1)S(1)} %pad_maximum_fusion.7), channel_id=1, source_target_pairs={{0,32},{32,64},{64,96},{96,128},{128,160},{160,192},{192,224},{224... | collective-permute-start | bytes 61448 | tf_op jit(solution)/shard_map/ppermute | solution.py:32
  7.0 11.0 %collective-permute-start.1 = (bf16[80,128]{1,0:T(8,128)(2,1)S(1)}, bf16[80,128]{1,0:T(8,128)(2,1)S(1)}, u32[]{:S(2)}, u32[]{:S(2)}) collective-permute-start(bf16[80,128]{1,0:T(8,128)(2,1)S(1)} %pad_maximum_fusion.8), channel_id=1, source_target_pairs={{32,0},{64,32},{96,64},{128,96},{160,128},{192,160},{224,192},{256... | collective-permute-start | bytes 61448 | tf_op jit(solution)/shard_map/ppermute | solution.py:33
  9.9 15.6 %all-to-all-start = ((f32[16,2,128]{2,1,0:T(2,128)}), f32[16,2,128]{2,1,0:T(2,128)S(1)}, u32[]{:S(2)}, u32[]{:S(2)}) async-start(f32[16,2,128]{2,1,0:T(2,128)} %shard_map.126), calls=%async_computation | async-start | bytes 32768 | tf_op jit(solution)/shard_map/all_to_all | solution.py:432
  19.4 22.5 %collective-permute-start.3 = (bf16[354,128]{1,0:T(8,128)(2,1)S(1)}, bf16[354,128]{1,0:T(8,128)(2,1)S(1)}, u32[]{:S(2)}, u32[]{:S(2)}) collective-permute-start(bf16[354,128]{1,0:T(8,128)(2,1)S(1)} %pad_maximum_fusion.3), channel_id=1, source_target_pairs={{0,1},{1,2},{2,3},{3,4},{4,5},{5,6},{6,7},{7,8},{8,9},{9,10},{10,1... | collective-permute-start | bytes 271880 | tf_op jit(solution)/shard_map/ppermute | solution.py:32
  22.9 19.0 %collective-permute-start.2 = (bf16[354,128]{1,0:T(8,128)(2,1)S(1)}, bf16[354,128]{1,0:T(8,128)(2,1)S(1)}, u32[]{:S(2)}, u32[]{:S(2)}) collective-permute-start(bf16[354,128]{1,0:T(8,128)(2,1)S(1)} %pad_maximum_fusion.2), channel_id=1, source_target_pairs={{1,0},{2,1},{3,2},{4,3},{5,4},{6,5},{7,6},{8,7},{9,8},{10,9},{11,1... | collective-permute-start | bytes 271880 | tf_op jit(solution)/shard_map/ppermute | solution.py:33
  25.6 0.6 copy-start.6
  27.5 23.1 %all-to-all-start.1 = ((f32[32,2,128]{2,1,0:T(2,128)}), f32[32,2,128]{2,1,0:T(2,128)S(1)}, u32[]{:S(2)}, u32[]{:S(2)}) async-start(f32[32,2,128]{2,1,0:T(2,128)} %shard_map.127), calls=%async_computation.1 | async-start | bytes 65536 | tf_op jit(solution)/shard_map/all_to_all | solution.py:434
  50.6 0.6 copy-start.4
  55.1 17.4 %all-to-all-start.2 = ((f32[16,4,128]{2,1,0:T(4,128)}), f32[16,4,128]{2,1,0:T(4,128)S(1)}, u32[]{:S(2)}, u32[]{:S(2)}) async-start(f32[16,4,128]{2,1,0:T(4,128)} %get-tuple-element.26), calls=%async_computation.2 | async-start | bytes 65536 | tf_op jit(solution)/shard_map/all_to_all | solution.py:432
  72.5 0.6 copy-start.5
  74.5 12.7 %all-to-all-start.3 = ((f32[32,4,128]{2,1,0:T(4,128)}), f32[32,4,128]{2,1,0:T(4,128)S(1)}, u32[]{:S(2)}, u32[]{:S(2)}) async-start(f32[32,4,128]{2,1,0:T(4,128)} %shard_map.129), calls=%async_computation.3 | async-start | bytes 131072 | tf_op jit(solution)/shard_map/all_to_all | solution.py:434
  79.3 30.0 %copy-start.1 = (bf16[3,3,128,128]{3,2,1,0:T(8,128)(2,1)S(1)}, bf16[3,3,128,128]{3,2,1,0:T(8,128)(2,1)}, u32[]{:S(2)}) copy-start(bf16[3,3,128,128]{3,2,1,0:T(8,128)(2,1)} %param.10) | copy-start | bytes 884740
  87.3 0.6 copy-start.3
  105.4 12.7 %all-to-all-start.5 = ((f32[32,4,128]{2,1,0:T(4,128)}), f32[32,4,128]{2,1,0:T(4,128)S(1)}, u32[]{:S(2)}, u32[]{:S(2)}) async-start(f32[32,4,128]{2,1,0:T(4,128)} %shard_map.133), calls=%async_computation.5 | async-start | bytes 131072 | tf_op jit(solution)/shard_map/all_to_all | solution.py:434
  118.1 0.6 copy-start.2
  134.3 15.5 %all-to-all-start.7 = ((bf16[4,768,128]{2,1,0:T(8,128)(2,1)}), bf16[4,768,128]{2,1,0:T(8,128)(2,1)S(1)}, u32[]{:S(2)}, u32[]{:S(2)}) async-start(bf16[4,768,128]{2,1,0:T(8,128)(2,1)} %bitcast.15), calls=%async_computation.7 | async-start | bytes 1572864 | tf_op jit(solution)/shard_map/all_to_all | solution.py:455
  150.8 17.1 %all-to-all-start.8 = ((bf16[64,12,128]{2,1,0:T(8,128)(2,1)}), bf16[64,12,128]{2,1,0:T(8,128)(2,1)S(1)}, u32[]{:S(2)}, u32[]{:S(2)}) async-start(bf16[64,12,128]{2,1,0:T(8,128)(2,1)} %reshape.134), calls=%async_computation.8 | async-start | bytes 524288 | tf_op jit(solution)/shard_map/all_to_all | solution.py:455

commit v3 on v2

--- a/solution.py
+++ b/solution.py
@@ -7,6 +7,7 @@
 from jax.experimental.pallas import tpu as pltpu
 from jax.sharding import Mesh
 from jax.sharding import PartitionSpec as P
+
 
 GROUPS = 32
 GY = ("gy_0", "gy_1")
@@ -18,27 +19,31 @@
 LANES = 128
 EPSILON = 1e-05
 
+HBM = pltpu.HBM
 PITCH = 32
 FINE_RIM = 3
 COARSE_RIM = 2
 
 
-def exchanged(parts, axis):
-    count = lax.axis_size(axis)
-    up = [(i, i + 1) for i in range(count - 1)]
-    down = [(i + 1, i) for i in range(count - 1)]
-    heads = jnp.concatenate([head.reshape(-1, LANES) for head, _ in parts])
-    tails = jnp.concatenate([tail.reshape(-1, LANES) for _, tail in parts])
-    before = lax.ppermute(tails, axis, up)
-    after = lax.ppermute(heads, axis, down)
-    result, at = [], 0
-    for head, _ in parts:
-        rows = head.size // LANES
-        result.append(
-            (before[at : at + rows].reshape(head.shape), after[at : at + rows].reshape(head.shape))
-        )
-        at += rows
-    return result
+def swap(heads, tails, axis):
+    ends = lax.axis_size(axis) - 1
+    before = lax.ppermute(tails, axis, [(i, i + 1) for i in range(ends)])
+    after = lax.ppermute(heads, axis, [(i + 1, i) for i in range(ends)])
+    return before, after
+
+
+def joined(fine, coarse):
+    cells = coarse.reshape(-1, coarse.shape[2])
+    return jnp.concatenate(
+        [fine.reshape(-1, LANES)] + [cells[:, k : k + LANES] for k in range(0, cells.shape[1], LANES)]
+    )
+
+
+def parted(rims, fine, coarse):
+    size = fine[0] * fine[1]
+    cells = coarse[0] * coarse[1]
+    halves = [rims[size + k * cells : size + (k + 1) * cells] for k in range(coarse[2] // LANES)]
+    return rims[:size].reshape(fine), jnp.concatenate(halves, axis=1).reshape(coarse)
 
 
 def ring(own, left, right, pitch):
@@ -47,28 +52,42 @@
     return jnp.concatenate([own, right, jnp.zeros((rows, gap, channels), own.dtype), left], axis=1)
 
 
-def with_rims(fine, coarse, wide, narrow):
-    (f0, f1), (c0, c1) = exchanged(
-        ((fine[:wide], fine[-wide:]), (coarse[:narrow], coarse[-narrow:])), GY
-    )
+def with_rims(fine, coarse, heads, tails):
+    shapes = (FINE_RIM,) + fine.shape[1:], (COARSE_RIM,) + coarse.shape[1:]
+    (f0, c0), (f1, c1) = (parted(r, *shapes) for r in swap(heads, tails, GY))
     fine = jnp.concatenate([f0, fine, f1])
     coarse = jnp.concatenate([c0, coarse, c1])
-    (f0, f1), (c0, c1) = exchanged(
-        ((fine[:, :wide], fine[:, -wide:]), (coarse[:, :narrow], coarse[:, -narrow:])), GX
-    )
+    shapes = (
+        (fine.shape[0], FINE_RIM, fine.shape[2]),
+        (coarse.shape[0], COARSE_RIM, coarse.shape[2]),
+    )
+    heads = joined(fine[:, :FINE_RIM], coarse[:, :COARSE_RIM])
+    tails = joined(fine[:, -FINE_RIM:], coarse[:, -COARSE_RIM:])
+    rims = swap(heads, tails, GX)
+    (f0, c0), (f1, c1) = (parted(r, *shapes) for r in rims)
     return ring(fine, f0, f1, PITCH), ring(coarse, c0, c1, PITCH // 2)
 
 
-def call(body, outs, *args, scratch=()):
+def call(body, outs, *args, scratch=(), plain=()):
     spaces = [
         pl.BlockSpec(memory_space=pltpu.SMEM if a.dtype == jnp.int32 else pltpu.VMEM) for a in args
     ]
+    args = [
+        a
+        if a.dtype == jnp.int32
+        else pltpu.with_memory_space_constraint(a, pltpu.HBM if k in plain else pltpu.VMEM)
+        for k, a in enumerate(args)
+    ]
     return pl.pallas_call(
         body,
-        out_shape=[jax.ShapeDtypeStruct(shape, dtype) for shape, dtype in outs],
+        out_shape=[
+            (pltpu.VMEM if len(o) == 2 else o[2] or jax.ShapeDtypeStruct)(o[0], o[1])
+            for o in outs
+        ],
         in_specs=spaces,
         out_specs=[pl.BlockSpec(memory_space=pltpu.VMEM) for _ in outs],
         scratch_shapes=[pltpu.VMEM(shape, dtype) for shape, dtype in scratch],
+        compiler_params=pltpu.CompilerParams(vmem_limit_bytes=24 << 20),
     )(*args)
 
 
@@ -115,7 +134,17 @@
         copies[:, k, :] = jnp.broadcast_to(row, (copies.shape[0], LANES))
 
 
-def field_sums(field, copies):
+def slab(rims, at, values):
+    cells = values.reshape(-1, values.shape[-1])
+    for lane in range(0, cells.shape[1], LANES):
+        rims[at : at + cells.shape[0]] = cells[:, lane : lane + LANES]
+        at += cells.shape[0]
+    return at
+
+
+def field_sums(field, grad, copies, heads, tails):
+    slab(heads, slab(heads, 0, field[:FINE_RIM]), grad[:COARSE_RIM])
+    slab(tails, slab(tails, 0, field[field.shape[0] - FINE_RIM :]), grad[grad.shape[0] - COARSE_RIM :])
     first = jnp.zeros((8, LANES), jnp.float32)
     second = jnp.zeros((8, LANES), jnp.float32)
     for at in range(0, field.shape[0], 8):
@@ -134,7 +163,7 @@
 
 
 def fine_forward(count, rows, cols, place, x, sums, gain, weight, projection,
-                 hidden, pooled, coarse, copies, stats, block):
+                 center, pooled, coarse, copies, stats, hidden, block):
     tot = jnp.sum(sums[...], axis=0)
     average, inverse = moments(tot[0:1], tot[1:2], count, LANES // GROUPS)
     stats[0] = average
@@ -152,6 +181,7 @@
         h = jnp.where(keep, h, 0.0)
         hidden[at : at + step, :, 0:LANES] = pltpu.roll(h, 1, 1).astype(jnp.bfloat16)
         hidden[at : at + step, :, LANES : 2 * LANES] = h.astype(jnp.bfloat16)
+        center[at : at + step] = h.astype(jnp.bfloat16)
         hidden[at : at + step, :, 2 * LANES :] = pltpu.roll(h, PITCH - 1, 1).astype(jnp.bfloat16)
     step = (lines - 2) // 4
     for at in range(0, lines - 2, step):
@@ -191,7 +221,10 @@
     spread(copies, [first[:, :LANES], first[:, LANES:], second[:, :LANES], second[:, LANES:]])
 
 
-def coarse_transpose(grad, weight, out, shifted):
+def coarse_transpose(grad, weight, fine_weight, out, fine_out, shifted):
+    for tap in range(9):
+        block = fine_weight[tap].astype(jnp.float32).T.astype(jnp.bfloat16)
+        fine_out[tap // 3, tap % 3 * LANES : (tap % 3 + 1) * LANES] = block
     half = PITCH // 2
     lines = grad.shape[0]
     step = lines // 4
@@ -242,9 +275,7 @@
         h = jnp.where(
             in_grid(h.shape, at - 1 + place[2], place[3], COARSE_RIM, rows, cols), h, 0.0
         )
-        hidden[at : at + step, :, 0:channels] = pltpu.roll(h, 1, 1).astype(jnp.bfloat16)
-        hidden[at : at + step, :, channels : 2 * channels] = h.astype(jnp.bfloat16)
-        hidden[at : at + step, :, 2 * channels :] = pltpu.roll(h, half - 1, 1).astype(jnp.bfloat16)
+        hidden[at : at + step] = h.astype(jnp.bfloat16)
         dact = pre[span] * (sigma * (1.0 + act * (1.0 - sigma)))
         dn = dact * gain[...]
         dnorm[span] = dn
@@ -256,10 +287,16 @@
     spread(copies, [first[:, :LANES], first[:, LANES:], second[:, :LANES], second[:, LANES:]])
 
 
-def coarse_rest(hidden, coarse, grad, weight, out, rows_out):
+def coarse_rest(center, coarse, grad, weight, out, rows_out, hidden):
     half = PITCH // 2
     height = out.shape[0]
     channels = out.shape[2]
+    step = center.shape[0] // 2
+    for at in range(0, center.shape[0], step):
+        h = center[at : at + step].astype(jnp.float32)
+        hidden[at : at + step, :, 0:channels] = pltpu.roll(h, 1, 1).astype(jnp.bfloat16)
+        hidden[at : at + step, :, channels : 2 * channels] = center[at : at + step]
+        hidden[at : at + step, :, 2 * channels :] = pltpu.roll(h, half - 1, 1).astype(jnp.bfloat16)
     step = height // 2
     for at in range(0, height, step):
         acc = coarse[(at + 1) * half : (at + 1 + step) * half].astype(jnp.float32)
@@ -368,33 +405,36 @@
         u = up[(at + 1) * PITCH : (at + 1 + step) * PITCH].reshape(step, PITCH, LANES)[:, 0:width]
         u = jnp.broadcast_to(u[:, None], (step, 2, width, LANES)).reshape(2 * step, width, LANES)
         partial[2 * at : 2 * at + 2 * step] = u + inverse * dn
-    d = up[PITCH : (lines - 1) * PITCH].reshape(lines - 2, PITCH, LANES)[:, 0:width]
-    d = jnp.broadcast_to(
-        d.astype(jnp.bfloat16)[:, None], (lines - 2, 2, width, LANES)
-    ).reshape(height * width, LANES)
+    for at in range(1, lines - 1, step):
+        u = up[at * PITCH : (at + step) * PITCH].reshape(step, PITCH, LANES)
+        own = lax.broadcasted_iota(jnp.int32, u.shape, 1) < width
+        u = jnp.where(own, u, 0.0)
+        shifted[at : at + step, :, 0:LANES] = pltpu.roll(u, PITCH - 1, 1).astype(jnp.bfloat16)
+        shifted[at : at + step, :, LANES : 2 * LANES] = u.astype(jnp.bfloat16)
+        shifted[at : at + step, :, 2 * LANES :] = pltpu.roll(u, 1, 1).astype(jnp.bfloat16)
+    d = shifted[1 : lines - 1]
+    d = jnp.broadcast_to(d[:, None], (lines - 2, 2) + d.shape[1:])
+    d = d.reshape(height * PITCH, 3 * LANES)
     at = 18 * channels
     for tap in range(3):
         begin = FINE_RIM - 1 + tap
         k = lax.dot_general(
-            hidden[begin : begin + height, 0:width, :].reshape(height * width, 3 * LANES),
+            hidden[begin : begin + height].reshape(height * PITCH, LANES),
             d,
             (((0,), (0,)), ((), ())),
             preferred_element_type=jnp.float32,
-        )
-        rows_out[at : at + 3 * LANES] = k.astype(jnp.bfloat16)
-        at += 3 * LANES
+        ).astype(jnp.bfloat16)
+        for col_tap in range(3):
+            rows_out[at : at + LANES] = k[:, col_tap * LANES : (col_tap + 1) * LANES]
+            at += LANES
     proj_grad = proj_grad.astype(jnp.bfloat16)
     rows_out[at : at + LANES] = proj_grad[:, :LANES]
     rows_out[at + LANES : at + 2 * LANES] = proj_grad[:, LANES:]
     at += 2 * LANES
     spare = rows_out.shape[0] - at
     small = jnp.concatenate([first, second], axis=0)
-    high = small.astype(jnp.bfloat16).astype(jnp.float32)
-    middle = (small - high).astype(jnp.bfloat16).astype(jnp.float32)
-    low = small - high - middle
-    tail = jnp.concatenate([high, middle, low, jnp.zeros_like(low)], axis=0)
     rows_out[at:] = jnp.concatenate(
-        [jnp.zeros((spare - 8, LANES), jnp.float32), tail], axis=0
+        [jnp.zeros((spare - 8, LANES), jnp.float32), split(small)], axis=0
     ).astype(jnp.bfloat16)
 
 
@@ -430,8 +470,37 @@
 def gathered(copies):
     far = lax.axis_size(FAR)
     received = lax.all_to_all(copies, NEAR, 0, 0, tiled=True)
-    (copies,) = call(relay, [((far,) + copies.shape[1:], jnp.float32)], received)
+    (copies,) = call(relay, [((far,) + copies.shape[1:], jnp.float32, None)], received)
     return lax.all_to_all(copies, FAR, 0, 0, tiled=True)
+
+
+def split(small):
+    high = small.astype(jnp.bfloat16).astype(jnp.float32)
+    middle = (small - high).astype(jnp.bfloat16).astype(jnp.float32)
+    low = small - high - middle
+    return jnp.concatenate([high, middle, low, jnp.zeros_like(low)], axis=0)
+
+
+def add_up(stage, place, pieces, out, *scratch):
+    rows = pieces.shape[1]
+    step = 256 if rows % 256 == 0 else rows
+    pitch = out.shape[-2]
+    for at in range(0, rows, step):
+        sums = pieces[0, at : at + step].astype(jnp.float32)
+        for k in range(1, pieces.shape[0]):
+            sums = sums + pieces[k, at : at + step].astype(jnp.float32)
+        if at + step == rows:
+            last = sums[step - 8 :]
+            tail = split(last[0:2] + last[2:4] + last[4:6])
+            tail = jnp.where(place[4 + stage] == 1, tail, last)
+            sums = jnp.concatenate([sums[: step - 8], tail], axis=0)
+        if scratch:
+            scratch[0][at : at + step] = sums
+        else:
+            out[at : at + step] = sums.astype(jnp.bfloat16)
+    if scratch:
+        for k in range(out.shape[0]):
+            out[k] = scratch[0][k * pitch : (k + 1) * pitch].astype(jnp.bfloat16)
 
 
 def planes(values):
@@ -443,22 +512,29 @@
     )
 
 
-def from_planes(rows):
-    rows = rows.astype(jnp.float32)
-    return rows[0:2] + rows[2:4] + rows[4:6]
-
-
-def gradient_totals(part):
-    holder = True
-    for axes in STAGES:
+def gradient_totals(part, place):
+    for stage, axes in enumerate(STAGES):
         count = lax.axis_size(axes)
         pieces = lax.all_to_all(part.reshape(count, -1, LANES), axes, 0, 0, tiled=True)
-        sums = jnp.sum(pieces.astype(jnp.float32), axis=0)
-        holder = holder & (lax.axis_index(axes) == count - 1)
-        tail = jnp.where(holder, planes(from_planes(sums[-8:])), sums[-8:].astype(jnp.bfloat16))
-        part = lax.dynamic_update_slice(
-            sums.astype(jnp.bfloat16), tail, (sums.shape[0] - 8, 0)
-        )
+        rows = pieces.shape[1]
+        kernel = functools.partial(add_up, stage)
+        if stage == 0:
+            (part,) = call(kernel, [((rows, LANES), jnp.bfloat16, None)], place, pieces)
+        elif stage == 1:
+            pitch = rows // lax.axis_size(STAGES[2])
+            (part,) = call(
+                kernel,
+                [((rows // pitch, pitch, LANES), jnp.bfloat16, None)],
+                place,
+                pieces,
+                scratch=[((rows, LANES), jnp.float32)],
+            )
+        else:
+            sums = jnp.sum(pieces.astype(jnp.float32), axis=0)
+            last = sums[-8:]
+            tail = planes(last[0:2] + last[2:4] + last[4:6])
+            tail = jnp.where(place[4 + stage] == 1, tail, last.astype(jnp.bfloat16))
+            part = jnp.concatenate([sums[:-8].astype(jnp.bfloat16), tail])
     for axes in STAGES[::-1]:
         count = lax.axis_size(axes)
         copies = jnp.broadcast_to(part[None], (count,) + part.shape)
@@ -477,29 +553,42 @@
     f32, bf16 = jnp.float32, jnp.bfloat16
     near = lax.axis_size(NEAR)
     row, col = lax.axis_index(GY), lax.axis_index(GX)
-    place = jnp.stack([row * height, col * width, row * half_h, col * half_w]).astype(jnp.int32)
+    holds, held = [], jnp.int32(1)
+    for axes in STAGES:
+        held = held * (lax.axis_index(axes) == lax.axis_size(axes) - 1)
+        holds.append(held)
+    place = jnp.stack([row * height, col * width, row * half_h, col * half_w] + holds)
+    place = place.astype(jnp.int32)
     gain_f, gain_c = gain_fine.reshape(1, -1), gain_coarse.reshape(1, -1)
-    weight_t = weight_fine.transpose(0, 1, 3, 2).reshape(3, 3 * chan_fine, chan_fine)
-
-    (copies,) = call(field_sums, [((near, 2, LANES), f32)], field)
+
+    slabs = FINE_RIM * width + COARSE_RIM * half_w * chan_coarse // LANES
+    copies, heads, tails = call(
+        field_sums,
+        [((near, 2, LANES), f32, None), ((slabs, LANES), bf16, None), ((slabs, LANES), bf16, None)],
+        field,
+        cotangent,
+        plain=(0, 1),
+    )
     sums = gathered(copies)
-    x, grad = with_rims(field, cotangent, FINE_RIM, COARSE_RIM)
+    x, grad = with_rims(field, cotangent, heads, tails)
     lines = half_h + 2
     cells = lines * PITCH // 2
-    (pre,) = call(
+    pre, weight_t = call(
         coarse_transpose,
-        [((cells, chan_coarse), f32)],
+        [((cells, chan_coarse), f32), ((3, 3 * chan_fine, chan_fine), bf16, HBM)],
         grad,
         weight_coarse,
+        weight_fine.reshape(9, chan_fine, chan_fine),
+        plain=(1, 2),
         scratch=[((3,) + grad.shape, bf16)],
     )
     hidden_f, pooled, coarse, copies, stats_f = call(
         functools.partial(fine_forward, fine_count, rows, cols),
         [
-            (x.shape[:2] + (3 * chan_fine,), bf16),
-            ((cells, chan_fine), bf16),
+            (x.shape, bf16, HBM),
+            ((cells, chan_fine), bf16, HBM),
             ((cells, chan_coarse), bf16),
-            ((near, 4, LANES), f32),
+            ((near, 4, LANES), f32, None),
             ((2, 8, chan_fine), f32),
         ],
         place,
@@ -508,15 +597,18 @@
         gain_f,
         weight_fine.reshape(3, 3 * chan_fine, chan_fine),
         projection,
-        scratch=[((2 * lines * PITCH + 8, chan_fine), f32)],
+        scratch=[
+            (x.shape[:2] + (3 * chan_fine,), bf16),
+            ((2 * lines * PITCH + 8, chan_fine), f32),
+        ],
     )
     sums = gathered(copies)
     hidden_c, dnorm, copies, stats_c = call(
         functools.partial(coarse_middle, coarse_count, rows // 2, cols // 2),
         [
-            ((lines, PITCH // 2, 3 * chan_coarse), bf16),
-            ((cells, chan_coarse), f32),
-            ((near, 4, LANES), f32),
+            ((lines, PITCH // 2, chan_coarse), bf16, HBM),
+            ((cells, chan_coarse), f32, HBM),
+            ((near, 4, LANES), f32, None),
             ((2, 8, chan_coarse), f32),
         ],
         place,
@@ -530,17 +622,19 @@
     used += -(used + 8) % (4 * lax.axis_size(GY_GX)) + 8
     coarse_output, parts = call(
         coarse_rest,
-        [((half_h, half_w, chan_coarse), bf16), ((18 * chan_coarse, LANES), bf16)],
+        [((half_h, half_w, chan_coarse), bf16, None), ((18 * chan_coarse, LANES), bf16)],
         hidden_c,
         coarse,
         grad,
         weight_coarse.reshape(3, 3 * chan_coarse, chan_coarse),
+        scratch=[((lines, PITCH // 2, 3 * chan_coarse), bf16)],
+        plain=(0, 3),
     )
     parts, coarse_gain_grad, partial = call(
         functools.partial(fine_backward, coarse_count, rows // 2, cols // 2),
         [
-            ((used, LANES), bf16),
-            ((1, chan_coarse), f32),
+            ((used, LANES), bf16, None),
+            ((1, chan_coarse), f32, None),
             ((height, width, chan_fine), f32),
         ],
         place,
@@ -563,16 +657,17 @@
             ((lines, PITCH, 3 * chan_fine), bf16),
             ((3, lines, PITCH // 2, chan_fine), f32),
         ],
-    )
-    totals = gradient_totals(parts)
+        plain=(3, 5, 8, 9, 11),
+    )
+    totals = gradient_totals(parts, place)
     field_grad, fine_weight_grad, fine_gain_grad, projection_grad, coarse_weight_grad = call(
         functools.partial(finish, fine_count),
         [
-            ((height, width, chan_fine), bf16),
-            ((9 * chan_fine, chan_fine), f32),
-            ((1, chan_fine), f32),
-            ((chan_fine, chan_coarse), f32),
-            ((9 * chan_coarse, chan_coarse), f32),
+            ((height, width, chan_fine), bf16, None),
+            ((9 * chan_fine, chan_fine), f32, None),
+            ((1, chan_fine), f32, None),
+            ((chan_fine, chan_coarse), f32, None),
+            ((9 * chan_coarse, chan_coarse), f32, None),
         ],
         totals,
         partial,
@@ -595,6 +690,7 @@
     finer = Mesh(mesh.devices.reshape(2, 8, 2, 8, 2), GY_GX)
     in_specs = (P(GY, GX, None), P(GY, GX, None), P(), P(), P(), P(), P())
     out_specs = (P(GY, GX, None), P(GY, GX, None), P(), P(), P(), P(), P())
+
     return jax.shard_map(
         on_device, mesh=finer, in_specs=in_specs, out_specs=out_specs, check_vma=False
     )

time: 213 us -> 201 us (0.944)
  blocking collectives: 59.6 us -> 70.5 us
  starting transfers between devices: 59.8 us -> 51.6 us
  local copies, waits for them, and re-layouts: 8.16 us -> 0.95 us
  Pallas kernels: 29.2 us -> 22.6 us
  waiting for transfers between devices: 47.8 us -> 50.9 us
  other arithmetic: 5.66 us -> 2.75 us
    all_to_all x1 -> x2, blocking collectives: 7.31 us -> 20.6 us  [gradient_totals(): lax.all_to_all(part.reshape(count, -1, LANES), axes, 0, 0, tiled=True)]
    all_to_all x2 -> x1, waiting for transfers between devices: 24.4 us -> 12.3 us  [gradient_totals(): lax.all_to_all(part.reshape(count, -1, LANES), axes, 0, 0, tiled=True)]
    all_to_all x2, waiting for transfers between devices: 7.2 us -> 14.4 us  [gathered(): received = lax.all_to_all(copies, NEAR, 0, 0, tiled=True)]
    pallas_call x10 -> x12, Pallas kernels: 29.2 us -> 22.6 us  [call(): pl.pallas_call(body, out_shape=[(pltpu.VMEM if len(o) == 2 else o[2] or j...]
    all_to_all x2, starting transfers between devices: 18 us -> 13.8 us  [gathered(): received = lax.all_to_all(copies, NEAR, 0, 0, tiled=True)]
    all_to_all x3, waiting for transfers between devices: 16.3 us -> 20.3 us  [gathered(): return lax.all_to_all(copies, FAR, 0, 0, tiled=True)]
    unnamed x16 -> x12, local copies, waits for them, and re-layouts: 4.02 us -> 0.04 us
    ppermute x4, waiting for transfers between devices: 0.01 us -> 3.85 us  [the longest x2 3.85 us: swap(): after = lax.ppermute(heads, axis, [(i + 1, i) for i in range(ends)])]
  transfers between devices with their start and end apart: 11 -> 10, of which waited for: 6 -> 7; matrix products, arithmetic and copies ran while one was open for 2% -> 0% of each run, Pallas kernels for 5% -> 3%
where the time goes in v3:
time: 201 us; the launch traced here: 200 us
  blocking collectives  70.5 us (35%)
  starting transfers between devices  51.6 us (26%)
  waiting for transfers between devices  50.9 us (25%)
  Pallas kernels  22.6 us (11%)
  other arithmetic  2.75 us (1%)
    all_to_all x3, blocking collectives, gradient_totals(): part = lax.all_to_all(copies, axes, 0, 0, tiled=True).reshape(-1, LANES)  38.5 us
    pallas_call x12, Pallas kernels, call(): pl.pallas_call(body, out_shape=[(pltpu.VMEM if len(o) == 2 else o[2] or j...  22.6 us
    all_to_all x2, blocking collectives, gradient_totals(): lax.all_to_all(part.reshape(count, -1, LANES), axes, 0, 0, tiled=True)  20.6 us
    all_to_all x3, waiting for transfers between devices, gathered(): return lax.all_to_all(copies, FAR, 0, 0, tiled=True)  20.3 us
    all_to_all x3, starting transfers between devices, gathered(): return lax.all_to_all(copies, FAR, 0, 0, tiled=True)  20 us
    all_to_all x2, waiting for transfers between devices, gathered(): received = lax.all_to_all(copies, NEAR, 0, 0, tiled=True)  14.4 us
    all_to_all x2, starting transfers between devices, gathered(): received = lax.all_to_all(copies, NEAR, 0, 0, tiled=True)  13.8 us
    all_to_all x1, waiting for transfers between devices, gradient_totals(): lax.all_to_all(part.reshape(count, -1, LANES), axes, 0, 0, tiled=True)  12.3 us
  transfers between devices with their start and end apart: 10, of which 7 were waited for; matrix products, arithmetic and copies ran while one was open for 0% of the time, Pallas kernels for 3%

profile of v3, /device:TPU:1, one launch (start us, length us, event | category | flops | bytes accessed | tf_op | source)
XLA Modules:
  0.0 200.3 jit_solution(5612439272129641316)
XLA Ops:
  0.6 1.7 shard_map.126
  2.3 4.8 %collective-permute-start = (bf16[80,128]{1,0:T(8,128)(2,1)S(1)}, bf16[80,128]{1,0:T(8,128)(2,1)S(1)}, u32[]{:S(2)}, u32[]{:S(2)}) collective-permute-start(bf16[80,128]{1,0:T(8,128)(2,1)S(1)} %get-tuple-element.31), channel_id=1, source_target_pairs={{0,32},{32,64},{64,96},{96,128},{128,160},{160,192},{192,224},{224... | collective-permute-start | bytes 61448 | tf_op jit(solution)/shard_map/ppermute | solution.py:30
  7.1 1.3 collective-permute-start.1
  8.4 3.8 %collective-permute-done.1 = bf16[80,128]{1,0:T(8,128)(2,1)S(1)} collective-permute-done((bf16[80,128]{1,0:T(8,128)(2,1)S(1)}, bf16[80,128]{1,0:T(8,128)(2,1)S(1)}, u32[]{:S(2)}, u32[]{:S(2)}) %collective-permute-start.1) | collective-permute-done | bytes 20512 | tf_op jit(solution)/shard_map/ppermute | solution.py:31
  12.3 1.1 pad_maximum_fusion.9
  14.6 5.0 %collective-permute-start.3 = (bf16[354,128]{1,0:T(8,128)(2,1)S(1)}, bf16[354,128]{1,0:T(8,128)(2,1)S(1)}, u32[]{:S(2)}, u32[]{:S(2)}) collective-permute-start(bf16[354,128]{1,0:T(8,128)(2,1)S(1)} %pad_maximum_fusion.3), channel_id=1, source_target_pairs={{0,1},{1,2},{2,3},{3,4},{4,5},{5,6},{6,7},{7,8},{8,9},{9,10},{10,1... | collective-permute-start | bytes 271880 | tf_op jit(solution)/shard_map/ppermute | solution.py:30
  19.8 2.1 %collective-permute-start.2 = (bf16[354,128]{1,0:T(8,128)(2,1)S(1)}, bf16[354,128]{1,0:T(8,128)(2,1)S(1)}, u32[]{:S(2)}, u32[]{:S(2)}) collective-permute-start(bf16[354,128]{1,0:T(8,128)(2,1)S(1)} %pad_maximum_fusion.2), channel_id=1, source_target_pairs={{1,0},{2,1},{3,2},{4,3},{5,4},{6,5},{7,6},{8,7},{9,8},{10,9},{11,1... | collective-permute-start | bytes 271880 | tf_op jit(solution)/shard_map/ppermute | solution.py:31
  21.9 8.7 %all-to-all-start = ((f32[16,2,128]{2,1,0:T(2,128)}), f32[16,2,128]{2,1,0:T(2,128)S(1)}, u32[]{:S(2)}, u32[]{:S(2)}) async-start(f32[16,2,128]{2,1,0:T(2,128)} %get-tuple-element.33), calls=%async_computation | async-start | bytes 32768 | tf_op jit(solution)/shard_map/all_to_all | solution.py:472
  30.8 7.1 %all-to-all-done.received = f32[16,2,128]{2,1,0:T(2,128)S(1)} async-done(((f32[16,2,128]{2,1,0:T(2,128)}), f32[16,2,128]{2,1,0:T(2,128)S(1)}, u32[]{:S(2)}, u32[]{:S(2)}) %all-to-all-start) | async-done | bytes 16416 | tf_op jit(solution)/shard_map/all_to_all | solution.py:472
  38.6 12.3 %all-to-all-start.1 = ((f32[32,2,128]{2,1,0:T(2,128)}), f32[32,2,128]{2,1,0:T(2,128)S(1)}, u32[]{:S(2)}, u32[]{:S(2)}) async-start(f32[32,2,128]{2,1,0:T(2,128)} %shard_map.127), calls=%async_computation.1 | async-start | bytes 65536 | tf_op jit(solution)/shard_map/all_to_all | solution.py:474
  51.2 8.4 %all-to-all-done.1.sums = f32[32,2,128]{2,1,0:T(2,128)S(1)} async-done(((f32[32,2,128]{2,1,0:T(2,128)}), f32[32,2,128]{2,1,0:T(2,128)S(1)}, u32[]{:S(2)}, u32[]{:S(2)}) %all-to-all-start.1) | async-done | bytes 32800 | tf_op jit(solution)/shard_map/all_to_all | solution.py:474
  59.6 3.2 %shard_map.128 = (bf16[70,32,128]{2,1,0:T(8,128)(2,1)}, bf16[544,128]{1,0:T(8,128)(2,1)}, bf16[544,256]{1,0:T(8,128)(2,1)S(1)}, f32[16,4,128]{2,1,0:T(4,128)}, f32[2,8,128]{2,1,0:T(8,128)S(1)}) custom-call(s32[7]{0:T(128)S(1)} %stack.31.place, bf16[70,32,128]{2,1,0:T(8,128)(2,1)S(1)} %pad_maximum_fusion.x, f32[32,2,128]{2,1,0:T(2,128)S(1)} %all-to-all-done.1.sums, ...), custom_call_target="tpu_custom_call" | custom-call | tf_op jit(solution)/shard_map/pallas_call | solution.py:81
  62.8 5.1 %all-to-all-start.2 = ((f32[16,4,128]{2,1,0:T(4,128)}), f32[16,4,128]{2,1,0:T(4,128)S(1)}, u32[]{:S(2)}, u32[]{:S(2)}) async-start(f32[16,4,128]{2,1,0:T(4,128)} %get-tuple-element.34), calls=%async_computation.2 | async-start | bytes 65536 | tf_op jit(solution)/shard_map/all_to_all | solution.py:472
  68.0 7.4 %all-to-all-done.2.received = f32[16,4,128]{2,1,0:T(4,128)S(1)} async-done(((f32[16,4,128]{2,1,0:T(4,128)}), f32[16,4,128]{2,1,0:T(4,128)S(1)}, u32[]{:S(2)}, u32[]{:S(2)}) %all-to-all-start.2) | async-done | bytes 32800 | tf_op jit(solution)/shard_map/all_to_all | solution.py:472
  76.0 3.9 %all-to-all-start.3 = ((f32[32,4,128]{2,1,0:T(4,128)}), f32[32,4,128]{2,1,0:T(4,128)S(1)}, u32[]{:S(2)}, u32[]{:S(2)}) async-start(f32[32,4,128]{2,1,0:T(4,128)} %shard_map.129), calls=%async_computation.3 | async-start | bytes 131072 | tf_op jit(solution)/shard_map/all_to_all | solution.py:474
  80.1 2.9 %shard_map.130 = (f32[544,256]{1,0:T(8,128)S(1)}, bf16[3,384,128]{2,1,0:T(8,128)(2,1)}) custom-call(bf16[36,16,256]{2,1,0:T(8,128)(2,1)S(1)} %pad_maximum_fusion.1.grad, bf16[3,3,256,256]{3,2,1,0:T(8,128)(2,1)} %weight.1, bf16[9,128,128]{2,1,0:T(8,128)(2,1)} %bitcast.29), custom_call_target="tpu_custom_call" | custom-call | tf_op jit(solution)/shard_map/pallas_call | solution.py:81
  83.0 5.8 %all-to-all-done.3.sums = f32[32,4,128]{2,1,0:T(4,128)S(1)} async-done(((f32[32,4,128]{2,1,0:T(4,128)}), f32[32,4,128]{2,1,0:T(4,128)S(1)}, u32[]{:S(2)}, u32[]{:S(2)}) %all-to-all-start.3) | async-done | bytes 65568 | tf_op jit(solution)/shard_map/all_to_all | solution.py:474
  88.8 2.1 %shard_map.131 = (bf16[34,16,256]{2,1,0:T(8,128)(2,1)}, f32[544,256]{1,0:T(8,128)}, f32[16,4,128]{2,1,0:T(4,128)S(1)}, f32[2,8,256]{2,1,0:T(8,128)S(1)}) custom-call(s32[7]{0:T(128)S(1)} %stack.31.place, f32[32,4,128]{2,1,0:T(4,128)S(1)} %all-to-all-done.3.sums, bf16[544,256]{1,0:T(8,128)(2,1)S(1)} %get-tuple-element.35.coarse, ...), custom_call_target="tpu_custom_call" | custom-call | tf_op jit(solution)/shard_map/pallas_call | solution.py:81
  90.9 11.4 %all_to_all.60.received = f32[16,4,128]{2,1,0:T(4,128)S(1)} all-to-all(f32[16,4,128]{2,1,0:T(4,128)S(1)} %get-tuple-element.39), channel_id=1, replica_groups=mesh['gy_0'=2,'gy_1'=8,'gx_0'=2,'gx_1'=8,'gx_2'=2] {'gx_1','gx_2'}, dimensions={0} | all-to-all | bytes 65536 | tf_op jit(solution)/shard_map/all_to_all | solution.py:472
  102.9 3.9 %all-to-all-start.5 = ((f32[32,4,128]{2,1,0:T(4,128)}), f32[32,4,128]{2,1,0:T(4,128)S(1)}, u32[]{:S(2)}, u32[]{:S(2)}) async-start(f32[32,4,128]{2,1,0:T(4,128)} %shard_map.133), calls=%async_computation.5 | async-start | bytes 131072 | tf_op jit(solution)/shard_map/all_to_all | solution.py:474
  106.8 2.8 %shard_map.132 = (bf16[32,8,256]{2,1,0:T(8,128)(2,1)}, bf16[4608,128]{1,0:T(8,128)(2,1)S(1)}) custom-call(bf16[34,16,256]{2,1,0:T(8,128)(2,1)} %get-tuple-element.37.center, bf16[544,256]{1,0:T(8,128)(2,1)S(1)} %get-tuple-element.35.coarse, bf16[36,16,256]{2,1,0:T(8,128)(2,1)S(1)} %pad_maximum_fusion.1.grad, bf16[3,768,256]{2,1,0:T(8,128)(2,1)} %bitcast.36), custom_call_target="tpu_custom_call" | custom-call | tf_op jit(solution)/shard_map/pallas_call | solution.py:81
  109.6 6.1 %all-to-all-done.5.sums = f32[32,4,128]{2,1,0:T(4,128)S(1)} async-done(((f32[32,4,128]{2,1,0:T(4,128)}), f32[32,4,128]{2,1,0:T(4,128)S(1)}, u32[]{:S(2)}, u32[]{:S(2)}) %all-to-all-start.5) | async-done | bytes 65568 | tf_op jit(solution)/shard_map/all_to_all | solution.py:474
  115.7 4.0 %shard_map.134 = (bf16[6144,128]{1,0:T(8,128)(2,1)S(1)}, f32[1,256]{1,0:T(1,128)}, f32[64,16,128]{2,1,0:T(8,128)S(1)}) custom-call(s32[7]{0:T(128)S(1)} %stack.31.place, f32[32,4,128]{2,1,0:T(4,128)S(1)} %all-to-all-done.5.sums, bf16[544,256]{1,0:T(8,128)(2,1)S(1)} %get-tuple-element.35.coarse, bf16[544,128]{1,0:T(8,128)(2,1)} %get-tuple-element.40.pooled, ...), custom_call_target="tpu_custom_call" | custom-call | tf_op jit(solution)/shard_map/pallas_call | solution.py:81
  119.7 6.1 %all_to_all.61.pieces = bf16[2,3072,128]{2,1,0:T(8,128)(2,1)S(1)} all-to-all(bf16[2,3072,128]{2,1,0:T(8,128)(2,1)S(1)} %bitcast.28), channel_id=1, replica_groups=mesh['gy_0'=2,'gy_1'=8,'gx_0'=2,'gx_1'=8,'gx_2'=2] {'gx_2'}, dimensions={0} | all-to-all | bytes 3145728 | tf_op jit(solution)/shard_map/all_to_all | solution.py:518
  126.6 14.4 %all_to_all.62.pieces = bf16[4,768,128]{2,1,0:T(8,128)(2,1)S(1)} all-to-all(bf16[4,768,128]{2,1,0:T(8,128)(2,1)S(1)} %bitcast.27), channel_id=1, replica_groups=mesh['gy_0'=2,'gy_1'=8,'gx_0'=2,'gx_1'=8,'gx_2'=2] {'gx_0','gy_0'}, dimensions={0} | all-to-all | bytes 1572864 | tf_op jit(solution)/shard_map/all_to_all | solution.py:518
  141.0 1.4 shard_map.136
  142.4 4.6 %all-to-all-start.8 = ((bf16[64,12,128]{2,1,0:T(8,128)(2,1)}), bf16[64,12,128]{2,1,0:T(8,128)(2,1)S(1)}, u32[]{:S(2)}, u32[]{:S(2)}) async-start(bf16[64,12,128]{2,1,0:T(8,128)(2,1)} %shard_map.136), calls=%async_computation.8 | async-start | bytes 524288 | tf_op jit(solution)/shard_map/all_to_all | solution.py:518
  147.1 12.3 %all-to-all-done.8 = bf16[64,12,128]{2,1,0:T(8,128)(2,1)S(1)} async-done(((bf16[64,12,128]{2,1,0:T(8,128)(2,1)}), bf16[64,12,128]{2,1,0:T(8,128)(2,1)S(1)}, u32[]{:S(2)}, u32[]{:S(2)}) %all-to-all-start.8) | async-done | bytes 196640 | tf_op jit(solution)/shard_map/all_to_all | solution.py:518
  159.7 18.2 %all_to_all.63 = bf16[64,12,128]{2,1,0:T(8,128)(2,1)S(1)} all-to-all(bf16[64,12,128]{2,1,0:T(8,128)(2,1)S(1)} %broadcast_in_dim.32), channel_id=1, replica_groups=mesh['gy_0'=2,'gy_1'=8,'gx_0'=2,'gx_1'=8,'gx_2'=2] {'gx_1','gy_1'}, dimensions={0} | all-to-all | bytes 393216 | tf_op jit(solution)/shard_map/all_to_all | solution.py:541
  178.1 11.0 %all_to_all.64 = bf16[4,768,128]{2,1,0:T(8,128)(2,1)S(1)} all-to-all(bf16[4,768,128]{2,1,0:T(8,128)(2,1)S(1)} %broadcast_in_dim.34), channel_id=1, replica_groups=mesh['gy_0'=2,'gy_1'=8,'gx_0'=2,'gx_1'=8,'gx_2'=2] {'gx_0','gy_0'}, dimensions={0} | all-to-all | bytes 1572864 | tf_op jit(solution)/shard_map/all_to_all | solution.py:541
  189.3 9.2 %all_to_all.65 = bf16[2,3072,128]{2,1,0:T(8,128)(2,1)S(1)} all-to-all(bf16[2,3072,128]{2,1,0:T(8,128)(2,1)S(1)} %broadcast_in_dim.36), channel_id=1, replica_groups=mesh['gy_0'=2,'gy_1'=8,'gx_0'=2,'gx_1'=8,'gx_2'=2] {'gx_2'}, dimensions={0} | all-to-all | bytes 3145728 | tf_op jit(solution)/shard_map/all_to_all | solution.py:541
  198.5 1.8 shard_map.137
  (63 shorter events, 5.3 us)
Async XLA Ops:
  2.3 6.1 %collective-permute-start = (bf16[80,128]{1,0:T(8,128)(2,1)S(1)}, bf16[80,128]{1,0:T(8,128)(2,1)S(1)}, u32[]{:S(2)}, u32[]{:S(2)}) collective-permute-start(bf16[80,128]{1,0:T(8,128)(2,1)S(1)} %get-tuple-element.31), channel_id=1, source_target_pairs={{0,32},{32,64},{64,96},{96,128},{128,160},{160,192},{192,224},{224... | collective-permute-start | bytes 61448 | tf_op jit(solution)/shard_map/ppermute | solution.py:30
  7.1 5.2 %collective-permute-start.1 = (bf16[80,128]{1,0:T(8,128)(2,1)S(1)}, bf16[80,128]{1,0:T(8,128)(2,1)S(1)}, u32[]{:S(2)}, u32[]{:S(2)}) collective-permute-start(bf16[80,128]{1,0:T(8,128)(2,1)S(1)} %get-tuple-element.32), channel_id=1, source_target_pairs={{32,0},{64,32},{96,64},{128,96},{160,128},{192,160},{224,192},{256... | collective-permute-start | bytes 61448 | tf_op jit(solution)/shard_map/ppermute | solution.py:31
  12.3 38.6 %copy-start.4 = (bf16[64,16,128]{2,1,0:T(8,128)(2,1)S(1)}, bf16[64,16,128]{2,1,0:T(8,128)(2,1)}, u32[]{:S(2)}) copy-start(bf16[64,16,128]{2,1,0:T(8,128)(2,1)} %field.1) | copy-start | bytes 786436
  14.5 45.1 %copy-start = (bf16[3,3,128,128]{3,2,1,0:T(8,128)(2,1)S(1)}, bf16[3,3,128,128]{3,2,1,0:T(8,128)(2,1)}, u32[]{:S(2)}) copy-start(bf16[3,3,128,128]{3,2,1,0:T(8,128)(2,1)} %param.10) | copy-start | bytes 884740
  14.5 45.1 %copy-start.1 = (bf16[128,256]{1,0:T(8,128)(2,1)S(1)}, bf16[128,256]{1,0:T(8,128)(2,1)}, u32[]{:S(2)}) copy-start(bf16[128,256]{1,0:T(8,128)(2,1)} %projection.3) | copy-start | bytes 196612
  14.5 45.1 %copy-start.2 = (f32[128]{0:T(128)S(1)}, f32[128]{0:T(128)}, u32[]{:S(2)}) copy-start(f32[128]{0:T(128)} %param.9) | copy-start | bytes 1540
  14.6 36.2 %collective-permute-start.3 = (bf16[354,128]{1,0:T(8,128)(2,1)S(1)}, bf16[354,128]{1,0:T(8,128)(2,1)S(1)}, u32[]{:S(2)}, u32[]{:S(2)}) collective-permute-start(bf16[354,128]{1,0:T(8,128)(2,1)S(1)} %pad_maximum_fusion.3), channel_id=1, source_target_pairs={{0,1},{1,2},{2,3},{3,4},{4,5},{5,6},{6,7},{7,8},{8,9},{9,10},{10,1... | collective-permute-start | bytes 271880 | tf_op jit(solution)/shard_map/ppermute | solution.py:30
  19.8 31.1 %collective-permute-start.2 = (bf16[354,128]{1,0:T(8,128)(2,1)S(1)}, bf16[354,128]{1,0:T(8,128)(2,1)S(1)}, u32[]{:S(2)}, u32[]{:S(2)}) collective-permute-start(bf16[354,128]{1,0:T(8,128)(2,1)S(1)} %pad_maximum_fusion.2), channel_id=1, source_target_pairs={{1,0},{2,1},{3,2},{4,3},{5,4},{6,5},{7,6},{8,7},{9,8},{10,9},{11,1... | collective-permute-start | bytes 271880 | tf_op jit(solution)/shard_map/ppermute | solution.py:31
  21.9 16.0 %all-to-all-start = ((f32[16,2,128]{2,1,0:T(2,128)}), f32[16,2,128]{2,1,0:T(2,128)S(1)}, u32[]{:S(2)}, u32[]{:S(2)}) async-start(f32[16,2,128]{2,1,0:T(2,128)} %get-tuple-element.33), calls=%async_computation | async-start | bytes 32768 | tf_op jit(solution)/shard_map/all_to_all | solution.py:472
  38.6 21.1 %all-to-all-start.1 = ((f32[32,2,128]{2,1,0:T(2,128)}), f32[32,2,128]{2,1,0:T(2,128)S(1)}, u32[]{:S(2)}, u32[]{:S(2)}) async-start(f32[32,2,128]{2,1,0:T(2,128)} %shard_map.127), calls=%async_computation.1 | async-start | bytes 65536 | tf_op jit(solution)/shard_map/all_to_all | solution.py:474
  51.0 28.9 %copy-start.5 = (bf16[32,8,256]{2,1,0:T(8,128)(2,1)S(1)}, bf16[32,8,256]{2,1,0:T(8,128)(2,1)}, u32[]{:S(2)}) copy-start(bf16[32,8,256]{2,1,0:T(8,128)(2,1)} %grad.1) | copy-start | bytes 393220
  62.8 12.5 %all-to-all-start.2 = ((f32[16,4,128]{2,1,0:T(4,128)}), f32[16,4,128]{2,1,0:T(4,128)S(1)}, u32[]{:S(2)}, u32[]{:S(2)}) async-start(f32[16,4,128]{2,1,0:T(4,128)} %get-tuple-element.34), calls=%async_computation.2 | async-start | bytes 65536 | tf_op jit(solution)/shard_map/all_to_all | solution.py:472
  76.0 12.7 %all-to-all-start.3 = ((f32[32,4,128]{2,1,0:T(4,128)}), f32[32,4,128]{2,1,0:T(4,128)S(1)}, u32[]{:S(2)}, u32[]{:S(2)}) async-start(f32[32,4,128]{2,1,0:T(4,128)} %shard_map.129), calls=%async_computation.3 | async-start | bytes 131072 | tf_op jit(solution)/shard_map/all_to_all | solution.py:474
  79.9 8.9 %copy-start.3 = (f32[256]{0:T(256)S(1)}, f32[256]{0:T(256)}, u32[]{:S(2)}) copy-start(f32[256]{0:T(256)} %param.12) | copy-start | bytes 3076
  102.9 12.7 %all-to-all-start.5 = ((f32[32,4,128]{2,1,0:T(4,128)}), f32[32,4,128]{2,1,0:T(4,128)S(1)}, u32[]{:S(2)}, u32[]{:S(2)}) async-start(f32[32,4,128]{2,1,0:T(4,128)} %shard_map.133), calls=%async_computation.5 | async-start | bytes 131072 | tf_op jit(solution)/shard_map/all_to_all | solution.py:474
  142.4 17.1 %all-to-all-start.8 = ((bf16[64,12,128]{2,1,0:T(8,128)(2,1)}), bf16[64,12,128]{2,1,0:T(8,128)(2,1)S(1)}, u32[]{:S(2)}, u32[]{:S(2)}) async-start(bf16[64,12,128]{2,1,0:T(8,128)(2,1)} %shard_map.136), calls=%async_computation.8 | async-start | bytes 524288 | tf_op jit(solution)/shard_map/all_to_all | solution.py:518

commit v4 on v3

--- a/solution.py
+++ b/solution.py
@@ -54,7 +54,8 @@
 
 def with_rims(fine, coarse, heads, tails):
     shapes = (FINE_RIM,) + fine.shape[1:], (COARSE_RIM,) + coarse.shape[1:]
-    (f0, c0), (f1, c1) = (parted(r, *shapes) for r in swap(heads, tails, GY))
+    rims = swap(heads, tails, GY)
+    (f0, c0), (f1, c1) = (parted(r, *shapes) for r in rims)
     fine = jnp.concatenate([f0, fine, f1])
     coarse = jnp.concatenate([c0, coarse, c1])
     shapes = (
@@ -64,8 +65,13 @@
     heads = joined(fine[:, :FINE_RIM], coarse[:, :COARSE_RIM])
     tails = joined(fine[:, -FINE_RIM:], coarse[:, -COARSE_RIM:])
     rims = swap(heads, tails, GX)
-    (f0, c0), (f1, c1) = (parted(r, *shapes) for r in rims)
-    return ring(fine, f0, f1, PITCH), ring(coarse, c0, c1, PITCH // 2)
+    f0, f1 = (parted(r, *shapes)[0] for r in rims)
+    return ring(fine, f0, f1, PITCH), (coarse, rims, shapes)
+
+
+def coarse_ring(coarse, rims, shapes):
+    c0, c1 = (parted(r, *shapes)[1] for r in rims)
+    return ring(coarse, c0, c1, PITCH // 2)
 
 
 def call(body, outs, *args, scratch=(), plain=()):
@@ -467,11 +473,14 @@
     proj[:, LANES:] = rows[at + LANES : at + 2 * LANES].astype(jnp.float32)
 
 
-def gathered(copies):
+def gathered(copies, late=None):
     far = lax.axis_size(FAR)
     received = lax.all_to_all(copies, NEAR, 0, 0, tiled=True)
     (copies,) = call(relay, [((far,) + copies.shape[1:], jnp.float32, None)], received)
-    return lax.all_to_all(copies, FAR, 0, 0, tiled=True)
+    if late is not None:
+        copies, late = lax.optimization_barrier((copies, late))
+    sums = lax.all_to_all(copies, FAR, 0, 0, tiled=True)
+    return sums if late is None else (sums, late)
 
 
 def split(small):
@@ -496,20 +505,14 @@
             sums = jnp.concatenate([sums[: step - 8], tail], axis=0)
         if scratch:
             scratch[0][at : at + step] = sums
+        elif len(out.shape) == 3:
+            for k in range(out.shape[0]):
+                out[k] = sums.astype(jnp.bfloat16)
         else:
             out[at : at + step] = sums.astype(jnp.bfloat16)
     if scratch:
         for k in range(out.shape[0]):
             out[k] = scratch[0][k * pitch : (k + 1) * pitch].astype(jnp.bfloat16)
-
-
-def planes(values):
-    high = lax.reduce_precision(values, 8, 7)
-    middle = lax.reduce_precision(values - high, 8, 7)
-    low = values - high - middle
-    return jnp.concatenate([high, middle, low, jnp.zeros((2, LANES), jnp.float32)]).astype(
-        jnp.bfloat16
-    )
 
 
 def gradient_totals(part, place):
@@ -530,12 +533,9 @@
                 scratch=[((rows, LANES), jnp.float32)],
             )
         else:
-            sums = jnp.sum(pieces.astype(jnp.float32), axis=0)
-            last = sums[-8:]
-            tail = planes(last[0:2] + last[2:4] + last[4:6])
-            tail = jnp.where(place[4 + stage] == 1, tail, last.astype(jnp.bfloat16))
-            part = jnp.concatenate([sums[:-8].astype(jnp.bfloat16), tail])
-    for axes in STAGES[::-1]:
+            (part,) = call(kernel, [((count, rows, LANES), jnp.bfloat16, None)], place, pieces)
+    part = lax.all_to_all(part, STAGES[2], 0, 0, tiled=True).reshape(-1, LANES)
+    for axes in STAGES[1::-1]:
         count = lax.axis_size(axes)
         copies = jnp.broadcast_to(part[None], (count,) + part.shape)
         part = lax.all_to_all(copies, axes, 0, 0, tiled=True).reshape(-1, LANES)
@@ -570,18 +570,9 @@
         plain=(0, 1),
     )
     sums = gathered(copies)
-    x, grad = with_rims(field, cotangent, heads, tails)
+    x, (tall, rims, shapes) = with_rims(field, cotangent, heads, tails)
     lines = half_h + 2
     cells = lines * PITCH // 2
-    pre, weight_t = call(
-        coarse_transpose,
-        [((cells, chan_coarse), f32), ((3, 3 * chan_fine, chan_fine), bf16, HBM)],
-        grad,
-        weight_coarse,
-        weight_fine.reshape(9, chan_fine, chan_fine),
-        plain=(1, 2),
-        scratch=[((3,) + grad.shape, bf16)],
-    )
     hidden_f, pooled, coarse, copies, stats_f = call(
         functools.partial(fine_forward, fine_count, rows, cols),
         [
@@ -602,7 +593,17 @@
             ((2 * lines * PITCH + 8, chan_fine), f32),
         ],
     )
-    sums = gathered(copies)
+    sums, (tall, rims) = gathered(copies, (tall, rims))
+    grad = coarse_ring(tall, rims, shapes)
+    pre, weight_t = call(
+        coarse_transpose,
+        [((cells, chan_coarse), f32), ((3, 3 * chan_fine, chan_fine), bf16, HBM)],
+        grad,
+        weight_coarse,
+        weight_fine.reshape(9, chan_fine, chan_fine),
+        plain=(1, 2),
+        scratch=[((3,) + grad.shape, bf16)],
+    )
     hidden_c, dnorm, copies, stats_c = call(
         functools.partial(coarse_middle, coarse_count, rows // 2, cols // 2),
         [

time: 201 us -> 199 us (0.990)
  blocking collectives: 70.5 us -> 86.7 us
  waiting for transfers between devices: 50.9 us -> 38.6 us
  starting transfers between devices: 51.6 us -> 47 us
    all_to_all x3 -> x2, blocking collectives: 38.5 us -> 20.3 us  [gradient_totals(): part = lax.all_to_all(copies, axes, 0, 0, tiled=True).reshape(-1, LANES)]
    all_to_all x0 -> x1, blocking collectives: none -> 18.2 us  [gradient_totals(): part = lax.all_to_all(part, STAGES[2], 0, 0, tiled=True).reshape(-1, LANES)]
    all_to_all x2 -> x3, blocking collectives: 20.6 us -> 36.8 us  [gradient_totals(): lax.all_to_all(part.reshape(count, -1, LANES), axes, 0, 0, tiled=True)]
    all_to_all x4 -> x3, waiting for transfers between devices: 32.6 us -> 20.2 us  [gathered(): sums = lax.all_to_all(copies, FAR, 0, 0, tiled=True)]
    all_to_all x4 -> x3, starting transfers between devices: 24.6 us -> 20 us  [gathered(): sums = lax.all_to_all(copies, FAR, 0, 0, tiled=True)]
    slice x2 -> x1, other arithmetic: 2.1 us -> 0.06 us  [with_rims(): heads = joined(fine[:, :FINE_RIM], coarse[:, :COARSE_RIM])]
    pallas_call x12 -> x13, Pallas kernels: 22.6 us -> 22.6 us  [call(): pl.pallas_call(body, out_shape=[(pltpu.VMEM if len(o) == 2 else o[2] or j...]
  transfers between devices with their start and end apart: 10 -> 9, of which waited for: 7 -> 6; matrix products, arithmetic and copies ran while one was open for 0% -> 0% of each run, Pallas kernels for 3% -> 3%
where the time goes in v4:
time: 199 us; the launch traced here: 198 us
  blocking collectives  86.7 us (44%)
  starting transfers between devices  47 us (24%)
  waiting for transfers between devices  38.6 us (19%)
  Pallas kernels  22.6 us (11%)
    all_to_all x3, blocking collectives, gradient_totals(): lax.all_to_all(part.reshape(count, -1, LANES), axes, 0, 0, tiled=True)  36.8 us
    pallas_call x13, Pallas kernels, call(): pl.pallas_call(body, out_shape=[(pltpu.VMEM if len(o) == 2 else o[2] or j...  22.6 us
    all_to_all x2, blocking collectives, gradient_totals(): part = lax.all_to_all(copies, axes, 0, 0, tiled=True).reshape(-1, LANES)  20.3 us
    all_to_all x3, waiting for transfers between devices, gathered(): sums = lax.all_to_all(copies, FAR, 0, 0, tiled=True)  20.2 us
    all_to_all x3, starting transfers between devices, gathered(): sums = lax.all_to_all(copies, FAR, 0, 0, tiled=True)  20 us
    all_to_all x1, blocking collectives, gradient_totals(): part = lax.all_to_all(part, STAGES[2], 0, 0, tiled=True).reshape(-1, LANES)  18.2 us
    all_to_all x2, waiting for transfers between devices, gathered(): received = lax.all_to_all(copies, NEAR, 0, 0, tiled=True)  14.6 us
    all_to_all x2, starting transfers between devices, gathered(): received = lax.all_to_all(copies, NEAR, 0, 0, tiled=True)  13.8 us
  transfers between devices with their start and end apart: 9, of which 6 were waited for; matrix products, arithmetic and copies ran while one was open for 0% of the time, Pallas kernels for 3%

profile of v4, /device:TPU:1, one launch (start us, length us, event | category | flops | bytes accessed | tf_op | source)
XLA Modules:
  0.0 198.2 jit_solution(11031156766143791172)
XLA Ops:
  0.6 1.7 shard_map.126
  2.4 4.8 %collective-permute-start = (bf16[80,128]{1,0:T(8,128)(2,1)S(1)}, bf16[80,128]{1,0:T(8,128)(2,1)S(1)}, u32[]{:S(2)}, u32[]{:S(2)}) collective-permute-start(bf16[80,128]{1,0:T(8,128)(2,1)S(1)} %get-tuple-element.35), channel_id=1, source_target_pairs={{0,32},{32,64},{64,96},{96,128},{128,160},{160,192},{192,224},{224... | collective-permute-start | bytes 61448 | tf_op jit(solution)/shard_map/ppermute | solution.py:30
  7.2 1.3 collective-permute-start.1
  8.5 3.8 %collective-permute-done.1 = bf16[80,128]{1,0:T(8,128)(2,1)S(1)} collective-permute-done((bf16[80,128]{1,0:T(8,128)(2,1)S(1)}, bf16[80,128]{1,0:T(8,128)(2,1)S(1)}, u32[]{:S(2)}, u32[]{:S(2)}) %collective-permute-start.1) | collective-permute-done | bytes 20512 | tf_op jit(solution)/shard_map/ppermute | solution.py:31
  12.4 0.9 pad_maximum_fusion.2
  13.6 5.0 %collective-permute-start.3 = (bf16[354,128]{1,0:T(8,128)(2,1)S(1)}, bf16[354,128]{1,0:T(8,128)(2,1)S(1)}, u32[]{:S(2)}, u32[]{:S(2)}) collective-permute-start(bf16[354,128]{1,0:T(8,128)(2,1)S(1)} %pad_maximum_fusion.4), channel_id=1, source_target_pairs={{0,1},{1,2},{2,3},{3,4},{4,5},{5,6},{6,7},{7,8},{8,9},{9,10},{10,1... | collective-permute-start | bytes 271880 | tf_op jit(solution)/shard_map/ppermute | solution.py:30
  18.8 2.1 %collective-permute-start.2 = (bf16[354,128]{1,0:T(8,128)(2,1)S(1)}, bf16[354,128]{1,0:T(8,128)(2,1)S(1)}, u32[]{:S(2)}, u32[]{:S(2)}) collective-permute-start(bf16[354,128]{1,0:T(8,128)(2,1)S(1)} %pad_maximum_fusion.3), channel_id=1, source_target_pairs={{1,0},{2,1},{3,2},{4,3},{5,4},{6,5},{7,6},{8,7},{9,8},{10,9},{11,1... | collective-permute-start | bytes 271880 | tf_op jit(solution)/shard_map/ppermute | solution.py:31
  20.9 8.7 %all-to-all-start = ((f32[16,2,128]{2,1,0:T(2,128)}), f32[16,2,128]{2,1,0:T(2,128)S(1)}, u32[]{:S(2)}, u32[]{:S(2)}) async-start(f32[16,2,128]{2,1,0:T(2,128)} %get-tuple-element.37), calls=%async_computation | async-start | bytes 32768 | tf_op jit(solution)/shard_map/all_to_all | solution.py:478
  29.7 7.2 %all-to-all-done.received = f32[16,2,128]{2,1,0:T(2,128)S(1)} async-done(((f32[16,2,128]{2,1,0:T(2,128)}), f32[16,2,128]{2,1,0:T(2,128)S(1)}, u32[]{:S(2)}, u32[]{:S(2)}) %all-to-all-start) | async-done | bytes 16416 | tf_op jit(solution)/shard_map/all_to_all | solution.py:478
  37.6 12.3 %all-to-all-start.1 = ((f32[32,2,128]{2,1,0:T(2,128)}), f32[32,2,128]{2,1,0:T(2,128)S(1)}, u32[]{:S(2)}, u32[]{:S(2)}) async-start(f32[32,2,128]{2,1,0:T(2,128)} %shard_map.127), calls=%async_computation.1 | async-start | bytes 65536 | tf_op jit(solution)/shard_map/all_to_all | solution.py:482
  50.2 8.4 %all-to-all-done.1.sums = f32[32,2,128]{2,1,0:T(2,128)S(1)} async-done(((f32[32,2,128]{2,1,0:T(2,128)}), f32[32,2,128]{2,1,0:T(2,128)S(1)}, u32[]{:S(2)}, u32[]{:S(2)}) %all-to-all-start.1) | async-done | bytes 32800 | tf_op jit(solution)/shard_map/all_to_all | solution.py:482
  58.6 3.2 %shard_map.128 = (bf16[70,32,128]{2,1,0:T(8,128)(2,1)}, bf16[544,128]{1,0:T(8,128)(2,1)}, bf16[544,256]{1,0:T(8,128)(2,1)S(1)}, f32[16,4,128]{2,1,0:T(4,128)}, f32[2,8,128]{2,1,0:T(8,128)S(1)}) custom-call(s32[7]{0:T(128)S(1)} %stack.31.place, bf16[70,32,128]{2,1,0:T(8,128)(2,1)S(1)} %pad_maximum_fusion.x, f32[32,2,128]{2,1,0:T(2,128)S(1)} %all-to-all-done.1.sums, ...), custom_call_target="tpu_custom_call" | custom-call | tf_op jit(solution)/shard_map/pallas_call | solution.py:87
  61.8 5.1 %all-to-all-start.2 = ((f32[16,4,128]{2,1,0:T(4,128)}), f32[16,4,128]{2,1,0:T(4,128)S(1)}, u32[]{:S(2)}, u32[]{:S(2)}) async-start(f32[16,4,128]{2,1,0:T(4,128)} %get-tuple-element.38), calls=%async_computation.2 | async-start | bytes 65536 | tf_op jit(solution)/shard_map/all_to_all | solution.py:478
  67.0 7.4 %all-to-all-done.2.received = f32[16,4,128]{2,1,0:T(4,128)S(1)} async-done(((f32[16,4,128]{2,1,0:T(4,128)}), f32[16,4,128]{2,1,0:T(4,128)S(1)}, u32[]{:S(2)}, u32[]{:S(2)}) %all-to-all-start.2) | async-done | bytes 32800 | tf_op jit(solution)/shard_map/all_to_all | solution.py:478
  75.1 3.9 %all-to-all-start.3 = ((f32[32,4,128]{2,1,0:T(4,128)}), f32[32,4,128]{2,1,0:T(4,128)S(1)}, u32[]{:S(2)}, u32[]{:S(2)}) async-start(f32[32,4,128]{2,1,0:T(4,128)} %shard_map.129), calls=%async_computation.3 | async-start | bytes 131072 | tf_op jit(solution)/shard_map/all_to_all | solution.py:482
  79.2 2.8 %shard_map.130 = (f32[544,256]{1,0:T(8,128)S(1)}, bf16[3,384,128]{2,1,0:T(8,128)(2,1)}) custom-call(bf16[36,16,256]{2,1,0:T(8,128)(2,1)S(1)} %pad_maximum_fusion.1.grad, bf16[3,3,256,256]{3,2,1,0:T(8,128)(2,1)} %weight.1, bf16[9,128,128]{2,1,0:T(8,128)(2,1)} %bitcast.29), custom_call_target="tpu_custom_call" | custom-call | tf_op jit(solution)/shard_map/pallas_call | solution.py:87
  82.1 5.7 %all-to-all-done.3.sums = f32[32,4,128]{2,1,0:T(4,128)S(1)} async-done(((f32[32,4,128]{2,1,0:T(4,128)}), f32[32,4,128]{2,1,0:T(4,128)S(1)}, u32[]{:S(2)}, u32[]{:S(2)}) %all-to-all-start.3) | async-done | bytes 65568 | tf_op jit(solution)/shard_map/all_to_all | solution.py:482
  87.8 2.1 %shard_map.131 = (bf16[34,16,256]{2,1,0:T(8,128)(2,1)}, f32[544,256]{1,0:T(8,128)}, f32[16,4,128]{2,1,0:T(4,128)S(1)}, f32[2,8,256]{2,1,0:T(8,128)S(1)}) custom-call(s32[7]{0:T(128)S(1)} %stack.31.place, f32[32,4,128]{2,1,0:T(4,128)S(1)} %all-to-all-done.3.sums, bf16[544,256]{1,0:T(8,128)(2,1)S(1)} %get-tuple-element.40.coarse, ...), custom_call_target="tpu_custom_call" | custom-call | tf_op jit(solution)/shard_map/pallas_call | solution.py:87
  89.9 11.4 %all_to_all.60.received = f32[16,4,128]{2,1,0:T(4,128)S(1)} all-to-all(f32[16,4,128]{2,1,0:T(4,128)S(1)} %get-tuple-element.47), channel_id=1, replica_groups=mesh['gy_0'=2,'gy_1'=8,'gx_0'=2,'gx_1'=8,'gx_2'=2] {'gx_1','gx_2'}, dimensions={0} | all-to-all | bytes 65536 | tf_op jit(solution)/shard_map/all_to_all | solution.py:478
  102.0 3.9 %all-to-all-start.5 = ((f32[32,4,128]{2,1,0:T(4,128)}), f32[32,4,128]{2,1,0:T(4,128)S(1)}, u32[]{:S(2)}, u32[]{:S(2)}) async-start(f32[32,4,128]{2,1,0:T(4,128)} %shard_map.133), calls=%async_computation.5 | async-start | bytes 131072 | tf_op jit(solution)/shard_map/all_to_all | solution.py:482
  105.8 2.8 %shard_map.132 = (bf16[32,8,256]{2,1,0:T(8,128)(2,1)}, bf16[4608,128]{1,0:T(8,128)(2,1)S(1)}) custom-call(bf16[34,16,256]{2,1,0:T(8,128)(2,1)} %get-tuple-element.45.center, bf16[544,256]{1,0:T(8,128)(2,1)S(1)} %get-tuple-element.40.coarse, bf16[36,16,256]{2,1,0:T(8,128)(2,1)S(1)} %pad_maximum_fusion.1.grad, bf16[3,768,256]{2,1,0:T(8,128)(2,1)} %bitcast.36), custom_call_target="tpu_custom_call" | custom-call | tf_op jit(solution)/shard_map/pallas_call | solution.py:87
  108.6 6.1 %all-to-all-done.5.sums = f32[32,4,128]{2,1,0:T(4,128)S(1)} async-done(((f32[32,4,128]{2,1,0:T(4,128)}), f32[32,4,128]{2,1,0:T(4,128)S(1)}, u32[]{:S(2)}, u32[]{:S(2)}) %all-to-all-start.5) | async-done | bytes 65568 | tf_op jit(solution)/shard_map/all_to_all | solution.py:482
  114.7 4.0 %shard_map.134 = (bf16[6144,128]{1,0:T(8,128)(2,1)S(1)}, f32[1,256]{1,0:T(1,128)}, f32[64,16,128]{2,1,0:T(8,128)S(1)}) custom-call(s32[7]{0:T(128)S(1)} %stack.31.place, f32[32,4,128]{2,1,0:T(4,128)S(1)} %all-to-all-done.5.sums, bf16[544,256]{1,0:T(8,128)(2,1)S(1)} %get-tuple-element.40.coarse, bf16[544,128]{1,0:T(8,128)(2,1)} %get-tuple-element.48.pooled, ...), custom_call_target="tpu_custom_call" | custom-call | tf_op jit(solution)/shard_map/pallas_call | solution.py:87
  118.7 6.1 %all_to_all.61.pieces = bf16[2,3072,128]{2,1,0:T(8,128)(2,1)S(1)} all-to-all(bf16[2,3072,128]{2,1,0:T(8,128)(2,1)S(1)} %bitcast.28), channel_id=1, replica_groups=mesh['gy_0'=2,'gy_1'=8,'gx_0'=2,'gx_1'=8,'gx_2'=2] {'gx_2'}, dimensions={0} | all-to-all | bytes 3145728 | tf_op jit(solution)/shard_map/all_to_all | solution.py:521
  124.9 0.7 shard_map.135
  125.6 14.4 %all_to_all.62.pieces = bf16[4,768,128]{2,1,0:T(8,128)(2,1)S(1)} all-to-all(bf16[4,768,128]{2,1,0:T(8,128)(2,1)S(1)} %bitcast.27), channel_id=1, replica_groups=mesh['gy_0'=2,'gy_1'=8,'gx_0'=2,'gx_1'=8,'gx_2'=2] {'gx_0','gy_0'}, dimensions={0} | all-to-all | bytes 1572864 | tf_op jit(solution)/shard_map/all_to_all | solution.py:521
  140.0 0.7 shard_map.136
  140.7 16.2 %all_to_all.63.pieces = bf16[64,12,128]{2,1,0:T(8,128)(2,1)S(1)} all-to-all(bf16[64,12,128]{2,1,0:T(8,128)(2,1)S(1)} %shard_map.136), channel_id=1, replica_groups=mesh['gy_0'=2,'gy_1'=8,'gx_0'=2,'gx_1'=8,'gx_2'=2] {'gx_1','gy_1'}, dimensions={0} | all-to-all | bytes 393216 | tf_op jit(solution)/shard_map/all_to_all | solution.py:521
  157.6 18.2 %all_to_all.64 = bf16[64,12,128]{2,1,0:T(8,128)(2,1)S(1)} all-to-all(bf16[64,12,128]{2,1,0:T(8,128)(2,1)S(1)} %shard_map.137), channel_id=1, replica_groups=mesh['gy_0'=2,'gy_1'=8,'gx_0'=2,'gx_1'=8,'gx_2'=2] {'gx_1','gy_1'}, dimensions={0} | all-to-all | bytes 393216 | tf_op jit(solution)/shard_map/all_to_all | solution.py:537
  176.0 11.0 %all_to_all.65 = bf16[4,768,128]{2,1,0:T(8,128)(2,1)S(1)} all-to-all(bf16[4,768,128]{2,1,0:T(8,128)(2,1)S(1)} %broadcast_in_dim.23), channel_id=1, replica_groups=mesh['gy_0'=2,'gy_1'=8,'gx_0'=2,'gx_1'=8,'gx_2'=2] {'gx_0','gy_0'}, dimensions={0} | all-to-all | bytes 1572864 | tf_op jit(solution)/shard_map/all_to_all | solution.py:541
  187.1 9.2 %all_to_all.66 = bf16[2,3072,128]{2,1,0:T(8,128)(2,1)S(1)} all-to-all(bf16[2,3072,128]{2,1,0:T(8,128)(2,1)S(1)} %broadcast_in_dim.25), channel_id=1, replica_groups=mesh['gy_0'=2,'gy_1'=8,'gx_0'=2,'gx_1'=8,'gx_2'=2] {'gx_2'}, dimensions={0} | all-to-all | bytes 3145728 | tf_op jit(solution)/shard_map/all_to_all | solution.py:541
  196.4 1.8 shard_map.138
  (52 shorter events, 4.0 us)
Async XLA Ops:
  0.6 12.8 %copy-start.4 = (bf16[64,16,128]{2,1,0:T(8,128)(2,1)S(1)}, bf16[64,16,128]{2,1,0:T(8,128)(2,1)}, u32[]{:S(2)}) copy-start(bf16[64,16,128]{2,1,0:T(8,128)(2,1)} %field.1) | copy-start | bytes 786436
  2.4 6.1 %collective-permute-start = (bf16[80,128]{1,0:T(8,128)(2,1)S(1)}, bf16[80,128]{1,0:T(8,128)(2,1)S(1)}, u32[]{:S(2)}, u32[]{:S(2)}) collective-permute-start(bf16[80,128]{1,0:T(8,128)(2,1)S(1)} %get-tuple-element.35), channel_id=1, source_target_pairs={{0,32},{32,64},{64,96},{96,128},{128,160},{160,192},{192,224},{224... | collective-permute-start | bytes 61448 | tf_op jit(solution)/shard_map/ppermute | solution.py:30
  7.2 5.2 %collective-permute-start.1 = (bf16[80,128]{1,0:T(8,128)(2,1)S(1)}, bf16[80,128]{1,0:T(8,128)(2,1)S(1)}, u32[]{:S(2)}, u32[]{:S(2)}) collective-permute-start(bf16[80,128]{1,0:T(8,128)(2,1)S(1)} %get-tuple-element.36), channel_id=1, source_target_pairs={{32,0},{64,32},{96,64},{128,96},{160,128},{192,160},{224,192},{256... | collective-permute-start | bytes 61448 | tf_op jit(solution)/shard_map/ppermute | solution.py:31
  13.5 45.1 %copy-start = (bf16[3,3,128,128]{3,2,1,0:T(8,128)(2,1)S(1)}, bf16[3,3,128,128]{3,2,1,0:T(8,128)(2,1)}, u32[]{:S(2)}) copy-start(bf16[3,3,128,128]{3,2,1,0:T(8,128)(2,1)} %param.10) | copy-start | bytes 884740
  13.5 45.1 %copy-start.1 = (bf16[128,256]{1,0:T(8,128)(2,1)S(1)}, bf16[128,256]{1,0:T(8,128)(2,1)}, u32[]{:S(2)}) copy-start(bf16[128,256]{1,0:T(8,128)(2,1)} %projection.3) | copy-start | bytes 196612
  13.6 45.1 %copy-start.2 = (f32[128]{0:T(128)S(1)}, f32[128]{0:T(128)}, u32[]{:S(2)}) copy-start(f32[128]{0:T(128)} %param.9) | copy-start | bytes 1540
  13.6 36.3 %collective-permute-start.3 = (bf16[354,128]{1,0:T(8,128)(2,1)S(1)}, bf16[354,128]{1,0:T(8,128)(2,1)S(1)}, u32[]{:S(2)}, u32[]{:S(2)}) collective-permute-start(bf16[354,128]{1,0:T(8,128)(2,1)S(1)} %pad_maximum_fusion.4), channel_id=1, source_target_pairs={{0,1},{1,2},{2,3},{3,4},{4,5},{5,6},{6,7},{7,8},{8,9},{9,10},{10,1... | collective-permute-start | bytes 271880 | tf_op jit(solution)/shard_map/ppermute | solution.py:30
  18.8 31.1 %collective-permute-start.2 = (bf16[354,128]{1,0:T(8,128)(2,1)S(1)}, bf16[354,128]{1,0:T(8,128)(2,1)S(1)}, u32[]{:S(2)}, u32[]{:S(2)}) collective-permute-start(bf16[354,128]{1,0:T(8,128)(2,1)S(1)} %pad_maximum_fusion.3), channel_id=1, source_target_pairs={{1,0},{2,1},{3,2},{4,3},{5,4},{6,5},{7,6},{8,7},{9,8},{10,9},{11,1... | collective-permute-start | bytes 271880 | tf_op jit(solution)/shard_map/ppermute | solution.py:31
  20.9 16.0 %all-to-all-start = ((f32[16,2,128]{2,1,0:T(2,128)}), f32[16,2,128]{2,1,0:T(2,128)S(1)}, u32[]{:S(2)}, u32[]{:S(2)}) async-start(f32[16,2,128]{2,1,0:T(2,128)} %get-tuple-element.37), calls=%async_computation | async-start | bytes 32768 | tf_op jit(solution)/shard_map/all_to_all | solution.py:478
  37.6 21.1 %all-to-all-start.1 = ((f32[32,2,128]{2,1,0:T(2,128)}), f32[32,2,128]{2,1,0:T(2,128)S(1)}, u32[]{:S(2)}, u32[]{:S(2)}) async-start(f32[32,2,128]{2,1,0:T(2,128)} %shard_map.127), calls=%async_computation.1 | async-start | bytes 65536 | tf_op jit(solution)/shard_map/all_to_all | solution.py:482
  61.8 12.5 %all-to-all-start.2 = ((f32[16,4,128]{2,1,0:T(4,128)}), f32[16,4,128]{2,1,0:T(4,128)S(1)}, u32[]{:S(2)}, u32[]{:S(2)}) async-start(f32[16,4,128]{2,1,0:T(4,128)} %get-tuple-element.38), calls=%async_computation.2 | async-start | bytes 65536 | tf_op jit(solution)/shard_map/all_to_all | solution.py:478
  75.1 12.7 %all-to-all-start.3 = ((f32[32,4,128]{2,1,0:T(4,128)}), f32[32,4,128]{2,1,0:T(4,128)S(1)}, u32[]{:S(2)}, u32[]{:S(2)}) async-start(f32[32,4,128]{2,1,0:T(4,128)} %shard_map.129), calls=%async_computation.3 | async-start | bytes 131072 | tf_op jit(solution)/shard_map/all_to_all | solution.py:482
  79.0 8.7 %copy-start.3 = (f32[256]{0:T(256)S(1)}, f32[256]{0:T(256)}, u32[]{:S(2)}) copy-start(f32[256]{0:T(256)} %param.12) | copy-start | bytes 3076
  102.0 12.7 %all-to-all-start.5 = ((f32[32,4,128]{2,1,0:T(4,128)}), f32[32,4,128]{2,1,0:T(4,128)S(1)}, u32[]{:S(2)}, u32[]{:S(2)}) async-start(f32[32,4,128]{2,1,0:T(4,128)} %shard_map.133), calls=%async_computation.5 | async-start | bytes 131072 | tf_op jit(solution)/shard_map/all_to_all | solution.py:482

commit v5 on v4

--- a/solution.py
+++ b/solution.py
@@ -25,11 +25,17 @@
 COARSE_RIM = 2
 
 
-def swap(heads, tails, axis):
-    ends = lax.axis_size(axis) - 1
-    before = lax.ppermute(tails, axis, [(i, i + 1) for i in range(ends)])
-    after = lax.ppermute(heads, axis, [(i + 1, i) for i in range(ends)])
-    return before, after
+def is_even(axis):
+    return lax.axis_index(axis) % 2 == 0
+
+
+def swap(inner, outer, axis):
+    count = lax.axis_size(axis)
+    mate = lax.ppermute(inner, axis, [(i, i ^ 1) for i in range(count)])
+    pairs = [(i, i + 1) for i in range(1, count - 1, 2)]
+    other = lax.ppermute(outer, axis, pairs + [(j, i) for i, j in pairs])
+    even = is_even(axis)
+    return jnp.where(even, other, mate), jnp.where(even, mate, other)
 
 
 def joined(fine, coarse):
@@ -52,9 +58,9 @@
     return jnp.concatenate([own, right, jnp.zeros((rows, gap, channels), own.dtype), left], axis=1)
 
 
-def with_rims(fine, coarse, heads, tails):
+def with_rims(fine, coarse, inner, outer):
     shapes = (FINE_RIM,) + fine.shape[1:], (COARSE_RIM,) + coarse.shape[1:]
-    rims = swap(heads, tails, GY)
+    rims = swap(inner, outer, GY)
     (f0, c0), (f1, c1) = (parted(r, *shapes) for r in rims)
     fine = jnp.concatenate([f0, fine, f1])
     coarse = jnp.concatenate([c0, coarse, c1])
@@ -64,7 +70,9 @@
     )
     heads = joined(fine[:, :FINE_RIM], coarse[:, :COARSE_RIM])
     tails = joined(fine[:, -FINE_RIM:], coarse[:, -COARSE_RIM:])
-    rims = swap(heads, tails, GX)
+    even = is_even(GX)
+    inner, outer = jnp.where(even, tails, heads), jnp.where(even, heads, tails)
+    rims = swap(inner, outer, GX)
     f0, f1 = (parted(r, *shapes)[0] for r in rims)
     return ring(fine, f0, f1, PITCH), (coarse, rims, shapes)
 
@@ -148,9 +156,16 @@
     return at
 
 
-def field_sums(field, grad, copies, heads, tails):
-    slab(heads, slab(heads, 0, field[:FINE_RIM]), grad[:COARSE_RIM])
-    slab(tails, slab(tails, 0, field[field.shape[0] - FINE_RIM :]), grad[grad.shape[0] - COARSE_RIM :])
+def field_sums(field, grad, copies, inner, outer):
+    even = is_even(GY)
+    low, high = field.shape[0] - FINE_RIM, grad.shape[0] - COARSE_RIM
+
+    def write(heads, tails):
+        slab(heads, slab(heads, 0, field[:FINE_RIM]), grad[:COARSE_RIM])
+        slab(tails, slab(tails, 0, field[low:]), grad[high:])
+
+    pl.when(even)(lambda: write(outer, inner))
+    pl.when(jnp.logical_not(even))(lambda: write(inner, outer))
     first = jnp.zeros((8, LANES), jnp.float32)
     second = jnp.zeros((8, LANES), jnp.float32)
     for at in range(0, field.shape[0], 8):
@@ -562,7 +577,7 @@
     gain_f, gain_c = gain_fine.reshape(1, -1), gain_coarse.reshape(1, -1)
 
     slabs = FINE_RIM * width + COARSE_RIM * half_w * chan_coarse // LANES
-    copies, heads, tails = call(
+    copies, inner, outer = call(
         field_sums,
         [((near, 2, LANES), f32, None), ((slabs, LANES), bf16, None), ((slabs, LANES), bf16, None)],
         field,
@@ -570,7 +585,7 @@
         plain=(0, 1),
     )
     sums = gathered(copies)
-    x, (tall, rims, shapes) = with_rims(field, cotangent, heads, tails)
+    x, (tall, rims, shapes) = with_rims(field, cotangent, inner, outer)
     lines = half_h + 2
     cells = lines * PITCH // 2
     hidden_f, pooled, coarse, copies, stats_f = call(

time: 199 us -> 196 us (0.985)
  waiting for transfers between devices: 38.6 us -> 35.8 us
    ppermute x4, waiting for transfers between devices: 3.85 us -> 1.12 us  [the longest x2 1.11 us: swap(): mate = lax.ppermute(inner, axis, [(i, i ^ 1) for i in range(count)])]
    ppermute x4, starting transfers between devices: 13.3 us -> 16 us  [the longest x2 13.4 us: swap(): mate = lax.ppermute(inner, axis, [(i, i ^ 1) for i in range(count)])]
    all_to_all x2, starting transfers between devices: 13.8 us -> 11.5 us  [gathered(): received = lax.all_to_all(copies, NEAR, 0, 0, tiled=True)]
where the time goes in v5:
time: 196 us; the launch traced here: 195 us
  blocking collectives  86.7 us (44%)
  starting transfers between devices  46.8 us (24%)
  waiting for transfers between devices  35.8 us (18%)
  Pallas kernels  22.6 us (12%)
    all_to_all x3, blocking collectives, gradient_totals(): lax.all_to_all(part.reshape(count, -1, LANES), axes, 0, 0, tiled=True)  36.8 us
    pallas_call x13, Pallas kernels, call(): pl.pallas_call(body, out_shape=[(pltpu.VMEM if len(o) == 2 else o[2] or j...  22.6 us
    all_to_all x2, blocking collectives, gradient_totals(): part = lax.all_to_all(copies, axes, 0, 0, tiled=True).reshape(-1, LANES)  20.3 us
    all_to_all x3, waiting for transfers between devices, gathered(): sums = lax.all_to_all(copies, FAR, 0, 0, tiled=True)  20.1 us
    all_to_all x3, starting transfers between devices, gathered(): sums = lax.all_to_all(copies, FAR, 0, 0, tiled=True)  19.3 us
    all_to_all x1, blocking collectives, gradient_totals(): part = lax.all_to_all(part, STAGES[2], 0, 0, tiled=True).reshape(-1, LANES)  18.2 us
    all_to_all x2, waiting for transfers between devices, gathered(): received = lax.all_to_all(copies, NEAR, 0, 0, tiled=True)  14.6 us
    ppermute x2, starting transfers between devices, swap(): mate = lax.ppermute(inner, axis, [(i, i ^ 1) for i in range(count)])  13.4 us
  transfers between devices with their start and end apart: 9, of which 6 were waited for; matrix products, arithmetic and copies ran while one was open for 0% of the time, Pallas kernels for 3%

profile of v5, /device:TPU:1, one launch (start us, length us, event | category | flops | bytes accessed | tf_op | source)
XLA Modules:
  0.0 195.3 jit_solution(11706091522347337322)
XLA Ops:
  0.6 1.7 shard_map.126
  3.0 8.2 %collective-permute-start.1 = (bf16[80,128]{1,0:T(8,128)(2,1)S(1)}, bf16[80,128]{1,0:T(8,128)(2,1)S(1)}, u32[]{:S(2)}, u32[]{:S(2)}) collective-permute-start(bf16[80,128]{1,0:T(8,128)(2,1)S(1)} %get-tuple-element.36), channel_id=1, source_target_pairs={{0,32},{32,0},{64,96},{96,64},{128,160},{160,128},{192,224},{224,1... | collective-permute-start | bytes 61448 | tf_op jit(solution)/shard_map/ppermute | solution.py:34
  11.2 1.1 collective-permute-done.1
  12.4 0.9 pad_maximum_fusion.2
  13.8 5.2 %collective-permute-start.2 = (bf16[354,128]{1,0:T(8,128)(2,1)S(1)}, bf16[354,128]{1,0:T(8,128)(2,1)S(1)}, u32[]{:S(2)}, u32[]{:S(2)}) collective-permute-start(bf16[354,128]{1,0:T(8,128)(2,1)S(1)} %get-tuple-element.67), channel_id=1, source_target_pairs={{0,1},{1,0},{2,3},{3,2},{4,5},{5,4},{6,7},{7,6},{8,9},{9,8},{10,11... | collective-permute-start | bytes 271880 | tf_op jit(solution)/shard_map/ppermute | solution.py:34
  19.0 1.9 collective-permute-start.3
  20.9 6.4 %all-to-all-start = ((f32[16,2,128]{2,1,0:T(2,128)}), f32[16,2,128]{2,1,0:T(2,128)S(1)}, u32[]{:S(2)}, u32[]{:S(2)}) async-start(f32[16,2,128]{2,1,0:T(2,128)} %get-tuple-element.37), calls=%async_computation | async-start | bytes 32768 | tf_op jit(solution)/shard_map/all_to_all | solution.py:493
  27.5 7.2 %all-to-all-done.received = f32[16,2,128]{2,1,0:T(2,128)S(1)} async-done(((f32[16,2,128]{2,1,0:T(2,128)}), f32[16,2,128]{2,1,0:T(2,128)S(1)}, u32[]{:S(2)}, u32[]{:S(2)}) %all-to-all-start) | async-done | bytes 16416 | tf_op jit(solution)/shard_map/all_to_all | solution.py:493
  35.3 11.6 %all-to-all-start.1 = ((f32[32,2,128]{2,1,0:T(2,128)}), f32[32,2,128]{2,1,0:T(2,128)S(1)}, u32[]{:S(2)}, u32[]{:S(2)}) async-start(f32[32,2,128]{2,1,0:T(2,128)} %shard_map.127), calls=%async_computation.1 | async-start | bytes 65536 | tf_op jit(solution)/shard_map/all_to_all | solution.py:497
  47.3 8.4 %all-to-all-done.1.sums = f32[32,2,128]{2,1,0:T(2,128)S(1)} async-done(((f32[32,2,128]{2,1,0:T(2,128)}), f32[32,2,128]{2,1,0:T(2,128)S(1)}, u32[]{:S(2)}, u32[]{:S(2)}) %all-to-all-start.1) | async-done | bytes 32800 | tf_op jit(solution)/shard_map/all_to_all | solution.py:497
  55.7 3.2 %shard_map.128 = (bf16[70,32,128]{2,1,0:T(8,128)(2,1)}, bf16[544,128]{1,0:T(8,128)(2,1)}, bf16[544,256]{1,0:T(8,128)(2,1)S(1)}, f32[16,4,128]{2,1,0:T(4,128)}, f32[2,8,128]{2,1,0:T(8,128)S(1)}) custom-call(s32[7]{0:T(128)S(1)} %stack.31.place, bf16[70,32,128]{2,1,0:T(8,128)(2,1)S(1)} %pad_maximum_fusion.x, f32[32,2,128]{2,1,0:T(2,128)S(1)} %all-to-all-done.1.sums, ...), custom_call_target="tpu_custom_call" | custom-call | tf_op jit(solution)/shard_map/pallas_call | solution.py:95
  58.9 5.1 %all-to-all-start.2 = ((f32[16,4,128]{2,1,0:T(4,128)}), f32[16,4,128]{2,1,0:T(4,128)S(1)}, u32[]{:S(2)}, u32[]{:S(2)}) async-start(f32[16,4,128]{2,1,0:T(4,128)} %get-tuple-element.38), calls=%async_computation.2 | async-start | bytes 65536 | tf_op jit(solution)/shard_map/all_to_all | solution.py:493
  64.1 7.4 %all-to-all-done.2.received = f32[16,4,128]{2,1,0:T(4,128)S(1)} async-done(((f32[16,4,128]{2,1,0:T(4,128)}), f32[16,4,128]{2,1,0:T(4,128)S(1)}, u32[]{:S(2)}, u32[]{:S(2)}) %all-to-all-start.2) | async-done | bytes 32800 | tf_op jit(solution)/shard_map/all_to_all | solution.py:493
  72.1 3.9 %all-to-all-start.3 = ((f32[32,4,128]{2,1,0:T(4,128)}), f32[32,4,128]{2,1,0:T(4,128)S(1)}, u32[]{:S(2)}, u32[]{:S(2)}) async-start(f32[32,4,128]{2,1,0:T(4,128)} %shard_map.129), calls=%async_computation.3 | async-start | bytes 131072 | tf_op jit(solution)/shard_map/all_to_all | solution.py:497
  76.3 2.9 %shard_map.130 = (f32[544,256]{1,0:T(8,128)S(1)}, bf16[3,384,128]{2,1,0:T(8,128)(2,1)}) custom-call(bf16[36,16,256]{2,1,0:T(8,128)(2,1)S(1)} %pad_maximum_fusion.1.grad, bf16[3,3,256,256]{3,2,1,0:T(8,128)(2,1)} %weight.1, bf16[9,128,128]{2,1,0:T(8,128)(2,1)} %bitcast.29), custom_call_target="tpu_custom_call" | custom-call | tf_op jit(solution)/shard_map/pallas_call | solution.py:95
  79.2 5.7 %all-to-all-done.3.sums = f32[32,4,128]{2,1,0:T(4,128)S(1)} async-done(((f32[32,4,128]{2,1,0:T(4,128)}), f32[32,4,128]{2,1,0:T(4,128)S(1)}, u32[]{:S(2)}, u32[]{:S(2)}) %all-to-all-start.3) | async-done | bytes 65568 | tf_op jit(solution)/shard_map/all_to_all | solution.py:497
  84.9 2.1 %shard_map.131 = (bf16[34,16,256]{2,1,0:T(8,128)(2,1)}, f32[544,256]{1,0:T(8,128)}, f32[16,4,128]{2,1,0:T(4,128)S(1)}, f32[2,8,256]{2,1,0:T(8,128)S(1)}) custom-call(s32[7]{0:T(128)S(1)} %stack.31.place, f32[32,4,128]{2,1,0:T(4,128)S(1)} %all-to-all-done.3.sums, bf16[544,256]{1,0:T(8,128)(2,1)S(1)} %get-tuple-element.40.coarse, ...), custom_call_target="tpu_custom_call" | custom-call | tf_op jit(solution)/shard_map/pallas_call | solution.py:95
  87.0 11.4 %all_to_all.60.received = f32[16,4,128]{2,1,0:T(4,128)S(1)} all-to-all(f32[16,4,128]{2,1,0:T(4,128)S(1)} %get-tuple-element.47), channel_id=1, replica_groups=mesh['gy_0'=2,'gy_1'=8,'gx_0'=2,'gx_1'=8,'gx_2'=2] {'gx_1','gx_2'}, dimensions={0} | all-to-all | bytes 65536 | tf_op jit(solution)/shard_map/all_to_all | solution.py:493
  98.4 0.7 shard_map.133
  99.0 3.9 %all-to-all-start.5 = ((f32[32,4,128]{2,1,0:T(4,128)}), f32[32,4,128]{2,1,0:T(4,128)S(1)}, u32[]{:S(2)}, u32[]{:S(2)}) async-start(f32[32,4,128]{2,1,0:T(4,128)} %shard_map.133), calls=%async_computation.5 | async-start | bytes 131072 | tf_op jit(solution)/shard_map/all_to_all | solution.py:497
  102.9 2.8 %shard_map.132 = (bf16[32,8,256]{2,1,0:T(8,128)(2,1)}, bf16[4608,128]{1,0:T(8,128)(2,1)S(1)}) custom-call(bf16[34,16,256]{2,1,0:T(8,128)(2,1)} %get-tuple-element.45.center, bf16[544,256]{1,0:T(8,128)(2,1)S(1)} %get-tuple-element.40.coarse, bf16[36,16,256]{2,1,0:T(8,128)(2,1)S(1)} %pad_maximum_fusion.1.grad, bf16[3,768,256]{2,1,0:T(8,128)(2,1)} %bitcast.36), custom_call_target="tpu_custom_call" | custom-call | tf_op jit(solution)/shard_map/pallas_call | solution.py:95
  105.7 6.1 %all-to-all-done.5.sums = f32[32,4,128]{2,1,0:T(4,128)S(1)} async-done(((f32[32,4,128]{2,1,0:T(4,128)}), f32[32,4,128]{2,1,0:T(4,128)S(1)}, u32[]{:S(2)}, u32[]{:S(2)}) %all-to-all-start.5) | async-done | bytes 65568 | tf_op jit(solution)/shard_map/all_to_all | solution.py:497
  111.8 4.0 %shard_map.134 = (bf16[6144,128]{1,0:T(8,128)(2,1)S(1)}, f32[1,256]{1,0:T(1,128)}, f32[64,16,128]{2,1,0:T(8,128)S(1)}) custom-call(s32[7]{0:T(128)S(1)} %stack.31.place, f32[32,4,128]{2,1,0:T(4,128)S(1)} %all-to-all-done.5.sums, bf16[544,256]{1,0:T(8,128)(2,1)S(1)} %get-tuple-element.40.coarse, bf16[544,128]{1,0:T(8,128)(2,1)} %get-tuple-element.48.pooled, ...), custom_call_target="tpu_custom_call" | custom-call | tf_op jit(solution)/shard_map/pallas_call | solution.py:95
  115.8 6.1 %all_to_all.61.pieces = bf16[2,3072,128]{2,1,0:T(8,128)(2,1)S(1)} all-to-all(bf16[2,3072,128]{2,1,0:T(8,128)(2,1)S(1)} %bitcast.28), channel_id=1, replica_groups=mesh['gy_0'=2,'gy_1'=8,'gx_0'=2,'gx_1'=8,'gx_2'=2] {'gx_2'}, dimensions={0} | all-to-all | bytes 3145728 | tf_op jit(solution)/shard_map/all_to_all | solution.py:536
  122.0 0.7 shard_map.135
  122.7 14.4 %all_to_all.62.pieces = bf16[4,768,128]{2,1,0:T(8,128)(2,1)S(1)} all-to-all(bf16[4,768,128]{2,1,0:T(8,128)(2,1)S(1)} %bitcast.27), channel_id=1, replica_groups=mesh['gy_0'=2,'gy_1'=8,'gx_0'=2,'gx_1'=8,'gx_2'=2] {'gx_0','gy_0'}, dimensions={0} | all-to-all | bytes 1572864 | tf_op jit(solution)/shard_map/all_to_all | solution.py:536
  137.1 0.7 shard_map.136
  137.8 16.2 %all_to_all.63.pieces = bf16[64,12,128]{2,1,0:T(8,128)(2,1)S(1)} all-to-all(bf16[64,12,128]{2,1,0:T(8,128)(2,1)S(1)} %shard_map.136), channel_id=1, replica_groups=mesh['gy_0'=2,'gy_1'=8,'gx_0'=2,'gx_1'=8,'gx_2'=2] {'gx_1','gy_1'}, dimensions={0} | all-to-all | bytes 393216 | tf_op jit(solution)/shard_map/all_to_all | solution.py:536
  154.7 18.2 %all_to_all.64 = bf16[64,12,128]{2,1,0:T(8,128)(2,1)S(1)} all-to-all(bf16[64,12,128]{2,1,0:T(8,128)(2,1)S(1)} %shard_map.137), channel_id=1, replica_groups=mesh['gy_0'=2,'gy_1'=8,'gx_0'=2,'gx_1'=8,'gx_2'=2] {'gx_1','gy_1'}, dimensions={0} | all-to-all | bytes 393216 | tf_op jit(solution)/shard_map/all_to_all | solution.py:552
  173.1 11.0 %all_to_all.65 = bf16[4,768,128]{2,1,0:T(8,128)(2,1)S(1)} all-to-all(bf16[4,768,128]{2,1,0:T(8,128)(2,1)S(1)} %broadcast_in_dim.23), channel_id=1, replica_groups=mesh['gy_0'=2,'gy_1'=8,'gx_0'=2,'gx_1'=8,'gx_2'=2] {'gx_0','gy_0'}, dimensions={0} | all-to-all | bytes 1572864 | tf_op jit(solution)/shard_map/all_to_all | solution.py:556
  184.2 9.2 %all_to_all.66 = bf16[2,3072,128]{2,1,0:T(8,128)(2,1)S(1)} all-to-all(bf16[2,3072,128]{2,1,0:T(8,128)(2,1)S(1)} %broadcast_in_dim.25), channel_id=1, replica_groups=mesh['gy_0'=2,'gy_1'=8,'gx_0'=2,'gx_1'=8,'gx_2'=2] {'gx_2'}, dimensions={0} | all-to-all | bytes 3145728 | tf_op jit(solution)/shard_map/all_to_all | solution.py:556
  193.5 1.8 shard_map.138
  (53 shorter events, 4.1 us)
Async XLA Ops:
  0.6 12.8 %copy-start.4 = (bf16[64,16,128]{2,1,0:T(8,128)(2,1)S(1)}, bf16[64,16,128]{2,1,0:T(8,128)(2,1)}, u32[]{:S(2)}) copy-start(bf16[64,16,128]{2,1,0:T(8,128)(2,1)} %field.1) | copy-start | bytes 786436
  2.4 8.9 %collective-permute-start = (bf16[80,128]{1,0:T(8,128)(2,1)S(1)}, bf16[80,128]{1,0:T(8,128)(2,1)S(1)}, u32[]{:S(2)}, u32[]{:S(2)}) collective-permute-start(bf16[80,128]{1,0:T(8,128)(2,1)S(1)} %get-tuple-element.35), channel_id=1, source_target_pairs={{32,64},{96,128},{160,192},{224,256},{288,320},{352,384},{416,448}... | collective-permute-start | bytes 61448 | tf_op jit(solution)/shard_map/ppermute | solution.py:36
  3.0 9.3 %collective-permute-start.1 = (bf16[80,128]{1,0:T(8,128)(2,1)S(1)}, bf16[80,128]{1,0:T(8,128)(2,1)S(1)}, u32[]{:S(2)}, u32[]{:S(2)}) collective-permute-start(bf16[80,128]{1,0:T(8,128)(2,1)S(1)} %get-tuple-element.36), channel_id=1, source_target_pairs={{0,32},{32,0},{64,96},{96,64},{128,160},{160,128},{192,224},{224,1... | collective-permute-start | bytes 61448 | tf_op jit(solution)/shard_map/ppermute | solution.py:34
  13.7 42.1 %copy-start = (bf16[3,3,128,128]{3,2,1,0:T(8,128)(2,1)S(1)}, bf16[3,3,128,128]{3,2,1,0:T(8,128)(2,1)}, u32[]{:S(2)}) copy-start(bf16[3,3,128,128]{3,2,1,0:T(8,128)(2,1)} %param.10) | copy-start | bytes 884740
  13.7 42.0 %copy-start.1 = (bf16[128,256]{1,0:T(8,128)(2,1)S(1)}, bf16[128,256]{1,0:T(8,128)(2,1)}, u32[]{:S(2)}) copy-start(bf16[128,256]{1,0:T(8,128)(2,1)} %projection.3) | copy-start | bytes 196612
  13.7 42.0 %copy-start.2 = (f32[128]{0:T(128)S(1)}, f32[128]{0:T(128)}, u32[]{:S(2)}) copy-start(f32[128]{0:T(128)} %param.9) | copy-start | bytes 1540
  13.8 33.2 %collective-permute-start.2 = (bf16[354,128]{1,0:T(8,128)(2,1)S(1)}, bf16[354,128]{1,0:T(8,128)(2,1)S(1)}, u32[]{:S(2)}, u32[]{:S(2)}) collective-permute-start(bf16[354,128]{1,0:T(8,128)(2,1)S(1)} %get-tuple-element.67), channel_id=1, source_target_pairs={{0,1},{1,0},{2,3},{3,2},{4,5},{5,4},{6,7},{7,6},{8,9},{9,8},{10,11... | collective-permute-start | bytes 271880 | tf_op jit(solution)/shard_map/ppermute | solution.py:34
  19.0 28.0 %collective-permute-start.3 = (bf16[354,128]{1,0:T(8,128)(2,1)S(1)}, bf16[354,128]{1,0:T(8,128)(2,1)S(1)}, u32[]{:S(2)}, u32[]{:S(2)}) collective-permute-start(bf16[354,128]{1,0:T(8,128)(2,1)S(1)} %get-tuple-element.68), channel_id=1, source_target_pairs={{1,2},{3,4},{5,6},{7,8},{9,10},{11,12},{13,14},{15,16},{17,18},{19... | collective-permute-start | bytes 271880 | tf_op jit(solution)/shard_map/ppermute | solution.py:36
  20.9 13.8 %all-to-all-start = ((f32[16,2,128]{2,1,0:T(2,128)}), f32[16,2,128]{2,1,0:T(2,128)S(1)}, u32[]{:S(2)}, u32[]{:S(2)}) async-start(f32[16,2,128]{2,1,0:T(2,128)} %get-tuple-element.37), calls=%async_computation | async-start | bytes 32768 | tf_op jit(solution)/shard_map/all_to_all | solution.py:493
  35.3 20.4 %all-to-all-start.1 = ((f32[32,2,128]{2,1,0:T(2,128)}), f32[32,2,128]{2,1,0:T(2,128)S(1)}, u32[]{:S(2)}, u32[]{:S(2)}) async-start(f32[32,2,128]{2,1,0:T(2,128)} %shard_map.127), calls=%async_computation.1 | async-start | bytes 65536 | tf_op jit(solution)/shard_map/all_to_all | solution.py:497
  58.9 12.5 %all-to-all-start.2 = ((f32[16,4,128]{2,1,0:T(4,128)}), f32[16,4,128]{2,1,0:T(4,128)S(1)}, u32[]{:S(2)}, u32[]{:S(2)}) async-start(f32[16,4,128]{2,1,0:T(4,128)} %get-tuple-element.38), calls=%async_computation.2 | async-start | bytes 65536 | tf_op jit(solution)/shard_map/all_to_all | solution.py:493
  72.1 12.7 %all-to-all-start.3 = ((f32[32,4,128]{2,1,0:T(4,128)}), f32[32,4,128]{2,1,0:T(4,128)S(1)}, u32[]{:S(2)}, u32[]{:S(2)}) async-start(f32[32,4,128]{2,1,0:T(4,128)} %shard_map.129), calls=%async_computation.3 | async-start | bytes 131072 | tf_op jit(solution)/shard_map/all_to_all | solution.py:497
  76.1 8.7 %copy-start.3 = (f32[256]{0:T(256)S(1)}, f32[256]{0:T(256)}, u32[]{:S(2)}) copy-start(f32[256]{0:T(256)} %param.12) | copy-start | bytes 3076
  99.0 12.7 %all-to-all-start.5 = ((f32[32,4,128]{2,1,0:T(4,128)}), f32[32,4,128]{2,1,0:T(4,128)S(1)}, u32[]{:S(2)}, u32[]{:S(2)}) async-start(f32[32,4,128]{2,1,0:T(4,128)} %shard_map.133), calls=%async_computation.5 | async-start | bytes 131072 | tf_op jit(solution)/shard_map/all_to_all | solution.py:497

commit v6 on v5

--- a/solution.py
+++ b/solution.py
@@ -11,11 +11,12 @@
 
 GROUPS = 32
 GY = ("gy_0", "gy_1")
-GX = ("gx_0", "gx_1", "gx_2")
+CORE = "gx_3"
+GX = ("gx_0", "gx_1", "gx_2", CORE)
 GY_GX = GY + GX
-NEAR = ("gx_1", "gx_2")
+NEAR = ("gx_1", "gx_2", CORE)
 FAR = ("gx_0", "gy_0", "gy_1")
-STAGES = (("gx_2",), ("gx_0", "gy_0"), ("gx_1", "gy_1"))
+STAGES = ((CORE,), ("gx_0", "gy_0", "gx_2"), ("gx_1", "gy_1"))
 LANES = 128
 EPSILON = 1e-05
 
@@ -349,7 +350,7 @@
 
 def fine_backward(coarse_count, rows, cols, place, sums, coarse, pooled, grad, dnorm, stats_c,
                   gain_c, projection, weight_t, x, hidden, stats_f, gain_f, rows_in,
-                  rows_out, gain_c_grad, partial, up, shifted, taps):
+                  keep, send, gain_c_grad, partial, rows_out, up, shifted, taps):
     rows_out[0 : rows_in.shape[0]] = rows_in[...]
     tot = jnp.sum(sums[...], axis=0)
     first = jnp.concatenate([tot[0:1], tot[1:2]], axis=1)
@@ -457,12 +458,36 @@
     rows_out[at:] = jnp.concatenate(
         [jnp.zeros((spare - 8, LANES), jnp.float32), split(small)], axis=0
     ).astype(jnp.bfloat16)
-
-
-def finish(fine_count, rows, partial, x, stats, gain,
+    half = keep.shape[0]
+
+    def part(first, last):
+        first[...] = rows_out[:half]
+        last[...] = rows_out[half:]
+
+    core = lax.axis_index(CORE)
+    pl.when(core == 0)(lambda: part(keep, send))
+    pl.when(core == 1)(lambda: part(send, keep))
+
+
+def spread_rows(low, high, at, out, lane):
+    half, count = low.shape[0], out.shape[0]
+    split_at = min(max(half - at, 0), count)
+    lanes = slice(lane, lane + LANES)
+    if split_at > 0:
+        out[:split_at, lanes] = low[at : at + split_at].astype(jnp.float32)
+    if split_at < count:
+        begin = at + split_at - half
+        out[split_at:, lanes] = high[begin : begin + count - split_at].astype(jnp.float32)
+    return at + count
+
+
+def finish(fine_count, own, other, partial, x, stats, gain,
            field_grad, weight_f, gain_f, proj, weight_c):
-    count = rows.shape[0]
-    small = rows[count - 8 :].astype(jnp.float32)
+    core = lax.axis_index(CORE)
+    last = own.shape[0] - 8
+    small = jnp.where(
+        core == 1, own[last:].astype(jnp.float32), other[last:].astype(jnp.float32)
+    )
     small = small[0:2] + small[2:4] + small[4:6]
     first, second = small[0:1], small[1:2]
     gain_f[...] = second
@@ -478,14 +503,16 @@
         field_grad[at : at + step] = (
             partial[at : at + step] - inverse * (a_sum + normed * b_sum)
         ).astype(jnp.bfloat16)
-    tall = weight_c.shape[0]
-    weight_c[:, :LANES] = rows[0:tall].astype(jnp.float32)
-    weight_c[:, LANES:] = rows[tall : 2 * tall].astype(jnp.float32)
-    at = 2 * tall
-    weight_f[...] = rows[at : at + weight_f.shape[0]].astype(jnp.float32)
-    at += weight_f.shape[0]
-    proj[:, :LANES] = rows[at : at + LANES].astype(jnp.float32)
-    proj[:, LANES:] = rows[at + LANES : at + 2 * LANES].astype(jnp.float32)
+
+    def weights(low, high):
+        at = spread_rows(low, high, 0, weight_c, 0)
+        at = spread_rows(low, high, at, weight_c, LANES)
+        at = spread_rows(low, high, at, weight_f, 0)
+        at = spread_rows(low, high, at, proj, 0)
+        spread_rows(low, high, at, proj, LANES)
+
+    pl.when(core == 0)(lambda: weights(own, other))
+    pl.when(core == 1)(lambda: weights(other, own))
 
 
 def gathered(copies, late=None):
@@ -505,14 +532,19 @@
     return jnp.concatenate([high, middle, low, jnp.zeros_like(low)], axis=0)
 
 
-def add_up(stage, place, pieces, out, *scratch):
-    rows = pieces.shape[1]
+def add_up(stage, place, *refs):
+    if stage == 0:
+        pieces, (out,), scratch = refs[:2], refs[2:], ()
+    else:
+        pieces = [refs[0].at[k] for k in range(refs[0].shape[0])]
+        out, scratch = refs[1], refs[2:]
+    rows = pieces[0].shape[0]
     step = 256 if rows % 256 == 0 else rows
     pitch = out.shape[-2]
     for at in range(0, rows, step):
-        sums = pieces[0, at : at + step].astype(jnp.float32)
-        for k in range(1, pieces.shape[0]):
-            sums = sums + pieces[k, at : at + step].astype(jnp.float32)
+        sums = pieces[0][at : at + step].astype(jnp.float32)
+        for piece in pieces[1:]:
+            sums = sums + piece[at : at + step].astype(jnp.float32)
         if at + step == rows:
             last = sums[step - 8 :]
             tail = split(last[0:2] + last[2:4] + last[4:6])
@@ -530,15 +562,21 @@
             out[k] = scratch[0][k * pitch : (k + 1) * pitch].astype(jnp.bfloat16)
 
 
-def gradient_totals(part, place):
-    for stage, axes in enumerate(STAGES):
+def traded(rows):
+    return lax.ppermute(rows, CORE, [(0, 1), (1, 0)])
+
+
+def gradient_totals(keep, send, place):
+    rows = keep.shape[0]
+    (part,) = call(
+        functools.partial(add_up, 0), [((rows, LANES), jnp.bfloat16, None)], place, keep, traded(send)
+    )
+    for stage, axes in list(enumerate(STAGES))[1:]:
         count = lax.axis_size(axes)
         pieces = lax.all_to_all(part.reshape(count, -1, LANES), axes, 0, 0, tiled=True)
         rows = pieces.shape[1]
         kernel = functools.partial(add_up, stage)
-        if stage == 0:
-            (part,) = call(kernel, [((rows, LANES), jnp.bfloat16, None)], place, pieces)
-        elif stage == 1:
+        if stage == 1:
             pitch = rows // lax.axis_size(STAGES[2])
             (part,) = call(
                 kernel,
@@ -550,11 +588,10 @@
         else:
             (part,) = call(kernel, [((count, rows, LANES), jnp.bfloat16, None)], place, pieces)
     part = lax.all_to_all(part, STAGES[2], 0, 0, tiled=True).reshape(-1, LANES)
-    for axes in STAGES[1::-1]:
-        count = lax.axis_size(axes)
-        copies = jnp.broadcast_to(part[None], (count,) + part.shape)
-        part = lax.all_to_all(copies, axes, 0, 0, tiled=True).reshape(-1, LANES)
-    return part
+    count = lax.axis_size(STAGES[1])
+    copies = jnp.broadcast_to(part[None], (count,) + part.shape)
+    part = lax.all_to_all(copies, STAGES[1], 0, 0, tiled=True).reshape(-1, LANES)
+    return part, traded(part)
 
 
 def on_device(field, cotangent, gain_fine, weight_fine, projection, gain_coarse, weight_coarse):
@@ -646,10 +683,11 @@
         scratch=[((lines, PITCH // 2, 3 * chan_coarse), bf16)],
         plain=(0, 3),
     )
-    parts, coarse_gain_grad, partial = call(
+    keep, send, coarse_gain_grad, partial = call(
         functools.partial(fine_backward, coarse_count, rows // 2, cols // 2),
         [
-            ((used, LANES), bf16, None),
+            ((used // 2, LANES), bf16),
+            ((used // 2, LANES), bf16, None),
             ((1, chan_coarse), f32, None),
             ((height, width, chan_fine), f32),
         ],
@@ -669,13 +707,14 @@
         gain_f,
         parts,
         scratch=[
+            ((used, LANES), bf16),
             ((lines * PITCH + 8, chan_fine), f32),
             ((lines, PITCH, 3 * chan_fine), bf16),
             ((3, lines, PITCH // 2, chan_fine), f32),
         ],
         plain=(3, 5, 8, 9, 11),
     )
-    totals = gradient_totals(parts, place)
+    own, other = gradient_totals(keep, send, place)
     field_grad, fine_weight_grad, fine_gain_grad, projection_grad, coarse_weight_grad = call(
         functools.partial(finish, fine_count),
         [
@@ -685,7 +724,8 @@
             ((chan_fine, chan_coarse), f32, None),
             ((9 * chan_coarse, chan_coarse), f32, None),
         ],
-        totals,
+        own,
+        other,
         partial,
         x,
         stats_f,
@@ -703,7 +743,7 @@
 
 
 def solution(mesh):
-    finer = Mesh(mesh.devices.reshape(2, 8, 2, 8, 2), GY_GX)
+    finer = Mesh(mesh.devices.reshape(2, 8, 2, 4, 2, 2), GY_GX)
     in_specs = (P(GY, GX, None), P(GY, GX, None), P(), P(), P(), P(), P())
     out_specs = (P(GY, GX, None), P(GY, GX, None), P(), P(), P(), P(), P())
 

time: 196 us -> 191 us (0.974)
  blocking collectives: 86.7 us -> 67 us
  starting transfers between devices: 46.8 us -> 56.9 us
  waiting for transfers between devices: 35.8 us -> 39.6 us
    ppermute x0 -> x2, starting transfers between devices: none -> 10.1 us  [traded(): return lax.ppermute(rows, CORE, [(0, 1), (1, 0)])]
    all_to_all x2 -> x1, blocking collectives: 20.3 us -> 11.5 us  [gradient_totals(): lax.all_to_all(copies, STAGES[1], 0, 0, tiled=True).reshape(-1, LANES)]
    all_to_all x3 -> x2, blocking collectives: 36.8 us -> 29.5 us  [gradient_totals(): lax.all_to_all(part.reshape(count, -1, LANES), axes, 0, 0, tiled=True)]
    ppermute x0 -> x2, waiting for transfers between devices: none -> 3.78 us  [traded(): return lax.ppermute(rows, CORE, [(0, 1), (1, 0)])]
    all_to_all x1, blocking collectives: 18.2 us -> 14.6 us  [gradient_totals(): part = lax.all_to_all(part, STAGES[2], 0, 0, tiled=True).reshape(-1, LANES)]
  transfers between devices with their start and end apart: 9 -> 11, of which waited for: 6 -> 8; matrix products, arithmetic and copies ran while one was open for 0% -> 0% of each run, Pallas kernels for 3% -> 3%
where the time goes in v6:
time: 191 us; the launch traced here: 190 us
  blocking collectives  67 us (35%)
  starting transfers between devices  56.9 us (30%)
  waiting for transfers between devices  39.6 us (21%)
  Pallas kernels  23.1 us (12%)
    all_to_all x2, blocking collectives, gradient_totals(): lax.all_to_all(part.reshape(count, -1, LANES), axes, 0, 0, tiled=True)  29.5 us
    pallas_call x13, Pallas kernels, call(): pl.pallas_call(body, out_shape=[(pltpu.VMEM if len(o) == 2 else o[2] or j...  23.1 us
    all_to_all x3, waiting for transfers between devices, gathered(): sums = lax.all_to_all(copies, FAR, 0, 0, tiled=True)  20.1 us
    all_to_all x3, starting transfers between devices, gathered(): sums = lax.all_to_all(copies, FAR, 0, 0, tiled=True)  19.3 us
    all_to_all x1, blocking collectives, gradient_totals(): part = lax.all_to_all(part, STAGES[2], 0, 0, tiled=True).reshape(-1, LANES)  14.6 us
    all_to_all x2, waiting for transfers between devices, gathered(): received = lax.all_to_all(copies, NEAR, 0, 0, tiled=True)  14.6 us
    ppermute x2, starting transfers between devices, swap(): mate = lax.ppermute(inner, axis, [(i, i ^ 1) for i in range(count)])  13.4 us
    all_to_all x2, starting transfers between devices, gathered(): received = lax.all_to_all(copies, NEAR, 0, 0, tiled=True)  11.5 us
  transfers between devices with their start and end apart: 11, of which 8 were waited for; matrix products, arithmetic and copies ran while one was open for 0% of the time, Pallas kernels for 3%

profile of v6, /device:TPU:1, one launch (start us, length us, event | category | flops | bytes accessed | tf_op | source)
XLA Modules:
  0.0 189.8 jit_solution(2247331045703031144)
XLA Ops:
  0.6 1.7 shard_map.126
  3.0 8.2 %collective-permute-start.1 = (bf16[80,128]{1,0:T(8,128)(2,1)S(1)}, bf16[80,128]{1,0:T(8,128)(2,1)S(1)}, u32[]{:S(2)}, u32[]{:S(2)}) collective-permute-start(bf16[80,128]{1,0:T(8,128)(2,1)S(1)} %get-tuple-element.37), channel_id=1, source_target_pairs={{0,32},{32,0},{64,96},{96,64},{128,160},{160,128},{192,224},{224,1... | collective-permute-start | bytes 61448 | tf_op jit(solution)/shard_map/ppermute | solution.py:35
  11.2 1.1 collective-permute-done.1
  12.4 0.9 pad_maximum_fusion.2
  13.8 5.2 %collective-permute-start.2 = (bf16[354,128]{1,0:T(8,128)(2,1)S(1)}, bf16[354,128]{1,0:T(8,128)(2,1)S(1)}, u32[]{:S(2)}, u32[]{:S(2)}) collective-permute-start(bf16[354,128]{1,0:T(8,128)(2,1)S(1)} %get-tuple-element.69), channel_id=1, source_target_pairs={{0,1},{1,0},{2,3},{3,2},{4,5},{5,4},{6,7},{7,6},{8,9},{9,8},{10,11... | collective-permute-start | bytes 271880 | tf_op jit(solution)/shard_map/ppermute | solution.py:35
  19.0 1.9 %collective-permute-start.3 = (bf16[354,128]{1,0:T(8,128)(2,1)S(1)}, bf16[354,128]{1,0:T(8,128)(2,1)S(1)}, u32[]{:S(2)}, u32[]{:S(2)}) collective-permute-start(bf16[354,128]{1,0:T(8,128)(2,1)S(1)} %get-tuple-element.70), channel_id=1, source_target_pairs={{1,2},{3,4},{5,6},{7,8},{9,10},{11,12},{13,14},{15,16},{17,18},{19... | collective-permute-start | bytes 271880 | tf_op jit(solution)/shard_map/ppermute | solution.py:37
  20.9 6.4 %all-to-all-start = ((f32[16,2,128]{2,1,0:T(2,128)}), f32[16,2,128]{2,1,0:T(2,128)S(1)}, u32[]{:S(2)}, u32[]{:S(2)}) async-start(f32[16,2,128]{2,1,0:T(2,128)} %get-tuple-element.38), calls=%async_computation | async-start | bytes 32768 | tf_op jit(solution)/shard_map/all_to_all | solution.py:520
  27.5 7.2 %all-to-all-done.received = f32[16,2,128]{2,1,0:T(2,128)S(1)} async-done(((f32[16,2,128]{2,1,0:T(2,128)}), f32[16,2,128]{2,1,0:T(2,128)S(1)}, u32[]{:S(2)}, u32[]{:S(2)}) %all-to-all-start) | async-done | bytes 16416 | tf_op jit(solution)/shard_map/all_to_all | solution.py:520
  35.3 11.6 %all-to-all-start.1 = ((f32[32,2,128]{2,1,0:T(2,128)}), f32[32,2,128]{2,1,0:T(2,128)S(1)}, u32[]{:S(2)}, u32[]{:S(2)}) async-start(f32[32,2,128]{2,1,0:T(2,128)} %shard_map.127), calls=%async_computation.1 | async-start | bytes 65536 | tf_op jit(solution)/shard_map/all_to_all | solution.py:524
  47.3 8.4 %all-to-all-done.1.sums = f32[32,2,128]{2,1,0:T(2,128)S(1)} async-done(((f32[32,2,128]{2,1,0:T(2,128)}), f32[32,2,128]{2,1,0:T(2,128)S(1)}, u32[]{:S(2)}, u32[]{:S(2)}) %all-to-all-start.1) | async-done | bytes 32800 | tf_op jit(solution)/shard_map/all_to_all | solution.py:524
  55.7 3.2 %shard_map.128 = (bf16[70,32,128]{2,1,0:T(8,128)(2,1)}, bf16[544,128]{1,0:T(8,128)(2,1)}, bf16[544,256]{1,0:T(8,128)(2,1)S(1)}, f32[16,4,128]{2,1,0:T(4,128)}, f32[2,8,128]{2,1,0:T(8,128)S(1)}) custom-call(s32[7]{0:T(128)S(1)} %stack.31.place, bf16[70,32,128]{2,1,0:T(8,128)(2,1)S(1)} %pad_maximum_fusion.x, f32[32,2,128]{2,1,0:T(2,128)S(1)} %all-to-all-done.1.sums, ...), custom_call_target="tpu_custom_call" | custom-call | tf_op jit(solution)/shard_map/pallas_call | solution.py:96
  58.9 5.1 %all-to-all-start.2 = ((f32[16,4,128]{2,1,0:T(4,128)}), f32[16,4,128]{2,1,0:T(4,128)S(1)}, u32[]{:S(2)}, u32[]{:S(2)}) async-start(f32[16,4,128]{2,1,0:T(4,128)} %get-tuple-element.39), calls=%async_computation.2 | async-start | bytes 65536 | tf_op jit(solution)/shard_map/all_to_all | solution.py:520
  64.1 7.4 %all-to-all-done.2.received = f32[16,4,128]{2,1,0:T(4,128)S(1)} async-done(((f32[16,4,128]{2,1,0:T(4,128)}), f32[16,4,128]{2,1,0:T(4,128)S(1)}, u32[]{:S(2)}, u32[]{:S(2)}) %all-to-all-start.2) | async-done | bytes 32800 | tf_op jit(solution)/shard_map/all_to_all | solution.py:520
  72.1 3.9 %all-to-all-start.3 = ((f32[32,4,128]{2,1,0:T(4,128)}), f32[32,4,128]{2,1,0:T(4,128)S(1)}, u32[]{:S(2)}, u32[]{:S(2)}) async-start(f32[32,4,128]{2,1,0:T(4,128)} %shard_map.129), calls=%async_computation.3 | async-start | bytes 131072 | tf_op jit(solution)/shard_map/all_to_all | solution.py:524
  76.3 2.8 %shard_map.130 = (f32[544,256]{1,0:T(8,128)S(1)}, bf16[3,384,128]{2,1,0:T(8,128)(2,1)}) custom-call(bf16[36,16,256]{2,1,0:T(8,128)(2,1)S(1)} %pad_maximum_fusion.1.grad, bf16[3,3,256,256]{3,2,1,0:T(8,128)(2,1)} %weight.1, bf16[9,128,128]{2,1,0:T(8,128)(2,1)} %bitcast.27), custom_call_target="tpu_custom_call" | custom-call | tf_op jit(solution)/shard_map/pallas_call | solution.py:96
  79.2 5.7 %all-to-all-done.3.sums = f32[32,4,128]{2,1,0:T(4,128)S(1)} async-done(((f32[32,4,128]{2,1,0:T(4,128)}), f32[32,4,128]{2,1,0:T(4,128)S(1)}, u32[]{:S(2)}, u32[]{:S(2)}) %all-to-all-start.3) | async-done | bytes 65568 | tf_op jit(solution)/shard_map/all_to_all | solution.py:524
  84.9 2.1 %shard_map.131 = (bf16[34,16,256]{2,1,0:T(8,128)(2,1)}, f32[544,256]{1,0:T(8,128)}, f32[16,4,128]{2,1,0:T(4,128)S(1)}, f32[2,8,256]{2,1,0:T(8,128)S(1)}) custom-call(s32[7]{0:T(128)S(1)} %stack.31.place, f32[32,4,128]{2,1,0:T(4,128)S(1)} %all-to-all-done.3.sums, bf16[544,256]{1,0:T(8,128)(2,1)S(1)} %get-tuple-element.41.coarse, ...), custom_call_target="tpu_custom_call" | custom-call | tf_op jit(solution)/shard_map/pallas_call | solution.py:96
  87.0 11.4 %all_to_all.50.received = f32[16,4,128]{2,1,0:T(4,128)S(1)} all-to-all(f32[16,4,128]{2,1,0:T(4,128)S(1)} %get-tuple-element.48), channel_id=1, replica_groups=mesh['gy_0'=2,'gy_1'=8,'gx_0'=2,'gx_1'=4,'gx_2'=2,'gx_3'=2] {'gx_1','gx_..., dimensions={0} | all-to-all | bytes 65536 | tf_op jit(solution)/shard_map/all_to_all | solution.py:520
  99.1 3.9 %all-to-all-start.5 = ((f32[32,4,128]{2,1,0:T(4,128)}), f32[32,4,128]{2,1,0:T(4,128)S(1)}, u32[]{:S(2)}, u32[]{:S(2)}) async-start(f32[32,4,128]{2,1,0:T(4,128)} %shard_map.133), calls=%async_computation.5 | async-start | bytes 131072 | tf_op jit(solution)/shard_map/all_to_all | solution.py:524
  102.9 2.8 %shard_map.132 = (bf16[32,8,256]{2,1,0:T(8,128)(2,1)}, bf16[4608,128]{1,0:T(8,128)(2,1)S(1)}) custom-call(bf16[34,16,256]{2,1,0:T(8,128)(2,1)} %get-tuple-element.46.center, bf16[544,256]{1,0:T(8,128)(2,1)S(1)} %get-tuple-element.41.coarse, bf16[36,16,256]{2,1,0:T(8,128)(2,1)S(1)} %pad_maximum_fusion.1.grad, bf16[3,768,256]{2,1,0:T(8,128)(2,1)} %bitcast.34), custom_call_target="tpu_custom_call" | custom-call | tf_op jit(solution)/shard_map/pallas_call | solution.py:96
  105.7 6.1 %all-to-all-done.5.sums = f32[32,4,128]{2,1,0:T(4,128)S(1)} async-done(((f32[32,4,128]{2,1,0:T(4,128)}), f32[32,4,128]{2,1,0:T(4,128)S(1)}, u32[]{:S(2)}, u32[]{:S(2)}) %all-to-all-start.5) | async-done | bytes 65568 | tf_op jit(solution)/shard_map/all_to_all | solution.py:524
  111.8 4.2 %shard_map.134 = (bf16[3072,128]{1,0:T(8,128)(2,1)S(1)}, bf16[3072,128]{1,0:T(8,128)(2,1)S(1)}, f32[1,256]{1,0:T(1,128)}, f32[64,16,128]{2,1,0:T(8,128)S(1)}) custom-call(s32[7]{0:T(128)S(1)} %stack.31.place, f32[32,4,128]{2,1,0:T(4,128)S(1)} %all-to-all-done.5.sums, bf16[544,256]{1,0:T(8,128)(2,1)S(1)} %get-tuple-element.41.coarse, ...), custom_call_target="tpu_custom_call" | custom-call | tf_op jit(solution)/shard_map/pallas_call | solution.py:96
  116.0 3.4 %collective-permute-start.4 = (bf16[3072,128]{1,0:T(8,128)(2,1)S(1)}, bf16[3072,128]{1,0:T(8,128)(2,1)S(1)}, u32[]{:S(2)}, u32[]{:S(2)}) collective-permute-start(bf16[3072,128]{1,0:T(8,128)(2,1)S(1)} %get-tuple-element.57), channel_id=1, source_target_pairs={{0,1},{1,0},{2,3},{3,2},{4,5},{5,4},{6,7},{7,6},{8,9},{9,8},{10,11... | collective-permute-start | bytes 2359304 | tf_op jit(solution)/shard_map/ppermute | solution.py:566
  119.4 1.9 collective-permute-done.4.refs_1_
  121.3 0.7 shard_map.135
  122.0 15.0 %all_to_all.51.refs_0_ = bf16[8,384,128]{2,1,0:T(8,128)(2,1)S(1)} all-to-all(bf16[8,384,128]{2,1,0:T(8,128)(2,1)S(1)} %bitcast.24), channel_id=1, replica_groups=mesh['gy_0'=2,'gy_1'=8,'gx_0'=2,'gx_1'=4,'gx_2'=2,'gx_3'=2] {'gx_0','gy_..., dimensions={0} | all-to-all | bytes 1572864 | tf_op jit(solution)/shard_map/all_to_all | solution.py:576
  137.8 14.5 %all_to_all.52.refs_0_ = bf16[32,12,128]{2,1,0:T(8,128)(2,1)S(1)} all-to-all(bf16[32,12,128]{2,1,0:T(8,128)(2,1)S(1)} %shard_map.136), channel_id=1, replica_groups=mesh['gy_0'=2,'gy_1'=8,'gx_0'=2,'gx_1'=4,'gx_2'=2,'gx_3'=2] {'gx_1','gy_1'}, dimensions={0} | all-to-all | bytes 196608 | tf_op jit(solution)/shard_map/all_to_all | solution.py:576
  152.8 14.6 %all_to_all.53 = bf16[32,12,128]{2,1,0:T(8,128)(2,1)S(1)} all-to-all(bf16[32,12,128]{2,1,0:T(8,128)(2,1)S(1)} %shard_map.137), channel_id=1, replica_groups=mesh['gy_0'=2,'gy_1'=8,'gx_0'=2,'gx_1'=4,'gx_2'=2,'gx_3'=2] {'gx_1','gy_1'}, dimensions={0} | all-to-all | bytes 196608 | tf_op jit(solution)/shard_map/all_to_all | solution.py:590
  167.6 11.5 %all_to_all.54 = bf16[8,384,128]{2,1,0:T(8,128)(2,1)S(1)} all-to-all(bf16[8,384,128]{2,1,0:T(8,128)(2,1)S(1)} %broadcast_in_dim.16), channel_id=1, replica_groups=mesh['gy_0'=2,'gy_1'=8,'gx_0'=2,'gx_1'=4,'gx_2'=2,'gx_3'=2] {'gx_0','gy_..., dimensions={0} | all-to-all | bytes 1572864 | tf_op jit(solution)/shard_map/all_to_all | solution.py:593
  179.1 6.7 %collective-permute-start.5 = (bf16[3072,128]{1,0:T(8,128)(2,1)S(1)}, bf16[3072,128]{1,0:T(8,128)(2,1)S(1)}, u32[]{:S(2)}, u32[]{:S(2)}) collective-permute-start(bf16[3072,128]{1,0:T(8,128)(2,1)S(1)} %bitcast.25), channel_id=1, source_target_pairs={{0,1},{1,0},{2,3},{3,2},{4,5},{5,4},{6,7},{7,6},{8,9},{9,8},{10,11... | collective-permute-start | bytes 2359304 | tf_op jit(solution)/shard_map/ppermute | solution.py:566
  185.8 1.9 collective-permute-done.5.other
  187.6 2.2 %shard_map.138 = (bf16[64,16,128]{2,1,0:T(8,128)(2,1)}, f32[1152,128]{1,0:T(8,128)}, f32[1,128]{1,0:T(1,128)}, f32[128,256]{1,0:T(8,128)}, f32[2304,256]{1,0:T(8,128)}) custom-call(bf16[3072,128]{1,0:T(8,128)(2,1)S(1)} %bitcast.26, bf16[3072,128]{1,0:T(8,128)(2,1)S(1)} %collective-permute-done.5.other, f32[64,16,128]{2,1,0:T(8,128)S(1)} %get-tuple-element.58.partial, ...), custom_call_target="tpu_custom_call" | custom-call | tf_op jit(solution)/shard_map/pallas_call | solution.py:96
  (54 shorter events, 5.3 us)
Async XLA Ops:
  0.6 12.8 %copy-start.4 = (bf16[64,16,128]{2,1,0:T(8,128)(2,1)S(1)}, bf16[64,16,128]{2,1,0:T(8,128)(2,1)}, u32[]{:S(2)}) copy-start(bf16[64,16,128]{2,1,0:T(8,128)(2,1)} %field.1) | copy-start | bytes 786436
  2.4 8.9 %collective-permute-start = (bf16[80,128]{1,0:T(8,128)(2,1)S(1)}, bf16[80,128]{1,0:T(8,128)(2,1)S(1)}, u32[]{:S(2)}, u32[]{:S(2)}) collective-permute-start(bf16[80,128]{1,0:T(8,128)(2,1)S(1)} %get-tuple-element.36), channel_id=1, source_target_pairs={{32,64},{96,128},{160,192},{224,256},{288,320},{352,384},{416,448}... | collective-permute-start | bytes 61448 | tf_op jit(solution)/shard_map/ppermute | solution.py:37
  3.0 9.3 %collective-permute-start.1 = (bf16[80,128]{1,0:T(8,128)(2,1)S(1)}, bf16[80,128]{1,0:T(8,128)(2,1)S(1)}, u32[]{:S(2)}, u32[]{:S(2)}) collective-permute-start(bf16[80,128]{1,0:T(8,128)(2,1)S(1)} %get-tuple-element.37), channel_id=1, source_target_pairs={{0,32},{32,0},{64,96},{96,64},{128,160},{160,128},{192,224},{224,1... | collective-permute-start | bytes 61448 | tf_op jit(solution)/shard_map/ppermute | solution.py:35
  13.7 42.1 %copy-start = (bf16[3,3,128,128]{3,2,1,0:T(8,128)(2,1)S(1)}, bf16[3,3,128,128]{3,2,1,0:T(8,128)(2,1)}, u32[]{:S(2)}) copy-start(bf16[3,3,128,128]{3,2,1,0:T(8,128)(2,1)} %param.10) | copy-start | bytes 884740
  13.7 42.0 %copy-start.1 = (bf16[128,256]{1,0:T(8,128)(2,1)S(1)}, bf16[128,256]{1,0:T(8,128)(2,1)}, u32[]{:S(2)}) copy-start(bf16[128,256]{1,0:T(8,128)(2,1)} %projection.3) | copy-start | bytes 196612
  13.7 42.0 %copy-start.2 = (f32[128]{0:T(128)S(1)}, f32[128]{0:T(128)}, u32[]{:S(2)}) copy-start(f32[128]{0:T(128)} %param.9) | copy-start | bytes 1540
  13.8 33.2 %collective-permute-start.2 = (bf16[354,128]{1,0:T(8,128)(2,1)S(1)}, bf16[354,128]{1,0:T(8,128)(2,1)S(1)}, u32[]{:S(2)}, u32[]{:S(2)}) collective-permute-start(bf16[354,128]{1,0:T(8,128)(2,1)S(1)} %get-tuple-element.69), channel_id=1, source_target_pairs={{0,1},{1,0},{2,3},{3,2},{4,5},{5,4},{6,7},{7,6},{8,9},{9,8},{10,11... | collective-permute-start | bytes 271880 | tf_op jit(solution)/shard_map/ppermute | solution.py:35
  19.0 28.0 %collective-permute-start.3 = (bf16[354,128]{1,0:T(8,128)(2,1)S(1)}, bf16[354,128]{1,0:T(8,128)(2,1)S(1)}, u32[]{:S(2)}, u32[]{:S(2)}) collective-permute-start(bf16[354,128]{1,0:T(8,128)(2,1)S(1)} %get-tuple-element.70), channel_id=1, source_target_pairs={{1,2},{3,4},{5,6},{7,8},{9,10},{11,12},{13,14},{15,16},{17,18},{19... | collective-permute-start | bytes 271880 | tf_op jit(solution)/shard_map/ppermute | solution.py:37
  20.9 13.8 %all-to-all-start = ((f32[16,2,128]{2,1,0:T(2,128)}), f32[16,2,128]{2,1,0:T(2,128)S(1)}, u32[]{:S(2)}, u32[]{:S(2)}) async-start(f32[16,2,128]{2,1,0:T(2,128)} %get-tuple-element.38), calls=%async_computation | async-start | bytes 32768 | tf_op jit(solution)/shard_map/all_to_all | solution.py:520
  35.3 20.4 %all-to-all-start.1 = ((f32[32,2,128]{2,1,0:T(2,128)}), f32[32,2,128]{2,1,0:T(2,128)S(1)}, u32[]{:S(2)}, u32[]{:S(2)}) async-start(f32[32,2,128]{2,1,0:T(2,128)} %shard_map.127), calls=%async_computation.1 | async-start | bytes 65536 | tf_op jit(solution)/shard_map/all_to_all | solution.py:524
  58.9 12.5 %all-to-all-start.2 = ((f32[16,4,128]{2,1,0:T(4,128)}), f32[16,4,128]{2,1,0:T(4,128)S(1)}, u32[]{:S(2)}, u32[]{:S(2)}) async-start(f32[16,4,128]{2,1,0:T(4,128)} %get-tuple-element.39), calls=%async_computation.2 | async-start | bytes 65536 | tf_op jit(solution)/shard_map/all_to_all | solution.py:520
  72.1 12.7 %all-to-all-start.3 = ((f32[32,4,128]{2,1,0:T(4,128)}), f32[32,4,128]{2,1,0:T(4,128)S(1)}, u32[]{:S(2)}, u32[]{:S(2)}) async-start(f32[32,4,128]{2,1,0:T(4,128)} %shard_map.129), calls=%async_computation.3 | async-start | bytes 131072 | tf_op jit(solution)/shard_map/all_to_all | solution.py:524
  76.1 8.7 %copy-start.3 = (f32[256]{0:T(256)S(1)}, f32[256]{0:T(256)}, u32[]{:S(2)}) copy-start(f32[256]{0:T(256)} %param.12) | copy-start | bytes 3076
  99.1 12.7 %all-to-all-start.5 = ((f32[32,4,128]{2,1,0:T(4,128)}), f32[32,4,128]{2,1,0:T(4,128)S(1)}, u32[]{:S(2)}, u32[]{:S(2)}) async-start(f32[32,4,128]{2,1,0:T(4,128)} %shard_map.133), calls=%async_computation.5 | async-start | bytes 131072 | tf_op jit(solution)/shard_map/all_to_all | solution.py:524
  116.0 5.3 %collective-permute-start.4 = (bf16[3072,128]{1,0:T(8,128)(2,1)S(1)}, bf16[3072,128]{1,0:T(8,128)(2,1)S(1)}, u32[]{:S(2)}, u32[]{:S(2)}) collective-permute-start(bf16[3072,128]{1,0:T(8,128)(2,1)S(1)} %get-tuple-element.57), channel_id=1, source_target_pairs={{0,1},{1,0},{2,3},{3,2},{4,5},{5,4},{6,7},{7,6},{8,9},{9,8},{10,11... | collective-permute-start | bytes 2359304 | tf_op jit(solution)/shard_map/ppermute | solution.py:566
  179.1 8.6 %collective-permute-start.5 = (bf16[3072,128]{1,0:T(8,128)(2,1)S(1)}, bf16[3072,128]{1,0:T(8,128)(2,1)S(1)}, u32[]{:S(2)}, u32[]{:S(2)}) collective-permute-start(bf16[3072,128]{1,0:T(8,128)(2,1)S(1)} %bitcast.25), channel_id=1, source_target_pairs={{0,1},{1,0},{2,3},{3,2},{4,5},{5,4},{6,7},{7,6},{8,9},{9,8},{10,11... | collective-permute-start | bytes 2359304 | tf_op jit(solution)/shard_map/ppermute | solution.py:566

commit v7 on v6

--- a/solution.py
+++ b/solution.py
@@ -309,7 +309,13 @@
     spread(copies, [first[:, :LANES], first[:, LANES:], second[:, :LANES], second[:, LANES:]])
 
 
-def coarse_rest(center, coarse, grad, weight, out, rows_out, hidden):
+def by_core(write, keep, send):
+    core = lax.axis_index(CORE)
+    pl.when(core == 0)(lambda: write(keep, send))
+    pl.when(core == 1)(lambda: write(send, keep))
+
+
+def coarse_rest(center, coarse, grad, weight, out, keep, send, hidden, halves):
     half = PITCH // 2
     height = out.shape[0]
     channels = out.shape[2]
@@ -335,7 +341,6 @@
     g = grad[2 : 2 + height].astype(jnp.float32)
     own = lax.broadcasted_iota(jnp.int32, g.shape, 1) < half // 2
     g = jnp.where(own, g, 0.0).astype(jnp.bfloat16).reshape(height * half, channels)
-    tall = 9 * channels
     for tap in range(3):
         k = lax.dot_general(
             hidden[tap : tap + height].reshape(height * half, 3 * channels),
@@ -343,15 +348,20 @@
             (((0,), (0,)), ((), ())),
             preferred_element_type=jnp.float32,
         ).astype(jnp.bfloat16)
-        at = tap * 3 * channels
-        rows_out[at : at + 3 * channels] = k[:, :LANES]
-        rows_out[tall + at : tall + at + 3 * channels] = k[:, LANES:]
+        span = slice(tap * 3 * channels, (tap + 1) * 3 * channels)
+        halves[0, span] = k[:, :LANES]
+        halves[1, span] = k[:, LANES:]
+
+    def write(first, second):
+        first[...] = halves[0]
+        second[...] = halves[1]
+
+    by_core(write, keep, send)
 
 
 def fine_backward(coarse_count, rows, cols, place, sums, coarse, pooled, grad, dnorm, stats_c,
-                  gain_c, projection, weight_t, x, hidden, stats_f, gain_f, rows_in,
+                  gain_c, projection, weight_t, x, hidden, stats_f, gain_f,
                   keep, send, gain_c_grad, partial, rows_out, up, shifted, taps):
-    rows_out[0 : rows_in.shape[0]] = rows_in[...]
     tot = jnp.sum(sums[...], axis=0)
     first = jnp.concatenate([tot[0:1], tot[1:2]], axis=1)
     second = jnp.concatenate([tot[2:3], tot[3:4]], axis=1)
@@ -437,7 +447,7 @@
     d = shifted[1 : lines - 1]
     d = jnp.broadcast_to(d[:, None], (lines - 2, 2) + d.shape[1:])
     d = d.reshape(height * PITCH, 3 * LANES)
-    at = 18 * channels
+    at = 0
     for tap in range(3):
         begin = FINE_RIM - 1 + tap
         k = lax.dot_general(
@@ -460,13 +470,11 @@
     ).astype(jnp.bfloat16)
     half = keep.shape[0]
 
-    def part(first, last):
+    def write(first, second):
         first[...] = rows_out[:half]
-        last[...] = rows_out[half:]
-
-    core = lax.axis_index(CORE)
-    pl.when(core == 0)(lambda: part(keep, send))
-    pl.when(core == 1)(lambda: part(send, keep))
+        second[...] = rows_out[half:]
+
+    by_core(write, keep, send)
 
 
 def spread_rows(low, high, at, out, lane):
@@ -505,9 +513,11 @@
         ).astype(jnp.bfloat16)
 
     def weights(low, high):
-        at = spread_rows(low, high, 0, weight_c, 0)
-        at = spread_rows(low, high, at, weight_c, LANES)
-        at = spread_rows(low, high, at, weight_f, 0)
+        tall = weight_c.shape[0]
+        weight_c[:, :LANES] = low[:tall].astype(jnp.float32)
+        weight_c[:, LANES:] = high[:tall].astype(jnp.float32)
+        low, high = low.at[tall:], high.at[tall:]
+        at = spread_rows(low, high, 0, weight_f, 0)
         at = spread_rows(low, high, at, proj, 0)
         spread_rows(low, high, at, proj, LANES)
 
@@ -532,12 +542,26 @@
     return jnp.concatenate([high, middle, low, jnp.zeros_like(low)], axis=0)
 
 
+def kept_split(sums, held):
+    last = sums[sums.shape[0] - 8 :]
+    tail = split(last[0:2] + last[2:4] + last[4:6])
+    return jnp.concatenate([sums[: sums.shape[0] - 8], jnp.where(held == 1, tail, last)], axis=0)
+
+
+def add_cores(place, early, early_got, late, late_got, out):
+    for k, g, base in ((early, early_got, 0), (late, late_got, early.shape[0])):
+        rows = k.shape[0]
+        step = rows // 3
+        for at in range(0, rows, step):
+            sums = k[at : at + step].astype(jnp.float32) + g[at : at + step].astype(jnp.float32)
+            if base > 0 and at + step == rows:
+                sums = kept_split(sums, place[4])
+            out[base + at : base + at + step] = sums.astype(jnp.bfloat16)
+
+
 def add_up(stage, place, *refs):
-    if stage == 0:
-        pieces, (out,), scratch = refs[:2], refs[2:], ()
-    else:
-        pieces = [refs[0].at[k] for k in range(refs[0].shape[0])]
-        out, scratch = refs[1], refs[2:]
+    pieces = [refs[0].at[k] for k in range(refs[0].shape[0])]
+    out, scratch = refs[1], refs[2:]
     rows = pieces[0].shape[0]
     step = 256 if rows % 256 == 0 else rows
     pitch = out.shape[-2]
@@ -546,10 +570,7 @@
         for piece in pieces[1:]:
             sums = sums + piece[at : at + step].astype(jnp.float32)
         if at + step == rows:
-            last = sums[step - 8 :]
-            tail = split(last[0:2] + last[2:4] + last[4:6])
-            tail = jnp.where(place[4 + stage] == 1, tail, last)
-            sums = jnp.concatenate([sums[: step - 8], tail], axis=0)
+            sums = kept_split(sums, place[4 + stage])
         if scratch:
             scratch[0][at : at + step] = sums
         elif len(out.shape) == 3:
@@ -566,11 +587,9 @@
     return lax.ppermute(rows, CORE, [(0, 1), (1, 0)])
 
 
-def gradient_totals(keep, send, place):
-    rows = keep.shape[0]
-    (part,) = call(
-        functools.partial(add_up, 0), [((rows, LANES), jnp.bfloat16, None)], place, keep, traded(send)
-    )
+def gradient_totals(halves, place):
+    rows = halves[0].shape[0] + halves[2].shape[0]
+    (part,) = call(add_cores, [((rows, LANES), jnp.bfloat16, None)], place, *halves)
     for stage, axes in list(enumerate(STAGES))[1:]:
         count = lax.axis_size(axes)
         pieces = lax.all_to_all(part.reshape(count, -1, LANES), axes, 0, 0, tiled=True)
@@ -670,24 +689,29 @@
         pre,
         gain_c,
     )
-    sums = gathered(copies)
+    sums, weight_late = gathered(copies, weight_coarse)
     used = 18 * chan_coarse + 9 * chan_fine + chan_coarse
     used += -(used + 8) % (4 * lax.axis_size(GY_GX)) + 8
-    coarse_output, parts = call(
+    coarse_output, keep_c, send_c = call(
         coarse_rest,
-        [((half_h, half_w, chan_coarse), bf16, None), ((18 * chan_coarse, LANES), bf16)],
+        [((half_h, half_w, chan_coarse), bf16, None), ((9 * chan_coarse, LANES), bf16), ((9 * chan_coarse, LANES), bf16, None)],
         hidden_c,
         coarse,
         grad,
-        weight_coarse.reshape(3, 3 * chan_coarse, chan_coarse),
-        scratch=[((lines, PITCH // 2, 3 * chan_coarse), bf16)],
+        weight_late.reshape(3, 3 * chan_coarse, chan_coarse),
+        scratch=[
+            ((lines, PITCH // 2, 3 * chan_coarse), bf16),
+            ((2, 9 * chan_coarse, LANES), bf16),
+        ],
         plain=(0, 3),
     )
-    keep, send, coarse_gain_grad, partial = call(
+    got_c = traded(send_c)
+    late = used - 18 * chan_coarse
+    keep_l, send_l, coarse_gain_grad, partial = call(
         functools.partial(fine_backward, coarse_count, rows // 2, cols // 2),
         [
-            ((used // 2, LANES), bf16),
-            ((used // 2, LANES), bf16, None),
+            ((late // 2, LANES), bf16),
+            ((late // 2, LANES), bf16, None),
             ((1, chan_coarse), f32, None),
             ((height, width, chan_fine), f32),
         ],
@@ -705,16 +729,15 @@
         hidden_f,
         stats_f,
         gain_f,
-        parts,
         scratch=[
-            ((used, LANES), bf16),
+            ((late, LANES), bf16),
             ((lines * PITCH + 8, chan_fine), f32),
             ((lines, PITCH, 3 * chan_fine), bf16),
             ((3, lines, PITCH // 2, chan_fine), f32),
         ],
         plain=(3, 5, 8, 9, 11),
     )
-    own, other = gradient_totals(keep, send, place)
+    own, other = gradient_totals((keep_c, got_c, keep_l, traded(send_l)), place)
     field_grad, fine_weight_grad, fine_gain_grad, projection_grad, coarse_weight_grad = call(
         functools.partial(finish, fine_count),
         [

time: 191 us -> 194 us (1.016)
  blocking collectives: 67 us -> 78.8 us
  waiting for transfers between devices: 39.6 us -> 32.7 us
    all_to_all x0 -> x1, blocking collectives: none -> 11.8 us  [gathered(): sums = lax.all_to_all(copies, FAR, 0, 0, tiled=True)]
    all_to_all x3 -> x2, waiting for transfers between devices: 20.1 us -> 14.1 us  [gathered(): sums = lax.all_to_all(copies, FAR, 0, 0, tiled=True)]
    all_to_all x3 -> x2, starting transfers between devices: 19.3 us -> 15.5 us  [gathered(): sums = lax.all_to_all(copies, FAR, 0, 0, tiled=True)]
    ppermute x2 -> x3, starting transfers between devices: 10.1 us -> 12.3 us  [traded(): return lax.ppermute(rows, CORE, [(0, 1), (1, 0)])]
  transfers between devices with their start and end apart: 11 -> 11, of which waited for: 8 -> 7; matrix products, arithmetic and copies ran while one was open for 0% -> 0% of each run, Pallas kernels for 3% -> 4%
where the time goes in v7:
time: 194 us; the launch traced here: 193 us
  blocking collectives  78.8 us (41%)
  starting transfers between devices  55.2 us (28%)
  waiting for transfers between devices  32.7 us (17%)
  Pallas kernels  23.1 us (12%)
    all_to_all x2, blocking collectives, gradient_totals(): lax.all_to_all(part.reshape(count, -1, LANES), axes, 0, 0, tiled=True)  29.5 us
    pallas_call x13, Pallas kernels, call(): pl.pallas_call(body, out_shape=[(pltpu.VMEM if len(o) == 2 else o[2] or j...  23.1 us
    all_to_all x2, starting transfers between devices, gathered(): sums = lax.all_to_all(copies, FAR, 0, 0, tiled=True)  15.5 us
    all_to_all x2, waiting for transfers between devices, gathered(): received = lax.all_to_all(copies, NEAR, 0, 0, tiled=True)  14.6 us
    all_to_all x1, blocking collectives, gradient_totals(): part = lax.all_to_all(part, STAGES[2], 0, 0, tiled=True).reshape(-1, LANES)  14.5 us
    all_to_all x2, waiting for transfers between devices, gathered(): sums = lax.all_to_all(copies, FAR, 0, 0, tiled=True)  14.1 us
    ppermute x2, starting transfers between devices, swap(): mate = lax.ppermute(inner, axis, [(i, i ^ 1) for i in range(count)])  13.4 us
    ppermute x3, starting transfers between devices, traded(): return lax.ppermute(rows, CORE, [(0, 1), (1, 0)])  12.3 us
  transfers between devices with their start and end apart: 11, of which 7 were waited for; matrix products, arithmetic and copies ran while one was open for 0% of the time, Pallas kernels for 4%

profile of v7, /device:TPU:1, one launch (start us, length us, event | category | flops | bytes accessed | tf_op | source)
XLA Modules:
  0.0 193.0 jit_solution(10466465289066651422)
XLA Ops:
  0.6 1.7 shard_map.126
  3.0 8.2 %collective-permute-start.1 = (bf16[80,128]{1,0:T(8,128)(2,1)S(1)}, bf16[80,128]{1,0:T(8,128)(2,1)S(1)}, u32[]{:S(2)}, u32[]{:S(2)}) collective-permute-start(bf16[80,128]{1,0:T(8,128)(2,1)S(1)} %get-tuple-element.40), channel_id=1, source_target_pairs={{0,32},{32,0},{64,96},{96,64},{128,160},{160,128},{192,224},{224,1... | collective-permute-start | bytes 61448 | tf_op jit(solution)/shard_map/ppermute | solution.py:35
  11.2 1.1 collective-permute-done.1
  12.4 0.9 pad_maximum_fusion.2
  13.8 5.2 %collective-permute-start.2 = (bf16[354,128]{1,0:T(8,128)(2,1)S(1)}, bf16[354,128]{1,0:T(8,128)(2,1)S(1)}, u32[]{:S(2)}, u32[]{:S(2)}) collective-permute-start(bf16[354,128]{1,0:T(8,128)(2,1)S(1)} %get-tuple-element.75), channel_id=1, source_target_pairs={{0,1},{1,0},{2,3},{3,2},{4,5},{5,4},{6,7},{7,6},{8,9},{9,8},{10,11... | collective-permute-start | bytes 271880 | tf_op jit(solution)/shard_map/ppermute | solution.py:35
  19.0 1.9 collective-permute-start.3
  20.9 6.4 %all-to-all-start = ((f32[16,2,128]{2,1,0:T(2,128)}), f32[16,2,128]{2,1,0:T(2,128)S(1)}, u32[]{:S(2)}, u32[]{:S(2)}) async-start(f32[16,2,128]{2,1,0:T(2,128)} %get-tuple-element.41), calls=%async_computation | async-start | bytes 32768 | tf_op jit(solution)/shard_map/all_to_all | solution.py:530
  27.5 7.2 %all-to-all-done.received = f32[16,2,128]{2,1,0:T(2,128)S(1)} async-done(((f32[16,2,128]{2,1,0:T(2,128)}), f32[16,2,128]{2,1,0:T(2,128)S(1)}, u32[]{:S(2)}, u32[]{:S(2)}) %all-to-all-start) | async-done | bytes 16416 | tf_op jit(solution)/shard_map/all_to_all | solution.py:530
  35.3 11.6 %all-to-all-start.1 = ((f32[32,2,128]{2,1,0:T(2,128)}), f32[32,2,128]{2,1,0:T(2,128)S(1)}, u32[]{:S(2)}, u32[]{:S(2)}) async-start(f32[32,2,128]{2,1,0:T(2,128)} %shard_map.127), calls=%async_computation.1 | async-start | bytes 65536 | tf_op jit(solution)/shard_map/all_to_all | solution.py:534
  47.3 8.4 %all-to-all-done.1.sums = f32[32,2,128]{2,1,0:T(2,128)S(1)} async-done(((f32[32,2,128]{2,1,0:T(2,128)}), f32[32,2,128]{2,1,0:T(2,128)S(1)}, u32[]{:S(2)}, u32[]{:S(2)}) %all-to-all-start.1) | async-done | bytes 32800 | tf_op jit(solution)/shard_map/all_to_all | solution.py:534
  55.7 3.2 %shard_map.128 = (bf16[70,32,128]{2,1,0:T(8,128)(2,1)}, bf16[544,128]{1,0:T(8,128)(2,1)}, bf16[544,256]{1,0:T(8,128)(2,1)S(1)}, f32[16,4,128]{2,1,0:T(4,128)}, f32[2,8,128]{2,1,0:T(8,128)S(1)}) custom-call(s32[7]{0:T(128)S(1)} %stack.31.place, bf16[70,32,128]{2,1,0:T(8,128)(2,1)S(1)} %pad_maximum_fusion.x, f32[32,2,128]{2,1,0:T(2,128)S(1)} %all-to-all-done.1.sums, ...), custom_call_target="tpu_custom_call" | custom-call | tf_op jit(solution)/shard_map/pallas_call | solution.py:96
  58.9 5.1 %all-to-all-start.2 = ((f32[16,4,128]{2,1,0:T(4,128)}), f32[16,4,128]{2,1,0:T(4,128)S(1)}, u32[]{:S(2)}, u32[]{:S(2)}) async-start(f32[16,4,128]{2,1,0:T(4,128)} %get-tuple-element.42), calls=%async_computation.2 | async-start | bytes 65536 | tf_op jit(solution)/shard_map/all_to_all | solution.py:530
  64.1 7.4 %all-to-all-done.2.received = f32[16,4,128]{2,1,0:T(4,128)S(1)} async-done(((f32[16,4,128]{2,1,0:T(4,128)}), f32[16,4,128]{2,1,0:T(4,128)S(1)}, u32[]{:S(2)}, u32[]{:S(2)}) %all-to-all-start.2) | async-done | bytes 32800 | tf_op jit(solution)/shard_map/all_to_all | solution.py:530
  72.1 3.9 %all-to-all-start.3 = ((f32[32,4,128]{2,1,0:T(4,128)}), f32[32,4,128]{2,1,0:T(4,128)S(1)}, u32[]{:S(2)}, u32[]{:S(2)}) async-start(f32[32,4,128]{2,1,0:T(4,128)} %shard_map.129), calls=%async_computation.3 | async-start | bytes 131072 | tf_op jit(solution)/shard_map/all_to_all | solution.py:534
  76.3 2.9 %shard_map.130 = (f32[544,256]{1,0:T(8,128)S(1)}, bf16[3,384,128]{2,1,0:T(8,128)(2,1)}) custom-call(bf16[36,16,256]{2,1,0:T(8,128)(2,1)S(1)} %pad_maximum_fusion.1.grad, bf16[3,3,256,256]{3,2,1,0:T(8,128)(2,1)} %weight.1, bf16[9,128,128]{2,1,0:T(8,128)(2,1)} %bitcast.27), custom_call_target="tpu_custom_call" | custom-call | tf_op jit(solution)/shard_map/pallas_call | solution.py:96
  79.2 5.7 %all-to-all-done.3.sums = f32[32,4,128]{2,1,0:T(4,128)S(1)} async-done(((f32[32,4,128]{2,1,0:T(4,128)}), f32[32,4,128]{2,1,0:T(4,128)S(1)}, u32[]{:S(2)}, u32[]{:S(2)}) %all-to-all-start.3) | async-done | bytes 65568 | tf_op jit(solution)/shard_map/all_to_all | solution.py:534
  84.9 2.1 %shard_map.131 = (bf16[34,16,256]{2,1,0:T(8,128)(2,1)}, f32[544,256]{1,0:T(8,128)}, f32[16,4,128]{2,1,0:T(4,128)S(1)}, f32[2,8,256]{2,1,0:T(8,128)S(1)}) custom-call(s32[7]{0:T(128)S(1)} %stack.31.place, f32[32,4,128]{2,1,0:T(4,128)S(1)} %all-to-all-done.3.sums, bf16[544,256]{1,0:T(8,128)(2,1)S(1)} %get-tuple-element.44.coarse, ...), custom_call_target="tpu_custom_call" | custom-call | tf_op jit(solution)/shard_map/pallas_call | solution.py:96
  87.0 11.4 %all_to_all.50.received = f32[16,4,128]{2,1,0:T(4,128)S(1)} all-to-all(f32[16,4,128]{2,1,0:T(4,128)S(1)} %get-tuple-element.50), channel_id=1, replica_groups=mesh['gy_0'=2,'gy_1'=8,'gx_0'=2,'gx_1'=4,'gx_2'=2,'gx_3'=2] {'gx_1','gx_..., dimensions={0} | all-to-all | bytes 65536 | tf_op jit(solution)/shard_map/all_to_all | solution.py:530
  98.4 3.5 %shard_map.133 = (bf16[32,8,256]{2,1,0:T(8,128)(2,1)}, bf16[2304,128]{1,0:T(8,128)(2,1)S(1)}, bf16[2304,128]{1,0:T(8,128)(2,1)S(1)}) custom-call(bf16[34,16,256]{2,1,0:T(8,128)(2,1)} %get-tuple-element.49.center, bf16[544,256]{1,0:T(8,128)(2,1)S(1)} %get-tuple-element.44.coarse, bf16[36,16,256]{2,1,0:T(8,128)(2,1)S(1)} %pad_maximum_fusion.1.grad, ...), custom_call_target="tpu_custom_call" | custom-call | tf_op jit(solution)/shard_map/pallas_call | solution.py:96
  101.9 2.3 %collective-permute-start.4 = (bf16[2304,128]{1,0:T(8,128)(2,1)S(1)}, bf16[2304,128]{1,0:T(8,128)(2,1)S(1)}, u32[]{:S(2)}, u32[]{:S(2)}) collective-permute-start(bf16[2304,128]{1,0:T(8,128)(2,1)S(1)} %get-tuple-element.54), channel_id=1, source_target_pairs={{0,1},{1,0},{2,3},{3,2},{4,5},{5,4},{6,7},{7,6},{8,9},{9,8},{10,11... | collective-permute-start | bytes 1769480 | tf_op jit(solution)/shard_map/ppermute | solution.py:587
  104.2 11.8 %all_to_all.51.sums = f32[32,4,128]{2,1,0:T(4,128)S(1)} all-to-all(f32[32,4,128]{2,1,0:T(4,128)S(1)} %shard_map.132), channel_id=1, replica_groups=mesh['gy_0'=2,'gy_1'=8,'gx_0'=2,'gx_1'=4,'gx_2'=2,'gx_3'=2] {'gx_0','gy_..., dimensions={0} | all-to-all | bytes 131072 | tf_op jit(solution)/shard_map/all_to_all | solution.py:534
  116.1 4.1 %shard_map.134 = (bf16[768,128]{1,0:T(8,128)(2,1)S(1)}, bf16[768,128]{1,0:T(8,128)(2,1)S(1)}, f32[1,256]{1,0:T(1,128)}, f32[64,16,128]{2,1,0:T(8,128)S(1)}) custom-call(s32[7]{0:T(128)S(1)} %stack.31.place, f32[32,4,128]{2,1,0:T(4,128)S(1)} %all_to_all.51.sums, bf16[544,256]{1,0:T(8,128)(2,1)S(1)} %get-tuple-element.44.coarse, ...), custom_call_target="tpu_custom_call" | custom-call | tf_op jit(solution)/shard_map/pallas_call | solution.py:96
  120.2 3.3 %collective-permute-start.5 = (bf16[768,128]{1,0:T(8,128)(2,1)S(1)}, bf16[768,128]{1,0:T(8,128)(2,1)S(1)}, u32[]{:S(2)}, u32[]{:S(2)}) collective-permute-start(bf16[768,128]{1,0:T(8,128)(2,1)S(1)} %get-tuple-element.63), channel_id=1, source_target_pairs={{0,1},{1,0},{2,3},{3,2},{4,5},{5,4},{6,7},{7,6},{8,9},{9,8},{10,11... | collective-permute-start | bytes 589832 | tf_op jit(solution)/shard_map/ppermute | solution.py:587
  123.5 1.0 collective-permute-done.5.late_got
  124.6 0.7 shard_map.135
  125.3 15.0 %all_to_all.52.refs_0_ = bf16[8,384,128]{2,1,0:T(8,128)(2,1)S(1)} all-to-all(bf16[8,384,128]{2,1,0:T(8,128)(2,1)S(1)} %bitcast.24), channel_id=1, replica_groups=mesh['gy_0'=2,'gy_1'=8,'gx_0'=2,'gx_1'=4,'gx_2'=2,'gx_3'=2] {'gx_0','gy_..., dimensions={0} | all-to-all | bytes 1572864 | tf_op jit(solution)/shard_map/all_to_all | solution.py:595
  141.0 14.5 %all_to_all.53.refs_0_ = bf16[32,12,128]{2,1,0:T(8,128)(2,1)S(1)} all-to-all(bf16[32,12,128]{2,1,0:T(8,128)(2,1)S(1)} %shard_map.136), channel_id=1, replica_groups=mesh['gy_0'=2,'gy_1'=8,'gx_0'=2,'gx_1'=4,'gx_2'=2,'gx_3'=2] {'gx_1','gy_1'}, dimensions={0} | all-to-all | bytes 196608 | tf_op jit(solution)/shard_map/all_to_all | solution.py:595
  156.1 14.5 %all_to_all.54 = bf16[32,12,128]{2,1,0:T(8,128)(2,1)S(1)} all-to-all(bf16[32,12,128]{2,1,0:T(8,128)(2,1)S(1)} %shard_map.137), channel_id=1, replica_groups=mesh['gy_0'=2,'gy_1'=8,'gx_0'=2,'gx_1'=4,'gx_2'=2,'gx_3'=2] {'gx_1','gy_1'}, dimensions={0} | all-to-all | bytes 196608 | tf_op jit(solution)/shard_map/all_to_all | solution.py:609
  170.8 11.5 %all_to_all.55 = bf16[8,384,128]{2,1,0:T(8,128)(2,1)S(1)} all-to-all(bf16[8,384,128]{2,1,0:T(8,128)(2,1)S(1)} %broadcast_in_dim.16), channel_id=1, replica_groups=mesh['gy_0'=2,'gy_1'=8,'gx_0'=2,'gx_1'=4,'gx_2'=2,'gx_3'=2] {'gx_0','gy_..., dimensions={0} | all-to-all | bytes 1572864 | tf_op jit(solution)/shard_map/all_to_all | solution.py:612
  182.3 6.7 %collective-permute-start.6 = (bf16[3072,128]{1,0:T(8,128)(2,1)S(1)}, bf16[3072,128]{1,0:T(8,128)(2,1)S(1)}, u32[]{:S(2)}, u32[]{:S(2)}) collective-permute-start(bf16[3072,128]{1,0:T(8,128)(2,1)S(1)} %bitcast.25), channel_id=1, source_target_pairs={{0,1},{1,0},{2,3},{3,2},{4,5},{5,4},{6,7},{7,6},{8,9},{9,8},{10,11... | collective-permute-start | bytes 2359304 | tf_op jit(solution)/shard_map/ppermute | solution.py:587
  189.0 1.9 collective-permute-done.6.other
  190.8 2.2 %shard_map.138 = (bf16[64,16,128]{2,1,0:T(8,128)(2,1)}, f32[1152,128]{1,0:T(8,128)}, f32[1,128]{1,0:T(1,128)}, f32[128,256]{1,0:T(8,128)}, f32[2304,256]{1,0:T(8,128)}) custom-call(bf16[3072,128]{1,0:T(8,128)(2,1)S(1)} %bitcast.26, bf16[3072,128]{1,0:T(8,128)(2,1)S(1)} %collective-permute-done.6.other, f32[64,16,128]{2,1,0:T(8,128)S(1)} %get-tuple-element.64.partial, ...), custom_call_target="tpu_custom_call" | custom-call | tf_op jit(solution)/shard_map/pallas_call | solution.py:96
  (55 shorter events, 4.6 us)
Async XLA Ops:
  0.6 12.8 %copy-start.4 = (bf16[64,16,128]{2,1,0:T(8,128)(2,1)S(1)}, bf16[64,16,128]{2,1,0:T(8,128)(2,1)}, u32[]{:S(2)}) copy-start(bf16[64,16,128]{2,1,0:T(8,128)(2,1)} %field.1) | copy-start | bytes 786436
  2.4 8.9 %collective-permute-start = (bf16[80,128]{1,0:T(8,128)(2,1)S(1)}, bf16[80,128]{1,0:T(8,128)(2,1)S(1)}, u32[]{:S(2)}, u32[]{:S(2)}) collective-permute-start(bf16[80,128]{1,0:T(8,128)(2,1)S(1)} %get-tuple-element.39), channel_id=1, source_target_pairs={{32,64},{96,128},{160,192},{224,256},{288,320},{352,384},{416,448}... | collective-permute-start | bytes 61448 | tf_op jit(solution)/shard_map/ppermute | solution.py:37
  3.0 9.3 %collective-permute-start.1 = (bf16[80,128]{1,0:T(8,128)(2,1)S(1)}, bf16[80,128]{1,0:T(8,128)(2,1)S(1)}, u32[]{:S(2)}, u32[]{:S(2)}) collective-permute-start(bf16[80,128]{1,0:T(8,128)(2,1)S(1)} %get-tuple-element.40), channel_id=1, source_target_pairs={{0,32},{32,0},{64,96},{96,64},{128,160},{160,128},{192,224},{224,1... | collective-permute-start | bytes 61448 | tf_op jit(solution)/shard_map/ppermute | solution.py:35
  13.7 42.1 %copy-start = (bf16[3,3,128,128]{3,2,1,0:T(8,128)(2,1)S(1)}, bf16[3,3,128,128]{3,2,1,0:T(8,128)(2,1)}, u32[]{:S(2)}) copy-start(bf16[3,3,128,128]{3,2,1,0:T(8,128)(2,1)} %param.10) | copy-start | bytes 884740
  13.7 42.0 %copy-start.1 = (bf16[128,256]{1,0:T(8,128)(2,1)S(1)}, bf16[128,256]{1,0:T(8,128)(2,1)}, u32[]{:S(2)}) copy-start(bf16[128,256]{1,0:T(8,128)(2,1)} %projection.3) | copy-start | bytes 196612
  13.7 42.0 %copy-start.2 = (f32[128]{0:T(128)S(1)}, f32[128]{0:T(128)}, u32[]{:S(2)}) copy-start(f32[128]{0:T(128)} %param.9) | copy-start | bytes 1540
  13.8 33.2 %collective-permute-start.2 = (bf16[354,128]{1,0:T(8,128)(2,1)S(1)}, bf16[354,128]{1,0:T(8,128)(2,1)S(1)}, u32[]{:S(2)}, u32[]{:S(2)}) collective-permute-start(bf16[354,128]{1,0:T(8,128)(2,1)S(1)} %get-tuple-element.75), channel_id=1, source_target_pairs={{0,1},{1,0},{2,3},{3,2},{4,5},{5,4},{6,7},{7,6},{8,9},{9,8},{10,11... | collective-permute-start | bytes 271880 | tf_op jit(solution)/shard_map/ppermute | solution.py:35
  19.0 28.0 %collective-permute-start.3 = (bf16[354,128]{1,0:T(8,128)(2,1)S(1)}, bf16[354,128]{1,0:T(8,128)(2,1)S(1)}, u32[]{:S(2)}, u32[]{:S(2)}) collective-permute-start(bf16[354,128]{1,0:T(8,128)(2,1)S(1)} %get-tuple-element.76), channel_id=1, source_target_pairs={{1,2},{3,4},{5,6},{7,8},{9,10},{11,12},{13,14},{15,16},{17,18},{19... | collective-permute-start | bytes 271880 | tf_op jit(solution)/shard_map/ppermute | solution.py:37
  20.9 13.8 %all-to-all-start = ((f32[16,2,128]{2,1,0:T(2,128)}), f32[16,2,128]{2,1,0:T(2,128)S(1)}, u32[]{:S(2)}, u32[]{:S(2)}) async-start(f32[16,2,128]{2,1,0:T(2,128)} %get-tuple-element.41), calls=%async_computation | async-start | bytes 32768 | tf_op jit(solution)/shard_map/all_to_all | solution.py:530
  35.3 20.4 %all-to-all-start.1 = ((f32[32,2,128]{2,1,0:T(2,128)}), f32[32,2,128]{2,1,0:T(2,128)S(1)}, u32[]{:S(2)}, u32[]{:S(2)}) async-start(f32[32,2,128]{2,1,0:T(2,128)} %shard_map.127), calls=%async_computation.1 | async-start | bytes 65536 | tf_op jit(solution)/shard_map/all_to_all | solution.py:534
  58.9 12.5 %all-to-all-start.2 = ((f32[16,4,128]{2,1,0:T(4,128)}), f32[16,4,128]{2,1,0:T(4,128)S(1)}, u32[]{:S(2)}, u32[]{:S(2)}) async-start(f32[16,4,128]{2,1,0:T(4,128)} %get-tuple-element.42), calls=%async_computation.2 | async-start | bytes 65536 | tf_op jit(solution)/shard_map/all_to_all | solution.py:530
  72.1 12.7 %all-to-all-start.3 = ((f32[32,4,128]{2,1,0:T(4,128)}), f32[32,4,128]{2,1,0:T(4,128)S(1)}, u32[]{:S(2)}, u32[]{:S(2)}) async-start(f32[32,4,128]{2,1,0:T(4,128)} %shard_map.129), calls=%async_computation.3 | async-start | bytes 131072 | tf_op jit(solution)/shard_map/all_to_all | solution.py:534
  76.1 8.7 %copy-start.3 = (f32[256]{0:T(256)S(1)}, f32[256]{0:T(256)}, u32[]{:S(2)}) copy-start(f32[256]{0:T(256)} %param.12) | copy-start | bytes 3076
  101.9 22.6 %collective-permute-start.4 = (bf16[2304,128]{1,0:T(8,128)(2,1)S(1)}, bf16[2304,128]{1,0:T(8,128)(2,1)S(1)}, u32[]{:S(2)}, u32[]{:S(2)}) collective-permute-start(bf16[2304,128]{1,0:T(8,128)(2,1)S(1)} %get-tuple-element.54), channel_id=1, source_target_pairs={{0,1},{1,0},{2,3},{3,2},{4,5},{5,4},{6,7},{7,6},{8,9},{9,8},{10,11... | collective-permute-start | bytes 1769480 | tf_op jit(solution)/shard_map/ppermute | solution.py:587
  120.2 4.4 %collective-permute-start.5 = (bf16[768,128]{1,0:T(8,128)(2,1)S(1)}, bf16[768,128]{1,0:T(8,128)(2,1)S(1)}, u32[]{:S(2)}, u32[]{:S(2)}) collective-permute-start(bf16[768,128]{1,0:T(8,128)(2,1)S(1)} %get-tuple-element.63), channel_id=1, source_target_pairs={{0,1},{1,0},{2,3},{3,2},{4,5},{5,4},{6,7},{7,6},{8,9},{9,8},{10,11... | collective-permute-start | bytes 589832 | tf_op jit(solution)/shard_map/ppermute | solution.py:587
  182.3 8.6 %collective-permute-start.6 = (bf16[3072,128]{1,0:T(8,128)(2,1)S(1)}, bf16[3072,128]{1,0:T(8,128)(2,1)S(1)}, u32[]{:S(2)}, u32[]{:S(2)}) collective-permute-start(bf16[3072,128]{1,0:T(8,128)(2,1)S(1)} %bitcast.25), channel_id=1, source_target_pairs={{0,1},{1,0},{2,3},{3,2},{4,5},{5,4},{6,7},{7,6},{8,9},{9,8},{10,11... | collective-permute-start | bytes 2359304 | tf_op jit(solution)/shard_map/ppermute | solution.py:587
